TPU v7x, 32 devices: a whole 2x2x4 slice. The times are simulated.
32 devices in a mesh: seq: 4 (over y, x), head: 8 (over z, core).
Axes of the slice: x: 2, y: 2, z: 4, core: 2. Of those that a mesh axis runs over, the one named last changes fastest.
Arguments:
- hidden_in: bfloat16 [16384, 1536], P('seq'), may hold values from -6 to 6
- norm_gain: float32 [1536], replicated, may hold values from 0.1 to 1.9
- gate_proj: bfloat16 [1536, 1024], P(None, 'head'), may hold values from -0.15625 to 0.15625
- value_proj: bfloat16 [1536, 1024], P(None, 'head'), may hold values from -0.21875 to 0.21875
- state_proj: bfloat16 [1536, 256], replicated, may hold values from -0.15625 to 0.15625
- step_proj: bfloat16 [1536, 16], P(None, 'head'), may hold values from -0.15625 to 0.15625
- conv_value: float32 [4, 1024], P(None, 'head'), may hold values from -3 to 3
- conv_value_bias: float32 [1024], P('head'), may hold values from -3 to 3
- conv_state: float32 [4, 256], replicated, may hold values from -3 to 3
- conv_state_bias: float32 [256], replicated, may hold values from -3 to 3
- step_bias: float32 [16], P('head'), may hold values from -1 to 1
- decay_rate: float32 [16], P('head'), may hold values from 3.0517578e-05 to 0.03
- skip_gain: float32 [16], P('head'), may hold values from 0.1 to 1.9
- mix_gain: float32 [1024], P('head'), may hold values from 0.1 to 1.9
- out_proj: bfloat16 [1024, 1536], P('head'), may hold values from -0.25 to 0.25
- out_grad: bfloat16 [16384, 1536], P('seq'), may hold values from -6 to 6
Outputs:
- block_out: bfloat16 [16384, 1536], P('seq', 'head')
- grad_input: float32 [16384, 1536], P('seq', 'head')
- grad_norm_gain: float32 [1536], P('head')
- grad_gate_proj: float32 [1536, 1024], P(None, 'head')
- grad_value_proj: float32 [1536, 1024], P(None, 'head')
- grad_state_proj: float32 [1536, 256], P('head')
- grad_step_proj: float32 [1536, 16], P(None, 'head')
- grad_conv_value: float32 [4, 1024], P(None, 'head')
- grad_conv_value_bias: float32 [1024], P('head')
- grad_conv_state: float32 [4, 256], replicated
- grad_conv_state_bias: float32 [256], replicated
- grad_step_bias: float32 [16], P('head')
- grad_decay_rate: float32 [16], P('head')
- grad_skip_gain: float32 [16], P('head')
- grad_mix_gain: float32 [1024], P('head')
- grad_out_proj: float32 [1024, 1536], P('head')
All inputs are finite; a program needn't handle non-finite values.
Results may differ from a plain program's by a relative error of at most 0.012.
The roundings to bfloat16 on the way count: a program that leaves them out, or rounds other values in their place, can miss the bound.
Values may be sent and summed in bfloat16 or wider, within the bound.
No kernel may reach another device: no remote copies, remote signals or barrier semaphores. Data moves between devices by JAX's collectives and lax.ppermute only.
A program may use at most 384 MiB of HBM per device.

v0:
```python
from functools import partial

import jax
import jax.numpy as jnp
from jax import lax
from jax.sharding import PartitionSpec as P

SPAN = 256


epsilon = 1e-05
highest = lax.Precision.HIGHEST


def passed_along(block, axis, distance):
    devices = range(lax.axis_size(axis))
    route = [(i - distance, i) for i in devices if i - distance in devices]
    return lax.ppermute(block, axis, route)


def prefix(value, axis, join, neutral, backward):
    count, mine = (lax.axis_size(axis), lax.axis_index(axis))
    pieces = jax.tree.map(lambda part: lax.all_gather(part, axis), value)
    if backward:
        pieces = jax.tree.map(lambda part: part[::-1], pieces)
        mine = count - 1 - mine
    subtotal = jax.tree.map(
        lambda part, zero: jnp.full_like(part, 0) + jnp.asarray(zero, part.dtype), value, neutral
    )

    def step(position, subtotal):
        longer = join(subtotal, jax.tree.map(lambda part: part[position], pieces))
        return jax.tree.map(lambda new, old: jnp.where(position < mine, new, old), longer, subtotal)

    return lax.fori_loop(0, count - 1, step, subtotal)


def chain_join(earlier, later):
    return (earlier[0] * later[0], later[0][:, None, None] * earlier[1] + later[1])


def silu_slope(values):
    logistic = jax.nn.sigmoid(values)
    return logistic * (1.0 + values * (1.0 - logistic))


def local_mixer(
    conv_out, step_raw, step_bias, decay_rate, skip_gain, head_width, state_width, block_len
):
    active = jax.nn.silu(conv_out)
    tokens_here = conv_out.shape[0]
    heads_here = step_raw.shape[1]
    block_count = tokens_here // block_len
    values = active[:, :head_width].reshape(
        block_count, block_len, heads_here, head_width // heads_here
    )
    keys_in = active[:, head_width : head_width + state_width].reshape(
        block_count, block_len, state_width
    )
    queries = active[:, head_width + state_width :]
    queries_b = queries.reshape(block_count, block_len, state_width)
    widths = jax.nn.softplus(step_raw + step_bias[None, :])
    log_decay = (-decay_rate[None, :] * widths).reshape(block_count, block_len, heads_here)
    widths_b = widths.reshape(block_count, block_len, heads_here)
    running = jnp.cumsum(log_decay, axis=1)
    scores = jnp.einsum("cin,cjn->cij", queries_b, keys_in, precision=highest)
    lower = jnp.arange(block_len)[:, None] >= jnp.arange(block_len)[None, :]
    spread = jnp.where(
        lower[None, :, :, None], running[:, :, None, :] - running[:, None, :, :], -jnp.inf
    )
    weights = scores[:, :, :, None] * jnp.exp(spread) * widths_b[:, None, :, :]
    outputs = jnp.einsum("cijh,cjhp->cihp", weights, values, precision=highest)
    tails = jnp.exp(running[:, -1:, :] - running) * widths_b
    states = jnp.einsum("cjh,cjn,cjhp->chpn", tails, keys_in, values, precision=highest)
    totals = running[:, -1, :]

    def advance(carried, inputs):
        return (jnp.exp(inputs[1])[:, None, None] * carried + inputs[0], carried)

    anchor = jnp.zeros(states.shape[1:], jnp.float32)
    sent_state, before = lax.scan(advance, anchor, (states, totals))
    outputs = outputs + jnp.exp(running)[..., None] * jnp.einsum(
        "cin,chpn->cihp", queries_b, before, precision=highest
    )
    outputs = outputs + skip_gain[None, None, :, None] * values
    offsets = jnp.cumsum(totals, axis=0) - totals
    log_reach = (running + offsets[:, None, :]).reshape(tokens_here, heads_here)
    return (outputs.reshape(tokens_here, heads_here, -1), sent_state, log_reach, queries)


def local(
    hidden_in,
    norm_gain,
    gate_proj,
    value_proj,
    state_proj,
    step_proj,
    conv_value,
    conv_value_bias,
    conv_state,
    conv_state_bias,
    step_bias,
    decay_rate,
    skip_gain,
    mix_gain,
    out_proj,
    out_grad,
):
    row_count = hidden_in.shape[0]
    model_width = hidden_in.shape[1]
    head_group = lax.axis_size("head")
    col_share = model_width // head_group
    first_col = lax.axis_index("head") * col_share
    inner_local = gate_proj.shape[1]
    inner_width = inner_local * head_group
    heads_here = step_proj.shape[1]
    state_width = state_proj.shape[1] // 2
    tap_count = conv_value.shape[0]
    edge_rows = tap_count - 1
    hidden = hidden_in.astype(jnp.float32)
    scale_in = lax.rsqrt(jnp.mean(hidden * hidden, axis=1, keepdims=True) + epsilon)
    normalized = hidden * scale_in
    projected = (normalized * norm_gain[None, :]).astype(jnp.bfloat16)
    gate_in = jnp.dot(projected, gate_proj, preferred_element_type=jnp.float32)
    stream = jnp.concatenate(
        [
            jnp.dot(projected, value_proj, preferred_element_type=jnp.float32).astype(jnp.bfloat16),
            jnp.dot(projected, state_proj, preferred_element_type=jnp.float32).astype(jnp.bfloat16),
        ],
        axis=1,
    )
    step_raw = jnp.dot(projected, step_proj, preferred_element_type=jnp.float32)
    channel_count = stream.shape[1]
    previous = passed_along(stream[row_count - edge_rows :], "seq", 1)
    extended = jnp.concatenate([previous, stream], axis=0).astype(jnp.float32)
    kernel = jnp.concatenate([conv_value, conv_state], axis=1)
    offset_row = jnp.concatenate([conv_value_bias, conv_state_bias])
    conv_out = offset_row[None, :] + kernel[0][None, :] * extended[0:row_count]
    for tap_index in range(1, tap_count):
        conv_out = (
            conv_out + kernel[tap_index][None, :] * extended[tap_index : tap_index + row_count]
        )
    mixer_fn = partial(local_mixer, head_width=inner_local, state_width=state_width, block_len=SPAN)
    mixer_out, mixer_back = jax.vjp(mixer_fn, conv_out, step_raw, step_bias, decay_rate, skip_gain)
    partial_out, sent_state, log_reach, queries = mixer_out
    device_decay = jnp.exp(log_reach[-1])
    identity = (jnp.ones_like(device_decay), jnp.zeros_like(sent_state))
    prior_decay, carried = prefix((device_decay, sent_state), "seq", chain_join, identity, False)
    reach = jnp.exp(log_reach)
    carried_out = reach[:, :, None] * jnp.einsum("tn,hpn->thp", queries, carried, precision=highest)
    mixed = (partial_out + carried_out).reshape(row_count, inner_local)
    gate_act = jax.nn.silu(gate_in)
    gated = mixed * gate_act
    square_sum = lax.psum(jnp.sum(gated * gated, axis=1), "head")
    scale_gate = lax.rsqrt(square_sum / inner_width + epsilon)[:, None]
    gated_hat = gated * scale_gate
    gated_rows = (gated_hat * mix_gain[None, :]).astype(jnp.bfloat16)
    hidden_own = lax.dynamic_slice_in_dim(hidden, first_col, col_share, 1)
    branch_out = (
        lax.psum_scatter(
            jnp.einsum(
                "kd,tk->dt", out_proj, gated_rows, preferred_element_type=jnp.float32
            ).astype(jnp.bfloat16),
            "head",
            scatter_dimension=0,
            tiled=True,
        )
        .astype(jnp.float32)
        .T
    )
    block_out = (hidden_own + branch_out).astype(jnp.bfloat16)
    grad_gated = jnp.einsum("td,kd->tk", out_grad, out_proj, preferred_element_type=jnp.float32)
    grad_out_proj = jnp.einsum(
        "tk,td->kd", gated_rows, out_grad, preferred_element_type=jnp.float32
    )
    grad_mix_gain = jnp.sum(grad_gated * gated_hat, axis=0)
    grad_hat = grad_gated * mix_gain[None, :]
    hat_dot = lax.psum(jnp.sum(grad_hat * gated_hat, axis=1), "head")
    grad_gated_pre = scale_gate * (grad_hat - gated_hat * (hat_dot / inner_width)[:, None])
    grad_mixed = (grad_gated_pre * gate_act).reshape(row_count, heads_here, -1)
    grad_gate_in = grad_gated_pre * mixed * silu_slope(gate_in)
    incoming = jnp.einsum("th,thp,tn->hpn", reach, grad_mixed, queries, precision=highest)
    later_decay, carried_grad = prefix((device_decay, incoming), "seq", chain_join, identity, True)
    grad_reach = jnp.sum(grad_mixed * carried_out, axis=2)
    grad_reach = grad_reach.at[-1].add(device_decay * jnp.sum(carried_grad * carried, axis=(1, 2)))
    grad_queries = jnp.einsum("th,thp,hpn->tn", reach, grad_mixed, carried, precision=highest)
    grad_conv, grad_step_raw, grad_step_bias, grad_decay, grad_skip = mixer_back(
        (grad_mixed, carried_grad, grad_reach, grad_queries)
    )
    state_sum = lax.psum(grad_conv[:, inner_local:], "head")
    grad_conv = jnp.concatenate([grad_conv[:, :inner_local], state_sum], axis=1)
    pad_block = jnp.zeros((edge_rows, channel_count), jnp.float32)
    padded = jnp.concatenate([pad_block, grad_conv, pad_block], axis=0)
    grad_ext = kernel[0][None, :] * padded[edge_rows : edge_rows + row_count + edge_rows]
    for tap_index in range(1, tap_count):
        lead = edge_rows - tap_index
        grad_ext = (
            grad_ext + kernel[tap_index][None, :] * padded[lead : lead + row_count + edge_rows]
        )
    grad_kernel = jnp.stack(
        [
            jnp.sum(grad_conv * extended[tap_index : tap_index + row_count], axis=0)
            for tap_index in range(tap_count)
        ]
    )
    grad_offset = jnp.sum(grad_conv, axis=0)
    from_next = passed_along(grad_ext[:edge_rows], "seq", -1)
    grad_stream = grad_ext[edge_rows:] + jnp.concatenate(
        [jnp.zeros((row_count - edge_rows, channel_count), jnp.float32), from_next], axis=0
    )
    grad_value16 = grad_stream[:, :inner_local].astype(jnp.bfloat16)
    grad_state16 = grad_stream[:, inner_local:].astype(jnp.bfloat16)
    grad_gate16 = grad_gate_in.astype(jnp.bfloat16)
    grad_step16 = grad_step_raw.astype(jnp.bfloat16)
    grad_gate_proj = jnp.einsum(
        "td,tk->dk", projected, grad_gate16, preferred_element_type=jnp.float32
    )
    grad_value_proj = jnp.einsum(
        "td,tk->dk", projected, grad_value16, preferred_element_type=jnp.float32
    )
    grad_step_proj = jnp.einsum(
        "td,tk->dk", projected, grad_step16, preferred_element_type=jnp.float32
    )
    projected_own = lax.dynamic_slice_in_dim(projected, first_col, col_share, 1)
    grad_state_proj = jnp.einsum(
        "td,tk->dk", projected_own, grad_state16, preferred_element_type=jnp.float32
    )
    total = jnp.einsum("dk,tk->dt", gate_proj, grad_gate16, preferred_element_type=jnp.float32)
    total = total + jnp.einsum(
        "dk,tk->dt", value_proj, grad_value16, preferred_element_type=jnp.float32
    )
    total = total + jnp.einsum(
        "dk,tk->dt", step_proj, grad_step16, preferred_element_type=jnp.float32
    )
    grad_projected = (
        lax.psum_scatter(total.astype(jnp.bfloat16), "head", scatter_dimension=0, tiled=True)
        .astype(jnp.float32)
        .T
    )
    state_rows = lax.dynamic_slice_in_dim(state_proj, first_col, col_share, 0)
    grad_projected = grad_projected + jnp.einsum(
        "tk,dk->td", grad_state16, state_rows, preferred_element_type=jnp.float32
    )
    gain_own = lax.dynamic_slice_in_dim(norm_gain, first_col, col_share, 0)
    normal_own = lax.dynamic_slice_in_dim(normalized, first_col, col_share, 1)
    grad_norm_gain = jnp.sum(grad_projected * normal_own, axis=0)
    grad_unit = grad_projected * gain_own[None, :]
    unit_dot = lax.psum(jnp.sum(grad_unit * normal_own, axis=1), "head")
    grad_input = scale_in * (grad_unit - normal_own * (unit_dot / model_width)[:, None])
    grad_input = grad_input + lax.dynamic_slice_in_dim(out_grad, first_col, col_share, 1).astype(
        jnp.float32
    )
    summed = lax.psum(
        (
            grad_norm_gain,
            grad_gate_proj,
            grad_value_proj,
            grad_state_proj,
            grad_step_proj,
            grad_kernel,
            grad_offset,
            grad_step_bias,
            grad_decay,
            grad_skip,
            grad_mix_gain,
            grad_out_proj,
        ),
        "seq",
    )
    (
        grad_norm_gain,
        grad_gate_proj,
        grad_value_proj,
        grad_state_proj,
        grad_step_proj,
        grad_kernel,
        grad_offset,
        grad_step_bias,
        grad_decay,
        grad_skip,
        grad_mix_gain,
        grad_out_proj,
    ) = summed
    return (
        block_out,
        grad_input,
        grad_norm_gain,
        grad_gate_proj,
        grad_value_proj,
        grad_state_proj,
        grad_step_proj,
        grad_kernel[:, :inner_local],
        grad_offset[:inner_local],
        grad_kernel[:, inner_local:],
        grad_offset[inner_local:],
        grad_step_bias,
        grad_decay,
        grad_skip,
        grad_mix_gain,
        grad_out_proj,
    )


def solution(mesh):
    in_specs = (
        P("seq", None),
        P(),
        P(None, "head"),
        P(None, "head"),
        P(),
        P(None, "head"),
        P(None, "head"),
        P("head"),
        P(),
        P(),
        P("head"),
        P("head"),
        P("head"),
        P("head"),
        P("head", None),
        P("seq", None),
    )
    out_specs = (
        P("seq", "head"),
        P("seq", "head"),
        P("head"),
        P(None, "head"),
        P(None, "head"),
        P("head", None),
        P(None, "head"),
        P(None, "head"),
        P("head"),
        P(),
        P(),
        P("head"),
        P("head"),
        P("head"),
        P("head"),
        P("head", None),
    )
    return jax.shard_map(local, mesh=mesh, in_specs=in_specs, out_specs=out_specs, check_vma=False)
```

profile of v0, /device:TPU:0, one launch (start us, length us, event | category | flops | bytes accessed | tf_op | source)
XLA Modules:
  0.0 856.1 jit_solution(7827187895138865095)
XLA Ops:
  7.2 16.8 %copy.377 = bf16[4096,1536]{0,1:T(8,128)(2,1)} copy(bf16[4096,1536]{1,0:T(8,128)(2,1)} %param.26) | data formatting | bytes 25165824 | tf_op args[0]
  31.2 15.0 %broadcast_multiply_fusion = (f32[4096,1536]{0,1:T(8,128)}, bf16[4096,1536]{0,1:T(8,128)(2,1)S(1)}) fusion(f32[4096]{0:T(1024)S(1)} %add_rsqrt_fusion.1, bf16[4096,1536]{0,1:T(8,128)(2,1)} %copy.377, f32[1536]{0:T(1024)S(1)} %copy-done.66), kind=kLoop, calls=%fused_computation.25 | loop fusion | flops 25165824 | bytes 50354176 | tf_op jit(solution)/shard_map/mul | solution.py:122
  101.4 33.6 %while.65 = (s32[]{:T(128)}, f32[2,64,128]{2,1,0:T(8,128)S(1)}, f32[16,2,64,128]{3,2,1,0:T(8,128)}, f32[16,2]{1,0:T(8,128)S(1)}, f32[16,2,1,1]{1,3,2,0:T(1,128)}...) while((s32[]{:T(128)}, f32[2,64,128]{2,1,0:T(8,128)S(1)}, ...), condition=%wide.region_4.5_spmd.clone, body=%wide.region_3.4_spmd.clone.sunk | while | flops 65539 | bytes 328360 | solution.py:81
  165.7 11.2 %fusion.47 = f32[16,2,8,8,256]{4,3,2,1,0:T(8,128)S(1)} fusion(f32[16,256,2,64]{1,3,2,0:T(8,128)S(1)} %fusion.122, f32[16,256,2]{1,2,0:T(2,128)S(1)} %bitcast.353, f32[16,256,2]{1,2,0:T(2,128)S(1)} %copy-done.46, f32[16,256,256]{2,1,0:T(8,128)S(1)} %fusion.121, pred[256,256]{1,0:T(8,128)(4,1)S(1)} %copy-done.42, f32[16,256,2,64]{1,0,3,2:T(8,128)S(1)} %bitcast.329, ...), kind=kOutput, calls=%fused_computation.96 | convolution fusion | flops 1621098496 | bytes 10649608 | tf_op jit(solution)/shard_map/jvp(cijh,cjhp->cihp)/dot_general | solution.py:72
  186.0 26.0 %psum.112 = f32[4096]{0:T(1024)S(1)} all-reduce(f32[4096]{0:T(1024)S(1)} %get-tuple-element.723), channel_id=1, replica_groups=mesh['seq'=4,'head'=8] {'head'}, use_global_device_ids=true, to_apply=%region_9.10 | all-reduce | flops 4096 | bytes 32768 | tf_op jit(solution)/shard_map/psum | solution.py:154
  212.0 10.5 %multiply_reduce_fusion.9 = (f32[128]{0:T(128)}, f32[4096]{0:T(1024)S(1)}, f32[4096,128]{0,1:T(8,128)}) fusion(f32[4096,128]{0,1:T(8,128)S(1)} %get-tuple-element.724, f32[4096]{0:T(1024)S(1)} %add_rsqrt_fusion, f32[128]{0:T(128)S(1)} %copy-done.64, bf16[4096,1536]{1,0:T(8,128)(2,1)} %param.41, bf16[128,1536]{1,0:T(8,128)(2,1)} %param.40), kind=kOutput, calls=%fused_computation.98 | convolution fusion | flops 1613754240 | bytes 17204224 | tf_op jit(solution)/shard_map/td,kd->tk/dot_general | solution.py:172
  222.5 26.1 %psum.113 = f32[4096]{0:T(1024)S(1)} all-reduce(f32[4096]{0:T(1024)S(1)} %get-tuple-element.648), channel_id=1, replica_groups=mesh['seq'=4,'head'=8] {'head'}, use_global_device_ids=true, to_apply=%region_12.13 | all-reduce | flops 4096 | bytes 32768 | tf_op jit(solution)/shard_map/psum | solution.py:178
  261.7 16.5 %fusion.23 = (f32[16,256,2]{1,2,0:T(2,128)}, f32[16,256,2]{1,2,0:T(2,128)}, f32[16,256,2]{1,2,0:T(2,128)}, f32[16,256,256]{2,1,0:T(8,128)}) fusion(f32[16,256,2]{1,2,0:T(2,128)S(1)} %bitcast.354, f32[16,256,2]{1,2,0:T(2,128)S(1)} %copy-done.46, f32[16,256,256]{2,1,0:T(8,128)S(1)} %copy-done.29, pred[256,256]{1,0:T(8,128)(4,1)S(1)} %copy-done.42, ...), kind=kOutput, calls=%fused_computation.59 | convolution fusion | flops 1636802560 | bytes 12812288 | tf_op jit(solution)/shard_map/transpose(jvp(cijh,cjhp->cihp))/dot_general | solution.py:72
  287.6 9.6 %all-gather.1 = f32[8,64,128]{2,1,0:T(8,128)} all-gather(f32[2,64,128]{2,1,0:T(8,128)S(1)} %fusion.43), channel_id=3, replica_groups=mesh['seq'=4,'head'=8] {'seq'}, dimensions={0}, use_global_device_ids=true | all-gather | bytes 327680 | tf_op jit(solution)/shard_map/all_gather | solution.py:23
  301.6 48.0 %while.64 = (s32[]{:T(128)}, f32[2,64,128]{2,1,0:T(8,128)S(1)}, f32[16,2,64,128]{3,2,1,0:T(8,128)}, f32[16,2]{1,0:T(8,128)S(1)}, f32[16,2,64,128]{3,2,1,0:T(8,12...) while((s32[]{:T(128)}, f32[2,64,128]{2,1,0:T(8,128)S(1)}, ...), condition=%wide.region_18.19_spmd, body=%wide.region_16.18_spmd.sunk | while | flops 65539 | bytes 393429 | solution.py:81
  407.7 9.8 %fusion.6 = bf16[1536,4096]{0,1:T(8,128)(2,1)} fusion(bf16[128,1536]{1,0:T(8,128)(2,1)} %param.40, f32[4096,128]{0,1:T(8,128)} %copy-done.4, f32[128]{0:T(128)S(1)} %copy-done.65, f32[4096]{0:T(1024)S(1)} %add_rsqrt_fusion), kind=kOutput, calls=%fused_computation.23 | convolution fusion | flops 1618477056 | bytes 15090176 | tf_op jit(solution)/shard_map/kd,tk->dt/dot_general | solution.py:161
  417.5 16.7 %copy.464 = bf16[1536,4096]{1,0:T(8,128)(2,1)} copy(bf16[1536,4096]{0,1:T(8,128)(2,1)} %fusion.6) | data formatting | bytes 25165824
  450.7 10.5 %fusion.101 = f32[4096,1536]{1,0:T(8,128)} fusion(bf16[1536,2]{0,1:T(2,128)(2,1)S(1)} %copy-done.54, bf16[4096,2]{0,1:T(2,128)(2,1)S(1)} %get-tuple-element.722), kind=kOutput, calls=%fused_computation.181 | convolution fusion | flops 25165824 | bytes 25188352 | tf_op jit(solution)/shard_map/dk,tk->dt/dot_general | solution.py:232
  461.2 39.8 %all-reduce.13.cloned.1.call-done = f32[4096,256]{0,1:T(8,128)} async-done(((f32[4096,256]{0,1:T(8,128)}), f32[4096,256]{0,1:T(8,128)}) %all-reduce.13.cloned.1.call-update) | async-done | bytes 4194320 | tf_op jit(solution)/shard_map/psum | solution.py:190
  501.0 16.7 %multiply_reduce_fusion.5 = (f32[384]{0:T(512)S(1)}, f32[384]{0:T(512)S(1)}, f32[384]{0:T(512)S(1)}, f32[384]{0:T(512)S(1)}, f32[384]{0:T(512)S(1)}, /*index=5*/f32[4096,384]{0,1:T(8,128)}) fusion(f32[4099,384]{0,1:T(8,128)} %copy-done.1, f32[4096,256]{0,1:T(8,128)} %all-reduce.13.cloned.1.call-done, f32[4096,128]{0,1:T(8,128)S(1)} %slice-done.6), kind=kLoop, calls=%fused_computation.50 | loop fusion | flops 15726720 | bytes 37756416 | tf_op jit(solution)/shard_map/reduce_sum | solution.py:202
  526.8 13.5 %fusion.16 = f32[4099,384]{0,1:T(8,128)S(1)} fusion(f32[4102,384]{0,1:T(8,128)} %concatenate.35, f32[4096,384]{0,1:T(8,128)} %get-tuple-element.734, f32[384]{0:T(512)S(1)} %copy-done.58, f32[384]{0:T(512)S(1)} %copy-done.60, f32[384]{0:T(512)S(1)} %copy-done.62, f32[384]{0:T(512)S(1)} %copy-done.56), kind=kLoop, calls=%fused_computation.39 | loop fusion | flops 11018112 | bytes 25185792 | tf_op jit(solution)/shard_map/add | solution.py:198
  541.6 10.6 %fusion.123 = f32[4096,1536]{1,0:T(8,128)} fusion(bf16[4096,128]{0,1:T(8,128)(2,1)S(1)} %copy-done.31, bf16[1536,128]{1,0:T(8,128)(2,1)S(1)} %copy-done.37), kind=kOutput, calls=%fused_computation.215 | convolution fusion | flops 1610612736 | bytes 26607616 | tf_op jit(solution)/shard_map/dk,tk->dt/dot_general | solution.py:228
  555.0 22.8 %fusion.7 = bf16[1536,4096]{0,1:T(8,128)(2,1)} fusion(f32[4096,1536]{1,0:T(8,128)} %fusion.101, f32[4096,1536]{1,0:T(8,128)} %fusion.123, bf16[1536,128]{1,0:T(8,128)(2,1)S(1)} %copy-done.35, bf16[4096,384]{0,1:T(8,128)(2,1)} %fusion.20), kind=kOutput, calls=%fused_computation.24 | convolution fusion | flops 1629487104 | bytes 64356352 | tf_op jit(solution)/shard_map/dk,tk->dt/dot_general | solution.py:229
  577.8 16.8 %copy.466 = bf16[1536,4096]{1,0:T(8,128)(2,1)} copy(bf16[1536,4096]{0,1:T(8,128)(2,1)} %fusion.7) | data formatting | bytes 25165824
  594.7 14.3 %convert_element_type.46 = f32[4096,1536]{0,1:T(8,128)} convert(bf16[4096,1536]{0,1:T(8,128)(2,1)} %copy.377) | non-fusion elementwise | flops 6291456 | bytes 37748736 | tf_op jit(solution)/shard_map/convert_element_type | solution.py:120
  648.9 113.6 %reduce-scatter.9.cloned.1.call-done = bf16[192,4096]{1,0:T(8,128)(2,1)} async-done(((bf16[1536,4096]{1,0:T(8,128)(2,1)}), bf16[192,4096]{1,0:T(8,128)(2,1)}) %reduce-scatter.9.cloned.1.call-update) | async-done | bytes 1572880 | tf_op jit(solution)/shard_map/reduce_scatter | solution.py:236
  768.4 18.3 %all-reduce.8 = (f32[192]{0:T(256)}, f32[1536,2]{0,1:T(2,128)}, f32[4,384]{1,0:T(4,128)S(1)}, f32[384]{0:T(512)S(1)}, f32[2]{0:T(128)}, /*index=5*/f32[2]{0:T(128)}, f32[2]{0:T(128)}, f32[128]{0:T(128)}) all-reduce(f32[192]{0:T(256)S(1)} %get-tuple-element.636, ...), channel_id=1, replica_groups=mesh['seq'=4,'head'=8] {'seq'}, use_global_device_ids=true, to_apply=%region_35.36 | all-reduce | flops 5318 | bytes 42544 | tf_op jit(solution)/shard_map/psum | solution.py:253
  788.9 25.9 %psum.115 = f32[4096]{0:T(1024)S(1)} all-reduce(f32[4096]{0:T(1024)S(1)} %get-tuple-element.637), channel_id=1, replica_groups=mesh['seq'=4,'head'=8] {'head'}, use_global_device_ids=true, to_apply=%region_33.34 | all-reduce | flops 4096 | bytes 32768 | tf_op jit(solution)/shard_map/psum | solution.py:248
  820.3 23.0 %all-reduce.15.cloned.1.call-done = (f32[1536,128]{1,0:T(8,128)}, f32[1536,128]{1,0:T(8,128)}, f32[192,256]{1,0:T(8,128)}, f32[128,1536]{1,0:T(8,128)}) async-done(((f32[1536,128]{1,0:T(8,128)}, f32[1536,128]{1,0:T(8,128)}, f32[192,256]{1,0:T(8,128)}, f32[128,1536]{1,0:T(8,128)}), (f32[1536,128]{1,0:T(8,128)}, f32[1536,128]{1,0:T(8,128)}, f32[192,256]{1,0:T(8,128)}, ...) | async-done | bytes 2555920 | tf_op jit(solution)/shard_map/psum | solution.py:253
  (487 shorter events, 360.7 us)
Async XLA Ops:
  7.2 41.0 %copy-start = (bf16[1536,256]{1,0:T(8,128)(2,1)S(1)}, bf16[1536,256]{1,0:T(8,128)(2,1)}, u32[]{:S(2)}) copy-start(bf16[1536,256]{1,0:T(8,128)(2,1)} %param.30) | copy-start | bytes 2359300
  7.2 493.8 %all-reduce.13.cloned.1.call-start = ((), (), s32[]{:S(2)}) async-start(), calls=%async_computation.2 | async-start | bytes 8388608 | tf_op jit(solution)/shard_map/psum | solution.py:190
  31.2 15.1 %copy-start.39 = (f32[4096]{0:T(1024)}, f32[4096]{0:T(1024)S(1)}, u32[]{:S(2)}) copy-start(f32[4096]{0:T(1024)S(1)} %add_rsqrt_fusion.1) | copy-start | bytes 49156
  52.8 20.5 %collective-permute-start = (bf16[3,384]{0,1:T(8,128)(2,1)}, bf16[3,384]{0,1:T(8,128)(2,1)S(1)}, u32[]{:S(2)}, u32[]{:S(2)}) collective-permute-start(bf16[3,384]{0,1:T(8,128)(2,1)} %pad_maximum_fusion.1), channel_id=1, source_target_pairs={{0,8},{8,16},{16,24},{1,9},{9,17},{17,25},{2,10},{10,18},{18,26},{... | collective-permute-start | bytes 6920 | tf_op jit(solution)/shard_map/ppermute | solution.py:18
  58.4 17.1 %copy-start.55 = (f32[384]{0:T(512)}, f32[384]{0:T(512)S(1)}, u32[]{:S(2)}) copy-start(f32[384]{0:T(512)S(1)} %get-tuple-element.651) | copy-start | bytes 4612
  58.4 17.1 %copy-start.57 = (f32[384]{0:T(512)}, f32[384]{0:T(512)S(1)}, u32[]{:S(2)}) copy-start(f32[384]{0:T(512)S(1)} %get-tuple-element.652) | copy-start | bytes 4612
  58.4 17.1 %copy-start.59 = (f32[384]{0:T(512)}, f32[384]{0:T(512)S(1)}, u32[]{:S(2)}) copy-start(f32[384]{0:T(512)S(1)} %get-tuple-element.653) | copy-start | bytes 4612
  58.4 17.1 %copy-start.61 = (f32[384]{0:T(512)}, f32[384]{0:T(512)S(1)}, u32[]{:S(2)}) copy-start(f32[384]{0:T(512)S(1)} %get-tuple-element.654) | copy-start | bytes 4612
  86.5 77.2 %copy-start.6 = (f32[16,8,16,256]{3,2,1,0:T(8,128)}, f32[16,8,16,256]{3,2,1,0:T(8,128)S(1)}, u32[]{:S(2)}) copy-start(f32[16,8,16,256]{3,2,1,0:T(8,128)S(1)} %copy.475) | copy-start | bytes 6291460
  165.7 16.7 %slice-start = ((s8[12582912]{0:T(1024)(128)(4,1)}), s8[4194304]{0:T(1024)(128)(4,1)S(1)}, s32[]{:S(2)}) async-start(s8[12582912]{0:T(1024)(128)(4,1)} %bitcast.321), calls=%async_computation.6 | async-start | bytes 8388608
  165.7 16.7 %slice-start.1 = ((s8[12582912]{0:T(1024)(128)(4,1)}), s8[4194304]{0:T(1024)(128)(4,1)S(1)}, s32[]{:S(2)}) async-start(s8[12582912]{0:T(1024)(128)(4,1)} %bitcast.321), calls=%async_computation.7 | async-start | bytes 8388608
  182.4 29.6 %copy-start.64 = (f32[128]{0:T(128)S(1)}, f32[128]{0:T(128)}, u32[]{:S(2)}) copy-start(f32[128]{0:T(128)} %param.39) | copy-start | bytes 1540
  186.0 36.5 %copy-start.4 = (f32[4096,128]{0,1:T(8,128)}, f32[4096,128]{0,1:T(8,128)S(1)}, u32[]{:S(2)}) copy-start(f32[4096,128]{0,1:T(8,128)S(1)} %get-tuple-element.724) | copy-start | bytes 6291460
  256.4 21.7 %copy-start.9 = (f32[16,8,16,256]{3,2,1,0:T(8,128)}, f32[16,8,16,256]{3,2,1,0:T(8,128)S(1)}, u32[]{:S(2)}) copy-start(f32[16,8,16,256]{3,2,1,0:T(8,128)S(1)} %copy.481) | copy-start | bytes 6291460
  261.7 16.5 %copy-start.20 = (f32[16,2,64,128]{3,2,1,0:T(8,128)S(1)}, f32[16,2,64,128]{3,2,1,0:T(8,128)}, u32[]{:S(2)}) copy-start(f32[16,2,64,128]{3,2,1,0:T(8,128)} %get-tuple-element.990) | copy-start | bytes 3145732
  407.1 237.9 %reduce-scatter.7.cloned.1.call-start = ((), (), s32[]{:S(2)}) async-start(), calls=%async_computation.3 | async-start | bytes 14155776 | tf_op jit(solution)/shard_map/reduce_scatter | solution.py:160
  434.2 328.2 %reduce-scatter.9.cloned.1.call-start = ((), (), s32[]{:S(2)}) async-start(), calls=%async_computation.4 | async-start | bytes 14155776 | tf_op jit(solution)/shard_map/reduce_scatter | solution.py:236
  450.7 50.3 %slice-start.6 = ((f32[4096,384]{0,1:T(8,128)}), f32[4096,128]{0,1:T(8,128)S(1)}, s32[]{:S(2)}) async-start(f32[4096,384]{0,1:T(8,128)} %copy-done.12), calls=%async_computation.12 | async-start | bytes 4194304 | tf_op jit(solution)/shard_map/slice | solution.py:191
  540.3 11.9 %collective-permute-start.1 = (f32[3,384]{0,1:T(8,128)S(1)}, f32[3,384]{0,1:T(8,128)S(1)}, u32[]{:S(2)}, u32[]{:S(2)}) collective-permute-start(f32[3,384]{0,1:T(8,128)S(1)} %slice.173), channel_id=1, source_target_pairs={{8,0},{16,8},{24,16},{9,1},{17,9},{25,17},{10,2},{18,10},{26,18},{... | collective-permute-start | bytes 13832 | tf_op jit(solution)/shard_map/ppermute | solution.py:18
  594.6 248.7 %all-reduce.15.cloned.1.call-start = ((), (), s32[]{:S(2)}) async-start(), calls=%async_computation.5 | async-start | bytes 5111808 | tf_op jit(solution)/shard_map/psum | solution.py:253
  618.6 15.8 %slice-start.3 = ((s8[12582912]{0:T(1024)(128)(4,1)}), s8[4194304]{0:T(1024)(128)(4,1)S(1)}, s32[]{:S(2)}) async-start(s8[12582912]{0:T(1024)(128)(4,1)} %bitcast.323), calls=%async_computation.9 | async-start | bytes 8388608
  618.7 15.8 %slice-start.4 = ((s8[12582912]{0:T(1024)(128)(4,1)}), s8[4194304]{0:T(1024)(128)(4,1)S(1)}, s32[]{:S(2)}) async-start(s8[12582912]{0:T(1024)(128)(4,1)} %bitcast.323), calls=%async_computation.10 | async-start | bytes 8388608
  762.4 52.4 %copy-start.26 = (bf16[4096,192]{0,1:T(8,128)(2,1)S(1)}, bf16[4096,192]{0,1:T(8,128)(2,1)}, u32[]{:S(2)}) copy-start(bf16[4096,192]{0,1:T(8,128)(2,1)} %copy.469) | copy-start | bytes 4718596
  762.4 52.4 %copy-start.40 = (f32[4096]{0:T(1024)S(1)}, f32[4096]{0:T(1024)}, u32[]{:S(2)}) copy-start(f32[4096]{0:T(1024)} %copy-done.39) | copy-start | bytes 49156
  (68 other events, 421.9 us)
Sparse Core Ops, SparseCore 0:
  407.2 93.7 all-reduce.12
  503.3 129.1 reduce-scatter.6
  634.8 127.5 reduce-scatter.8
  766.9 76.3 all-reduce.14
where the time goes:
time: 868 us; the launch traced here: 856 us
  matrix products  204 us (24%)
  waiting for transfers between devices  177 us (20%)
  other arithmetic  171 us (20%)
  local copies, waits for them, and re-layouts  160 us (18%)
  blocking collectives  122 us (14%)
  between operations  15.6 us (2%)
    reduce_scatter x1, waiting for transfers between devices, local(): lax.psum_scatter(total.astype(jnp.bfloat16), 'head', scatter_dimension=0,...  114 us
    unnamed x192, local copies, waits for them, and re-layouts  79.5 us
    psum x1, waiting for transfers between devices, local(): state_sum = lax.psum(grad_conv[:, inner_local:], 'head')  39.8 us
    dot_general x3, matrix products, local_mixer(): outputs = jnp.einsum('cijh,cjhp->cihp', weights, values, precision=highest)  36.8 us
    psum x1, blocking collectives, local(): hat_dot = lax.psum(jnp.sum(grad_hat * gated_hat, axis=1), 'head')  26.1 us
    psum x1, blocking collectives, local(): square_sum = lax.psum(jnp.sum(gated * gated, axis=1), 'head')  26 us
    psum x1, blocking collectives, local(): unit_dot = lax.psum(jnp.sum(grad_unit * normal_own, axis=1), 'head')  25.9 us
    all_gather x3, blocking collectives, prefix(): pieces = jax.tree.map(lambda part: lax.all_gather(part, axis), value)  25.7 us
  transfers between devices with their start and end apart: 6, of which 3 were waited for; matrix products, arithmetic and copies ran while one was open for 26% of the time, Pallas kernels for 0%

commit v1 on v0

v1 whole, which is shorter than its diff:
```python
from functools import partial

import jax
import jax.numpy as jnp
from jax import lax
from jax.experimental import pallas as pl
from jax.experimental.pallas import tpu as pltpu
from jax.sharding import PartitionSpec as P


SPAN = 256
epsilon = 1e-05
f32 = jnp.float32
bf16 = jnp.bfloat16


def mm(a, b):
    return jnp.dot(a, b, preferred_element_type=f32)


def mm_nt(a, b):
    return lax.dot_general(a, b, (((1,), (1,)), ((), ())), preferred_element_type=f32)


def mm_tn(a, b):
    return lax.dot_general(a, b, (((0,), (0,)), ((), ())), preferred_element_type=f32)


def halves(x):
    high = x.astype(bf16)
    return jnp.concatenate([high, (x - high.astype(f32)).astype(bf16)], axis=1)


def two(x):
    high = x.astype(bf16)
    return high, (x - high.astype(f32)).astype(bf16)


def left_terms(x, axis):
    high, low = two(x)
    return jnp.concatenate([high, high, low], axis=axis)


def right_terms(x):
    high, low = two(x)
    return jnp.concatenate([high, low, high], axis=0)


def wide_terms(x):
    high, low = two(x)
    return jnp.concatenate([high, low, high], axis=1)


def folded(x):
    width = x.shape[1] // 2
    return x[:, :width] + x[:, width:]


def logistic(x):
    return 1.0 / (1.0 + jnp.exp(-x))


def softplus(x):
    return jnp.maximum(x, 0.0) + jnp.log1p(jnp.exp(-jnp.abs(x)))


def iota(shape, axis):
    return lax.broadcasted_iota(jnp.int32, shape, axis)


def params(grid_axes=1, limit=56 << 20):
    return pltpu.CompilerParams(
        dimension_semantics=("arbitrary",) * grid_axes, vmem_limit_bytes=limit
    )


def spec(shape, index):
    return pl.BlockSpec(shape, index)


def whole_block(array):
    rank = array.ndim
    return pl.BlockSpec(array.shape, lambda *i: (0,) * rank)


def project_kernel(
    hidden_ref, gain_ref, gate_ref, value_ref, state_ref, step_ref,
    projected_ref, gate_out, stream_out, step_out, scale_out, weights,
):
    @pl.when(pl.program_id(0) == 0)
    def _():
        weights[:, 0:128] = gate_ref[...]
        weights[:, 128:256] = value_ref[...]
        weights[:, 256:512] = state_ref[...]
        weights[:, 512:640] = step_ref[...]

    hidden = hidden_ref[...].astype(f32)
    scale = lax.rsqrt(jnp.mean(hidden * hidden, axis=1, keepdims=True) + epsilon)
    projected = (hidden * scale * gain_ref[...]).astype(bf16)
    projected_ref[...] = projected
    scale_out[...] = jnp.broadcast_to(scale, scale_out.shape)
    result = mm(projected, weights[...])
    gate_out[...] = result[:, 0:128]
    stream_out[...] = result[:, 128:512].astype(bf16)
    step_out[...] = result[:, 512:640]


def project(hidden_in, norm_gain, gate_proj, value_proj, state_proj, step_wide):
    rows, width = hidden_in.shape
    span = 512
    row = lambda i: (i, 0)
    gain = norm_gain[None, :]
    return pl.pallas_call(
        project_kernel,
        grid=(rows // span,),
        in_specs=[
            spec((span, width), row), whole_block(gain), whole_block(gate_proj),
            whole_block(value_proj), whole_block(state_proj), whole_block(step_wide),
        ],
        out_specs=[
            spec((span, width), row), spec((span, 128), row), spec((span, 384), row),
            spec((span, 128), row), spec((span, 128), row),
        ],
        out_shape=[
            jax.ShapeDtypeStruct((rows, width), bf16),
            jax.ShapeDtypeStruct((rows, 128), f32),
            jax.ShapeDtypeStruct((rows, 384), bf16),
            jax.ShapeDtypeStruct((rows, 128), f32),
            jax.ShapeDtypeStruct((rows, 128), f32),
        ],
        scratch_shapes=[pltpu.VMEM((width, 640), bf16)],
        compiler_params=params(),
        cost_estimate=pl.CostEstimate(
            flops=2 * rows * width * 640, bytes_accessed=rows * width * 4, transcendentals=0
        ),
        name="project",
    )(hidden_in, gain, gate_proj, value_proj, state_proj, step_wide)


def convolved(ext, taps, bias):
    span = SPAN
    total = bias + taps[0:1] * ext[5 : 5 + span]
    for tap in range(1, 4):
        total = total + taps[tap : tap + 1] * ext[5 + tap : 5 + tap + span]
    return total


def running_sums(log_decay):
    span = log_decay.shape[0]
    lower = (iota((span, span), 0) >= iota((span, span), 1)).astype(bf16)
    return folded(mm(lower, halves(log_decay)))


def decay_matrix(running, running_rows, head):
    span = running.shape[0]
    at = 64 * head
    spread = running[:, at : at + 1] - running_rows[at : at + 1, :]
    return jnp.exp(jnp.where(iota((span, span), 0) >= iota((span, span), 1), spread, -jnp.inf))


def forward_kernel(
    stream_ref, edge_ref, step_ref, taps_ref, bias_ref, step_bias_ref, rate_ref, skip_ref,
    mixed_out, query_out, reach_out, states_out,
    ext, state, offset,
):
    span = SPAN
    first = pl.program_id(0) == 0

    @pl.when(first)
    def _():
        ext[0:8] = edge_ref[...].astype(f32)
        state[...] = jnp.zeros_like(state)
        offset[...] = jnp.zeros_like(offset)

    ext[8 : 8 + span] = stream_ref[...].astype(f32)
    conv = convolved(ext, taps_ref[...], bias_ref[...])
    ext[0:8] = ext[span : span + 8]
    active = conv * logistic(conv)
    values = active[:, 0:128]
    keys = active[:, 128:256]
    queries = active[:, 256:384]
    widths = softplus(step_ref[...] + step_bias_ref[...])
    running = running_sums(-rate_ref[...] * widths)
    running_rows = running.T
    last = running[span - 1 : span, :]
    fed = widths * values
    fed_terms = right_terms(fed)
    query_terms = left_terms(queries, 1)
    scores = mm_nt(query_terms, wide_terms(keys))
    low = iota((span, 128), 1) < 64
    heads = [
        mm(left_terms(scores * decay_matrix(running, running_rows, head), 1), fed_terms)
        for head in range(2)
    ]
    before = state[...]
    mixed = jnp.where(low, heads[0], heads[1])
    mixed = mixed + jnp.exp(running) * mm_nt(query_terms, wide_terms(before))
    mixed_out[...] = mixed + skip_ref[...] * values
    query_out[...] = queries
    reach_out[...] = running + offset[0:1]
    offset[...] = offset[...] + last
    tails = left_terms(jnp.exp(last - running) * fed, 0)
    after = jnp.exp(running_rows[:, span - 1 : span]) * before + mm_tn(tails, right_terms(keys))
    state[...] = after
    states_out[0] = after


def scan_forward(stream, edge, step, taps, bias, step_bias, rate, skip):
    rows = stream.shape[0]
    span = SPAN
    count = rows // span
    row = lambda i: (i, 0)
    return pl.pallas_call(
        forward_kernel,
        grid=(count,),
        in_specs=[
            spec((span, 384), row), whole_block(edge), spec((span, 128), row), whole_block(taps),
            whole_block(bias), whole_block(step_bias), whole_block(rate), whole_block(skip),
        ],
        out_specs=[
            spec((span, 128), row), spec((span, 128), row), spec((span, 128), row),
            spec((1, 128, 128), lambda i: (i, 0, 0)),
        ],
        out_shape=[
            jax.ShapeDtypeStruct((rows, 128), f32),
            jax.ShapeDtypeStruct((rows, 128), f32),
            jax.ShapeDtypeStruct((rows, 128), f32),
            jax.ShapeDtypeStruct((count, 128, 128), f32),
        ],
        scratch_shapes=[
            pltpu.VMEM((span + 8, 384), f32), pltpu.VMEM((128, 128), f32), pltpu.VMEM((8, 128), f32),
        ],
        compiler_params=params(),
        cost_estimate=pl.CostEstimate(
            flops=count * 2 * span * span * 600, bytes_accessed=rows * 128 * 20, transcendentals=0
        ),
        name="scan_forward",
    )(stream, edge, step, taps, bias, step_bias, rate, skip)


def join_kernel(
    mixed_ref, query_ref, reach_ref, gate_ref, grad_ref, carried_ref, gain_ref, mixed_out, sums_out
):
    inner = mm_nt(left_terms(query_ref[...], 1), wide_terms(carried_ref[...]))
    mixed = mixed_ref[...] + jnp.exp(reach_ref[...]) * inner
    mixed_out[...] = mixed
    gate = gate_ref[...]
    gated = mixed * (gate * logistic(gate))
    sums_out[0:1, :] = jnp.sum((gated * gated).T, axis=0, keepdims=True)
    sums_out[1:2, :] = jnp.sum((grad_ref[...] * gain_ref[...] * gated).T, axis=0, keepdims=True)


def join(mixed, query, reach, gate, grad, carried, gain):
    rows = mixed.shape[0]
    block = 512
    row = lambda i: (i, 0)
    blocks = spec((block, 128), row)
    return pl.pallas_call(
        join_kernel,
        grid=(rows // block,),
        in_specs=[blocks] * 5 + [whole_block(carried), whole_block(gain)],
        out_specs=[blocks, spec((2, block), lambda i: (0, i))],
        out_shape=[
            jax.ShapeDtypeStruct((rows, 128), f32), jax.ShapeDtypeStruct((2, rows), f32),
        ],
        compiler_params=params(),
        cost_estimate=pl.CostEstimate(
            flops=2 * rows * 128 * 128, bytes_accessed=rows * 128 * 22, transcendentals=0
        ),
        name="join",
    )(mixed, query, reach, gate, grad, carried, gain)


def gate_kernel(
    inner_width,
    mixed_ref, query_ref, reach_ref, gate_ref, grad_ref, sums_ref, gain_ref,
    rows_out, gate_out, mixed_grad_out, gain_out, incoming_out,
):
    @pl.when(pl.program_id(0) == 0)
    def _():
        gain_out[...] = jnp.zeros_like(gain_out)
        incoming_out[...] = jnp.zeros_like(incoming_out)

    block = mixed_ref.shape[0]
    square = jnp.broadcast_to(sums_ref[0:1, :], (128, block)).T
    product = jnp.broadcast_to(sums_ref[1:2, :], (128, block)).T
    scale = lax.rsqrt(square / inner_width + epsilon)
    gate = gate_ref[...]
    chance = logistic(gate)
    act = gate * chance
    mixed = mixed_ref[...]
    hat = mixed * act * scale
    rows_out[...] = (hat * gain_ref[...]).astype(bf16)
    grad = grad_ref[...]
    gain_out[...] += jnp.sum(grad * hat, axis=0, keepdims=True)
    pre = scale * (grad * gain_ref[...] - hat * (product * scale / inner_width))
    mixed_grad = pre * act
    mixed_grad_out[...] = mixed_grad
    gate_out[...] = (pre * mixed * (chance * (1.0 + gate * (1.0 - chance)))).astype(bf16)
    incoming_out[...] += mm_tn(
        left_terms(jnp.exp(reach_ref[...]) * mixed_grad, 0), right_terms(query_ref[...])
    )


def gate_step(mixed, query, reach, gate, grad, sums, gain, inner_width):
    rows = mixed.shape[0]
    block = 512
    row = lambda i: (i, 0)
    blocks = spec((block, 128), row)
    return pl.pallas_call(
        partial(gate_kernel, inner_width),
        grid=(rows // block,),
        in_specs=[blocks] * 5 + [spec((2, block), lambda i: (0, i)), whole_block(gain)],
        out_specs=[
            blocks, blocks, blocks, spec((1, 128), lambda i: (0, 0)),
            spec((128, 128), lambda i: (0, 0)),
        ],
        out_shape=[
            jax.ShapeDtypeStruct((rows, 128), bf16),
            jax.ShapeDtypeStruct((rows, 128), bf16),
            jax.ShapeDtypeStruct((rows, 128), f32),
            jax.ShapeDtypeStruct((1, 128), f32),
            jax.ShapeDtypeStruct((128, 128), f32),
        ],
        compiler_params=params(),
        cost_estimate=pl.CostEstimate(
            flops=2 * rows * 128 * 128, bytes_accessed=rows * 128 * 26, transcendentals=0
        ),
        name="gate_step",
    )(mixed, query, reach, gate, grad, sums, gain)


def head_sums(x):
    same = (iota((128, 128), 0) < 64) == (iota((128, 128), 1) < 64)
    ones = same.astype(bf16)
    high = x.astype(bf16)
    return mm(high, ones) + mm((x - high.astype(f32)).astype(bf16), ones)


def backward_kernel(
    stream_ref, before_ref, edge_ref, step_ref, taps_ref, bias_ref, step_bias_ref, rate_ref,
    skip_ref, mixed_ref, grad_ref, reach_ref, start_ref, end_ref, carried_ref, arriving_ref,
    stream_grad_out, tail_out, head_out, sums_out,
    ext, grads, state_grad,
):
    span = SPAN
    count = pl.num_programs(0)
    chunk = count - 1 - pl.program_id(0)

    @pl.when(pl.program_id(0) == 0)
    def _():
        state_grad[...] = arriving_ref[...]
        grads[span : span + 8] = jnp.zeros_like(grads[span : span + 8])
        sums_out[...] = jnp.zeros_like(sums_out)

    @pl.when(chunk == 0)
    def _():
        ext[0:8] = edge_ref[...].astype(f32)

    @pl.when(chunk > 0)
    def _():
        ext[0:8] = before_ref[8:16].astype(f32)

    ext[8 : 8 + span] = stream_ref[...].astype(f32)
    taps = taps_ref[...]
    conv = convolved(ext, taps, bias_ref[...])
    chance = logistic(conv)
    active = conv * chance
    slope = chance * (1.0 + conv * (1.0 - chance))
    values = active[:, 0:128]
    keys = active[:, 128:256]
    queries = active[:, 256:384]
    keys16 = keys.astype(bf16)
    step = step_ref[...] + step_bias_ref[...]
    rate = rate_ref[...]
    widths = softplus(step)
    running = running_sums(-rate * widths)
    running_rows = running.T
    last = running[span - 1 : span, :]
    fed = widths * values
    fed16 = fed.astype(bf16)
    grad = grad_ref[...]
    grad16 = grad.astype(bf16)
    scores = mm_nt(queries.astype(bf16), keys16)
    low = iota((span, 128), 1) < 64
    grad_turned = pltpu.roll(grad, 64, 1)
    fed_turned = pltpu.roll(fed, 64, 1)
    score_grad = None
    fed_grads = []
    for head in range(2):
        decay = decay_matrix(running, running_rows, head)
        mine = low == (head == 0)
        grad_high, grad_low = two(jnp.where(mine, grad, grad_turned))
        left = [jnp.where(low, grad_high, grad_low), jnp.where(low, grad_high, 0)]
        right = two(jnp.where(mine, fed, fed_turned))
        part = mm_nt(jnp.concatenate(left, axis=1), jnp.concatenate(right, axis=1)) * decay
        score_grad = part if score_grad is None else score_grad + part
        fed_grads.append(mm_tn((scores * decay).astype(bf16), grad16))

    offset = (reach_ref[span - 8 : span, :] - running[span - 8 : span, :]).T[:, 7:8]
    carried = jnp.exp(offset) * carried_ref[...]
    before = jnp.where(chunk > 0, start_ref[0], 0.0) + carried
    last_rows = jnp.exp(running_rows[:, span - 1 : span])
    after = end_ref[0] + last_rows * carried
    after_grad = state_grad[...]
    tail = jnp.exp(last - running)
    reached = jnp.exp(running) * grad
    query_terms = right_terms(queries)
    fed_grad = jnp.where(low, fed_grads[0], fed_grads[1])
    fed_grad = fed_grad + tail * mm_nt(keys16, after_grad.astype(bf16))
    score_high, score_low = two(score_grad)
    query_grad = mm(
        jnp.concatenate([score_high, score_high, score_low], axis=1), right_terms(keys)
    ) + mm(left_terms(reached, 1), right_terms(before))
    key_grad = mm_tn(
        jnp.concatenate([score_high, score_high, score_low], axis=0), query_terms
    ) + mm(left_terms(tail * fed, 1), right_terms(after_grad))
    state_grad[...] = last_rows * after_grad + mm_tn(left_terms(reached, 0), query_terms)
    value_grad = widths * fed_grad + skip_ref[...] * grad

    mixed = mixed_ref[...] - skip_ref[...] * values
    balance = head_sums(grad16.astype(f32) * mixed - fed16.astype(f32) * fed_grad)
    upper = (iota((span, span), 0) <= iota((span, span), 1)).astype(bf16)
    boundary = head_sums(
        jnp.broadcast_to(jnp.sum((after_grad * after).T, axis=0, keepdims=True), (8, 128))
    )
    decay_grad = folded(mm(upper, halves(balance))) + boundary[0:1]
    width_grad = head_sums(values * fed_grad) - rate * decay_grad
    step_grad = width_grad * logistic(step)
    sums_out[0:1, 384:512] += jnp.sum(step_grad, axis=0, keepdims=True)
    sums_out[1:2, 384:512] += jnp.sum(-widths * decay_grad, axis=0, keepdims=True)
    sums_out[2:3, 384:512] += jnp.sum(grad * values, axis=0, keepdims=True)

    conv_grad = jnp.concatenate([value_grad, key_grad, query_grad], axis=1) * slope
    grads[0:span] = conv_grad
    for tap in range(4):
        sums_out[tap : tap + 1, 0:384] += jnp.sum(
            conv_grad * ext[5 + tap : 5 + tap + span], axis=0, keepdims=True
        )
    sums_out[4:5, 0:384] += jnp.sum(conv_grad, axis=0, keepdims=True)
    stream_grad = taps[3:4] * conv_grad
    for tap in range(3):
        stream_grad = stream_grad + taps[tap : tap + 1] * grads[3 - tap : 3 - tap + span]
    high = stream_grad.astype(bf16)
    stream_grad_out[:, 0:384] = high
    stream_grad_out[:, 384:512] = step_grad.astype(bf16)
    stream_grad_out[:, 512:768] = (stream_grad - high.astype(f32))[:, 128:384].astype(bf16)

    @pl.when(pl.program_id(0) == 0)
    def _():
        tail_out[...] = stream_grad[span - 8 :]

    head_out[...] = conv_grad[0:8]
    grads[span : span + 8] = conv_grad[0:8]


def scan_backward(
    stream, edge, step, taps, bias, step_bias, rate, skip, mixed, grad, reach, states, carried,
    arriving,
):
    rows = stream.shape[0]
    span = SPAN
    count = rows // span
    row = lambda i: (count - 1 - i, 0)
    fixed = lambda i: (0, 0)
    return pl.pallas_call(
        backward_kernel,
        grid=(count,),
        in_specs=[
            spec((span, 384), row),
            spec((16, 384), lambda i: (jnp.maximum((count - 1 - i) * (span // 16) - 1, 0), 0)),
            whole_block(edge), spec((span, 128), row), whole_block(taps), whole_block(bias),
            whole_block(step_bias), whole_block(rate), whole_block(skip), spec((span, 128), row),
            spec((span, 128), row), spec((span, 128), row),
            spec((1, 128, 128), lambda i: (jnp.maximum(count - 2 - i, 0), 0, 0)),
            spec((1, 128, 128), lambda i: (count - 1 - i, 0, 0)),
            whole_block(carried), whole_block(arriving),
        ],
        out_specs=[
            spec((span, 768), row), spec((8, 384), fixed), spec((8, 384), fixed),
            spec((8, 512), fixed),
        ],
        out_shape=[
            jax.ShapeDtypeStruct((rows, 768), bf16),
            jax.ShapeDtypeStruct((8, 384), f32),
            jax.ShapeDtypeStruct((8, 384), f32),
            jax.ShapeDtypeStruct((8, 512), f32),
        ],
        scratch_shapes=[
            pltpu.VMEM((span + 8, 384), f32), pltpu.VMEM((span + 8, 384), f32),
            pltpu.VMEM((128, 128), f32),
        ],
        compiler_params=params(),
        cost_estimate=pl.CostEstimate(
            flops=count * 2 * span * span * 1200, bytes_accessed=rows * 128 * 30, transcendentals=0
        ),
        name="scan_backward",
    )(
        stream, stream, edge, step, taps, bias, step_bias, rate, skip, mixed, grad, reach, states,
        states, carried, arriving,
    )


def parts_kernel(
    gate_ref, rest_ref, weights_ref, hidden_ref, scale_ref, gain_ref, tail_ref, next_ref, taps_ref,
    parts_out, dots_out, sums_out,
    left, edge,
):
    @pl.when(pl.program_id(0) == 0)
    def _():
        sums_out[...] = jnp.zeros_like(sums_out)

    block = left.shape[0]
    left[:, 0:128] = gate_ref[...]
    left[:, 128:896] = rest_ref[...]

    @pl.when(pl.program_id(0) == pl.num_programs(0) - 1)
    def _():
        edge[0:8] = jnp.zeros_like(edge[0:8])
        edge[8:16] = next_ref[...]
        fixed = tail_ref[...]
        for tap in range(3):
            fixed = fixed + taps_ref[tap : tap + 1] * edge[3 - tap : 11 - tap]
        high = fixed.astype(bf16)
        left[block - 8 :, 128:512] = high
        left[block - 8 :, 640:896] = (fixed - high.astype(f32))[:, 128:].astype(bf16)

    groups, _, share = parts_out.shape
    total = mm(left[...], weights_ref[...]).astype(bf16)
    scale = scale_ref[...]
    summed = None
    for at in range(0, total.shape[1], 128):
        lanes = slice(at, at + 128)
        product = total[:, lanes].astype(f32) * (hidden_ref[:, lanes].astype(f32) * scale)
        sums_out[0:1, lanes] += jnp.sum(product, axis=0, keepdims=True)
        product = product * gain_ref[:, lanes]
        summed = product if summed is None else summed + product
    dots_out[...] = jnp.sum(summed.T, axis=0, keepdims=True)
    for group in range(groups):
        parts_out[group] = total[:, group * share : (group + 1) * share]


def input_parts(
    gate16, rest16, weights, hidden_in, scale, gain, tail, next_head, taps, groups
):
    rows, width = hidden_in.shape
    block = 512
    row = lambda i: (i, 0)
    share = width // groups
    return pl.pallas_call(
        parts_kernel,
        grid=(rows // block,),
        in_specs=[
            spec((block, 128), row), spec((block, 768), row), whole_block(weights),
            spec((block, width), row), spec((block, 128), row), whole_block(gain),
            whole_block(tail), whole_block(next_head), whole_block(taps),
        ],
        out_specs=[
            spec((groups, block, share), lambda i: (0, i, 0)), spec((1, block), lambda i: (0, i)),
            spec((1, width), lambda i: (0, 0)),
        ],
        out_shape=[
            jax.ShapeDtypeStruct((groups, rows, share), bf16),
            jax.ShapeDtypeStruct((1, rows), f32),
            jax.ShapeDtypeStruct((1, width), f32),
        ],
        scratch_shapes=[pltpu.VMEM((block, 896), bf16), pltpu.VMEM((16, 384), f32)],
        compiler_params=params(),
        cost_estimate=pl.CostEstimate(
            flops=2 * rows * width * 896, bytes_accessed=rows * width * 5, transcendentals=0
        ),
        name="input_parts",
    )(gate16, rest16, weights, hidden_in, scale, gain, tail, next_head, taps)


def output_kernel(rows_ref, weights_ref, hidden_ref, parts_out):
    groups, _, share = parts_out.shape
    total = hidden_ref[...].astype(f32)
    summed = None
    for group in range(groups):
        term = mm(rows_ref[group], weights_ref[group]).astype(bf16).astype(f32)
        summed = term if summed is None else summed + term
    total = (total + summed).astype(bf16)
    for group in range(groups):
        parts_out[group] = total[:, group * share : (group + 1) * share]


def output_rows(rows, weights, hidden):
    groups, tokens, inner = rows.shape
    width = hidden.shape[1]
    block = 128
    share = width // groups
    return pl.pallas_call(
        output_kernel,
        grid=(tokens // block,),
        in_specs=[
            spec((groups, block, inner), lambda i: (0, i, 0)), whole_block(weights),
            spec((block, width), lambda i: (i, 0)),
        ],
        out_specs=spec((groups, block, share), lambda i: (0, i, 0)),
        out_shape=jax.ShapeDtypeStruct((groups, tokens, share), bf16),
        compiler_params=params(),
        cost_estimate=pl.CostEstimate(
            flops=2 * tokens * groups * inner * width, bytes_accessed=8 << 20, transcendentals=0
        ),
        name="output_rows",
    )(rows, weights, hidden)


def passed_along(block, axis, distance):
    devices = range(lax.axis_size(axis))
    route = [(i - distance, i) for i in devices if i - distance in devices]
    return lax.ppermute(block, axis, route)


def bits_of(axis):
    count = lax.axis_size(axis)
    assert count & (count - 1) == 0
    return [1 << n for n in range(count.bit_length() - 1)]


def summed_over(value, axis, turned=False):
    count = lax.axis_size(axis)
    bits = bits_of(axis)
    for bit in reversed(bits) if turned else bits:
        value = value + lax.ppermute(value, axis, [(i, i ^ bit) for i in range(count)])
    return value


def scattered_sum(value, axis):
    count = lax.axis_size(axis)
    bits = bits_of(axis)
    mine = lax.axis_index(axis)
    value = value.reshape([2] * len(bits) + [value.shape[0] // count] + list(value.shape[1:]))
    for place, bit in enumerate(bits):
        at = len(bits) - 1 - place
        own = (mine // bit) % 2
        kept = lax.dynamic_index_in_dim(value, own, at, False)
        sent = lax.dynamic_index_in_dim(value, 1 - own, at, False)
        value = kept + lax.ppermute(sent, axis, [(i, i ^ bit) for i in range(count)])
    return value


def chained(states, decays, mine, backward):
    count = states.shape[0]
    order = range(count)
    if backward:
        order = reversed(order)
    total = jnp.zeros_like(states[0])
    for at in order:
        use = at > mine if backward else at < mine
        total = jnp.where(use, decays[at][:, None] * total + states[at], total)
    return total


def block(
    hidden_in, norm_gain, gate_proj, value_proj, state_proj, step_proj, conv_value,
    conv_value_bias, conv_state, conv_state_bias, step_bias, decay_rate, skip_gain, mix_gain,
    out_proj, out_grad,
):
    rows, width = hidden_in.shape
    groups = lax.axis_size("head")
    share = width // groups
    mine = lax.axis_index("head")
    first_col = mine * share
    inner_local = gate_proj.shape[1]
    inner_width = inner_local * groups
    heads = step_proj.shape[1]
    head_size = inner_local // heads

    def wide(x):
        return jnp.repeat(x, head_size, axis=-1)

    step_wide = wide(step_proj)
    rate, skip, step_shift = (wide(x)[None, :] for x in (decay_rate, skip_gain, step_bias))
    taps = jnp.concatenate([conv_value, conv_state], axis=1)
    bias = jnp.concatenate([conv_value_bias, conv_state_bias])[None, :]
    gain = mix_gain[None, :]

    all_out_proj = lax.all_gather(out_proj, "head")
    projected, gate_in, stream, step, scale_in = project(
        hidden_in, norm_gain, gate_proj, value_proj, state_proj, step_wide
    )
    edge = passed_along(stream[rows - 8 :], "seq", 1)
    grad_gated = lax.dot_general(
        out_grad, out_proj, (((1,), (1,)), ((), ())), preferred_element_type=f32
    )
    partial_mixed, queries, reach, states = scan_forward(
        stream, edge, step, taps, bias, step_shift, rate, skip
    )
    place = lax.axis_index("seq")
    decay_here = jnp.exp(reach[rows - 1])
    packed = jnp.concatenate([states[-1], jnp.broadcast_to(decay_here[None, :], (8, 128))])
    gathered = lax.all_gather(packed, "seq")
    decays = gathered[:, 128]
    carried = chained(gathered[:, :128], decays, place, False)
    mixed, sums = join(partial_mixed, queries, reach, gate_in, grad_gated, carried, gain)
    sums = summed_over(sums, "head")
    gated_rows, grad_gate16, grad_mixed, grad_mix_gain, incoming = gate_step(
        mixed, queries, reach, gate_in, grad_gated, sums, gain, inner_width
    )

    own_tokens = rows // groups
    group_rows = lax.all_to_all(
        gated_rows.reshape(groups, own_tokens, inner_local), "head", 0, 0, tiled=False
    )
    hidden_rows = lax.dynamic_slice_in_dim(hidden_in, mine * own_tokens, own_tokens, 0)
    out_parts = output_rows(group_rows, all_out_proj, hidden_rows)
    block_out = lax.all_to_all(out_parts, "head", 0, 0, tiled=False).reshape(rows, share)

    arriving = chained(lax.all_gather(incoming, "seq"), decays, place, True)
    rest16, tail, head, sums = scan_backward(
        stream, edge, step, taps, bias, step_shift, rate, skip, mixed, grad_mixed, reach,
        states, carried, arriving,
    )
    next_head = passed_along(head, "seq", -1)
    step_back = wide(step_proj).T * (1.0 / head_size)
    weights = jnp.concatenate(
        [gate_proj.T, value_proj.T, state_proj.T, step_back.astype(bf16), state_proj.T], axis=0
    )
    parts, dots, norm_sums = input_parts(
        grad_gate16, rest16, weights, hidden_in, scale_in, norm_gain[None, :], tail, next_head,
        taps, groups,
    )
    grad_projected = lax.psum_scatter(parts, "head", scatter_dimension=0, tiled=False).astype(f32)

    rest16, next_head, projected, _ = lax.optimization_barrier(
        (rest16, next_head, projected, parts)
    )
    extra = [sum(taps[tap] * next_head[row - tap] for tap in range(row + 1)) for row in range(3)]
    tail = tail.at[5:].add(jnp.stack(extra))
    tail16 = tail.astype(bf16)
    rest16 = lax.dynamic_update_slice(rest16, tail16, (rows - 8, 0))
    low16 = (tail - tail16.astype(f32))[:, inner_local:].astype(bf16)
    rest16 = lax.dynamic_update_slice(rest16, low16, (rows - 8, 512))
    grad_gate_proj = lax.dot_general(
        projected, grad_gate16, (((0,), (0,)), ((), ())), preferred_element_type=f32
    )
    gated_rows, _ = lax.optimization_barrier((gated_rows, parts))
    grad_out_proj = lax.dot_general(
        gated_rows, out_grad, (((0,), (0,)), ((), ())), preferred_element_type=f32
    )
    grad_rest = lax.dot_general(
        projected, rest16, (((0,), (0,)), ((), ())), preferred_element_type=f32
    )
    grad_gate_proj = summed_over(grad_gate_proj, "seq")
    grad_out_proj = summed_over(grad_out_proj, "seq", True)
    grad_value_proj = summed_over(grad_rest[:, :128], "seq")
    grad_state_proj = scattered_sum(grad_rest[:, 128:384] + grad_rest[:, 512:768], "head")
    grad_state_proj = summed_over(grad_state_proj, "seq", True)
    grad_step_proj = summed_over(grad_rest[:, 384:512:head_size].T, "seq", True).T

    sums = sums.at[5, :128].set(grad_mix_gain[0])
    small = summed_over(
        jnp.concatenate([sums.reshape(-1), norm_sums.reshape(-1)]).reshape(-1, 128), "seq"
    )
    total = summed_over(jnp.concatenate([small, dots.reshape(-1, 128)]), "head").reshape(-1)
    small = small.reshape(-1)
    sums = small[: 8 * 512].reshape(8, 512)
    state_sums = total[: 8 * 512].reshape(8, 512)[:, 128:384]
    grad_norm_gain = lax.dynamic_slice_in_dim(total, 8 * 512 + first_col, share, 0)
    unit_dot = total[8 * 512 + width :]

    hidden_own = lax.dynamic_slice_in_dim(hidden_in, first_col, share, 1).astype(f32)
    gain_own = lax.dynamic_slice_in_dim(norm_gain, first_col, share, 0)
    scale_col = scale_in[:, :1]
    normal_own = hidden_own * scale_col
    grad_unit = grad_projected * gain_own[None, :]
    grad_input = scale_col * (grad_unit - normal_own * (unit_dot / width)[:, None])
    grad_input = grad_input + lax.dynamic_slice_in_dim(out_grad, first_col, share, 1).astype(f32)

    head_rows = sums[:3, 384:512].reshape(3, heads, head_size)
    return (
        block_out,
        grad_input,
        grad_norm_gain,
        grad_gate_proj,
        grad_value_proj,
        grad_state_proj,
        grad_step_proj,
        sums[:4, :128],
        sums[4, :128],
        state_sums[:4],
        state_sums[4],
        head_rows[0, :, 0],
        head_rows[1, :, 0],
        jnp.sum(head_rows[2], axis=1),
        sums[5, :128],
        grad_out_proj,
    )


def solution(mesh):
    in_specs = (
        P("seq", None), P(), P(None, "head"), P(None, "head"), P(), P(None, "head"),
        P(None, "head"), P("head"), P(), P(), P("head"), P("head"), P("head"), P("head"),
        P("head", None), P("seq", None),
    )
    out_specs = (
        P("seq", "head"), P("seq", "head"), P("head"), P(None, "head"), P(None, "head"),
        P("head", None), P(None, "head"), P(None, "head"), P("head"), P(), P(), P("head"),
        P("head"), P("head"), P("head"), P("head", None),
    )
    return jax.shard_map(block, mesh=mesh, in_specs=in_specs, out_specs=out_specs, check_vma=False)
```

time: 868 us -> 436 us (0.50)
  the two profiles are of different devices: /device:TPU:0 before, /device:TPU:9 now
where the time goes in v1:
time: 436 us; the launch traced here: 433 us
  Pallas kernels  122 us (28%)
  waiting for transfers between devices  111 us (25%)
  local copies, waits for them, and re-layouts  52.1 us (12%)
  starting transfers between devices  43.3 us (10%)
  matrix products  41.1 us (9%)
  other arithmetic  35.5 us (8%)
  between operations  14.6 us (3%)
  blocking collectives  13.7 us (3%)
    ppermute x3, waiting for transfers between devices, scattered_sum(): lax.ppermute(sent, axis, [(i, i ^ bit) for i in range(count)])  65.6 us
    pallas_call x1, Pallas kernels, scan_backward(): pl.pallas_call(backward_kernel, grid=(count,), in_specs=[spec((span, 384)...  35.8 us
    pallas_call x1, Pallas kernels, input_parts(): pl.pallas_call(parts_kernel, grid=(rows // block,), in_specs=[spec((block...  23.4 us
    reduce_scatter x1, waiting for transfers between devices, block(): lax.psum_scatter(parts, 'head', scatter_dimension=0, tiled=False)  22 us
    ppermute x18, waiting for transfers between devices, summed_over(): lax.ppermute(value, axis, [(i, i ^ bit) for i in range(count)])  20.8 us
    pallas_call x1, Pallas kernels, scan_forward(): pl.pallas_call(forward_kernel, grid=(count,), in_specs=[spec((span, 384),...  20.1 us
    ppermute x18, starting transfers between devices, summed_over(): lax.ppermute(value, axis, [(i, i ^ bit) for i in range(count)])  18.3 us
    add x17, other arithmetic, summed_over(): value + lax.ppermute(value, axis, [(i, i ^ bit) for i in range(count)])  17.8 us
  transfers between devices with their start and end apart: 27, of which 7 were waited for; matrix products, arithmetic and copies ran while one was open for 26% of the time, Pallas kernels for 28%

profile of v1, /device:TPU:9, one launch (start us, length us, event | category | flops | bytes accessed | tf_op | source)
XLA Modules:
  0.0 433.5 jit_solution(3684771973183146687)
XLA Ops:
  10.9 17.2 %project.1 = (bf16[4096,1536]{1,0:T(8,128)(2,1)}, f32[4096,128]{1,0:T(8,128)}, bf16[4096,384]{1,0:T(8,128)(2,1)}, f32[4096,128]{1,0:T(8,128)}, f32[4096,128]{1,0:T(8,128)}) custom-call(bf16[4096,1536]{1,0:T(8,128)(2,1)} %hidden_ref.3, f32[1,1536]{1,0:T(1,128)} %broadcast_in_dim.33.gain_ref, bf16[1536,128]{1,0:T(8,128)(2,1)} %gate_ref.1, ...), custom_call_target="tpu_custom_call" | custom-call | flops 8053063680 | bytes 25165824 | tf_op jit(solution)/shard_map/project/pallas_call | solution.py:113
  32.3 7.9 %fusion.23.grad_ref = f32[4096,128]{1,0:T(8,128)} fusion(bf16[4096,1536]{1,0:T(8,128)(2,1)} %param.35, bf16[128,1536]{1,0:T(8,128)(2,1)S(1)} %copy-done.2), kind=kOutput, calls=%fused_computation.73 | convolution fusion | flops 1610612736 | bytes 15073280 | tf_op jit(solution)/shard_map/dot_general | solution.py:685
  44.3 20.1 %scan_forward.1 = (f32[4096,128]{1,0:T(8,128)}, f32[4096,128]{1,0:T(8,128)}, f32[4096,128]{1,0:T(8,128)}, f32[16,128,128]{2,1,0:T(8,128)}) custom-call(bf16[4096,384]{1,0:T(8,128)(2,1)} %get-tuple-element.67.stream_ref.before_ref, bf16[8,384]{1,0:T(8,128)(2,1)} %copy-done.12, f32[4096,128]{1,0:T(8,128)} %get-tuple-element.68.step_ref, f32[4,384]{1,0:T(4,128)} %copy-done.9, ...), custom_call_target="tpu_custom_call" | custom-call | flops 1258291200 | bytes 10485760 | tf_op jit(solution)/shard_map/scan_forward/pallas_call | solution.py:213
  66.0 7.2 %all-gather = f32[544,128]{1,0:T(8,128)S(1)} all-gather(f32[136,128]{1,0:T(8,128)S(1)} %pad_maximum_fusion), channel_id=2, replica_groups=mesh['seq'=4,'head'=8] {'seq'}, dimensions={0}, use_global_device_ids=true | all-gather | bytes 348160 | tf_op jit(solution)/shard_map/all_gather | solution.py:694
  73.9 8.6 %join.1 = (f32[4096,128]{1,0:T(8,128)}, f32[2,4096]{1,0:T(2,128)}) custom-call(f32[4096,128]{1,0:T(8,128)} %get-tuple-element.69.mixed_ref, f32[4096,128]{1,0:T(8,128)} %get-tuple-element.70.query_ref, f32[4096,128]{1,0:T(8,128)} %get-tuple-element.71.reach_ref, f32[4096,128]{1,0:T(8,128)} %get-tuple-element.72.gate_ref, f32[4096,128]{1,0:T(8,128)} %fusion.23.grad_ref, ...), custom_call_target="tpu_custom_call" | custom-call | flops 134217728 | bytes 11534336 | tf_op jit(solution)/shard_map/join/pallas_call | solution.py:258
  82.5 3.4 collective-permute-start.1
  95.0 9.1 %gate_step.1 = (bf16[4096,128]{1,0:T(8,128)(2,1)}, bf16[4096,128]{1,0:T(8,128)(2,1)}, f32[4096,128]{1,0:T(8,128)}, f32[1,128]{1,0:T(1,128)}, f32[128,128]{1,0:T(8,128)}) custom-call(f32[4096,128]{1,0:T(8,128)} %get-tuple-element.74.mixed_ref, f32[4096,128]{1,0:T(8,128)} %get-tuple-element.70.query_ref, f32[4096,128]{1,0:T(8,128)} %get-tuple-element.71.reach_ref, ...), custom_call_target="tpu_custom_call" | custom-call | flops 134217728 | bytes 13631488 | tf_op jit(solution)/shard_map/gate_step/pallas_call | solution.py:310
  104.1 6.6 %all-gather.2 = f32[512,128]{1,0:T(8,128)S(1)} all-gather(f32[128,128]{1,0:T(8,128)} %get-tuple-element.80), channel_id=4, replica_groups=mesh['seq'=4,'head'=8] {'seq'}, dimensions={0}, use_global_device_ids=true | all-gather | bytes 327680 | tf_op jit(solution)/shard_map/all_gather | solution.py:711
  111.4 35.8 %scan_backward.1 = (bf16[4096,768]{1,0:T(8,128)(2,1)}, f32[8,384]{1,0:T(8,128)}, f32[8,384]{1,0:T(8,128)}, f32[8,512]{1,0:T(8,128)}) custom-call(bf16[4096,384]{1,0:T(8,128)(2,1)} %get-tuple-element.67.stream_ref.before_ref, bf16[4096,384]{1,0:T(8,128)(2,1)} %get-tuple-element.67.stream_ref.before_ref, bf16[8,384]{1,0:T(8,128)(2,1)} %copy-done.12, ...), custom_call_target="tpu_custom_call" | custom-call | flops 2516582400 | bytes 15728640 | tf_op jit(solution)/shard_map/scan_backward/pallas_call | solution.py:466
  152.5 23.4 %input_parts.1 = (bf16[8,4096,192]{2,1,0:T(8,128)(2,1)}, f32[1,4096]{1,0:T(1,128)}, f32[1,1536]{1,0:T(1,128)}) custom-call(bf16[4096,128]{1,0:T(8,128)(2,1)} %get-tuple-element.78.gate_ref, bf16[4096,768]{1,0:T(8,128)(2,1)} %get-tuple-element.91.rest_ref, bf16[896,1536]{1,0:T(8,128)(2,1)} %bitcast_dynamic-update-slice_fusion.1.weights_ref, ...), custom_call_target="tpu_custom_call" | custom-call | flops 11274289152 | bytes 31457280 | tf_op jit(solution)/shard_map/input_parts/pallas_call | solution.py:550
  180.8 10.2 %all-to-all-start = ((bf16[8,512,128]{2,1,0:T(8,128)(2,1)}), bf16[8,512,128]{2,1,0:T(8,128)(2,1)S(1)}, u32[]{:S(2)}, u32[]{:S(2)}) async-start(bf16[8,512,128]{2,1,0:T(8,128)(2,1)} %bitcast.13), calls=%async_computation | async-start | bytes 2097152 | tf_op jit(solution)/shard_map/all_to_all | solution.py:704
  193.6 16.3 %fusion.25 = f32[1536,768]{1,0:T(8,128)} fusion(bf16[4096,1536]{1,0:T(8,128)(2,1)} %get-tuple-element.90, bf16[4096,768]{1,0:T(8,128)(2,1)} %fusion.17), kind=kOutput, calls=%fused_computation.75 | convolution fusion | flops 9663676416 | bytes 23592960 | tf_op jit(solution)/shard_map/dot_general | solution.py:743
  209.9 4.4 %slice.216 = f32[1536,2]{1,0:T(8,128)S(1)} slice(f32[1536,768]{1,0:T(8,128)} %fusion.25), slice={[0:1536:1], [384:512:64]} | slice | bytes 24576 | tf_op jit(solution)/shard_map/slice | solution.py:751
  221.3 9.2 %fusion.24 = f32[1536,128]{1,0:T(8,128)} fusion(bf16[4096,1536]{1,0:T(8,128)(2,1)} %get-tuple-element.90, bf16[4096,128]{1,0:T(8,128)(2,1)} %get-tuple-element.78.gate_ref), kind=kOutput, calls=%fused_computation.74 | convolution fusion | flops 1610612736 | bytes 14417920 | tf_op jit(solution)/shard_map/dot_general | solution.py:736
  230.5 7.7 %fusion.26 = f32[128,1536]{1,0:T(8,128)} fusion(bf16[4096,128]{1,0:T(8,128)(2,1)} %get-tuple-element.93, bf16[4096,1536]{1,0:T(8,128)(2,1)} %param.35), kind=kOutput, calls=%fused_computation.76 | convolution fusion | flops 1610612736 | bytes 14417920 | tf_op jit(solution)/shard_map/dot_general | solution.py:740
  242.9 18.2 %collective-permute-done.6 = f32[44,128]{1,0:T(8,128)S(1)} collective-permute-done((f32[44,128]{1,0:T(8,128)S(1)}, f32[44,128]{1,0:T(8,128)S(1)}, u32[]{:S(2)}, u32[]{:S(2)}) %collective-permute-start.6) | collective-permute-done | bytes 22560 | tf_op jit(solution)/shard_map/ppermute | solution.py:626
  262.6 7.5 %output_rows.1 = bf16[8,512,192]{2,1,0:T(8,128)(2,1)} custom-call(bf16[8,512,128]{2,1,0:T(8,128)(2,1)} %copy-done, bf16[8,128,1536]{2,1,0:T(8,128)(2,1)} %bitcast.114, bf16[512,1536]{1,0:T(8,128)(2,1)} %constant_dynamic-slice_fusion.hidden_ref), custom_call_target="tpu_custom_call" | custom-call | flops 1610612736 | bytes 8388608 | tf_op jit(solution)/shard_map/output_rows/pallas_call | solution.py:593
  270.1 3.9 copy.78
  274.0 6.0 %all-to-all-start.1 = ((bf16[8,512,192]{1,2,0:T(8,128)(2,1)}), bf16[8,512,192]{1,2,0:T(8,128)(2,1)S(1)}, u32[]{:S(2)}, u32[]{:S(2)}) async-start(bf16[8,512,192]{1,2,0:T(8,128)(2,1)} %copy.78), calls=%async_computation.1 | async-start | bytes 3145728 | tf_op jit(solution)/shard_map/all_to_all | solution.py:709
  293.0 55.3 %collective-permute-done.15 = f32[2,192,256]{2,1,0:T(8,128)S(1)} collective-permute-done((f32[2,192,256]{2,1,0:T(8,128)S(1)}, f32[2,192,256]{2,1,0:T(8,128)S(1)}, u32[]{:S(2)}, u32[]{:S(2)}) %collective-permute-start.15) | collective-permute-done | bytes 393248 | tf_op jit(solution)/shard_map/ppermute | solution.py:640
  357.2 10.4 %collective-permute-done.16 = f32[192,256]{1,0:T(8,128)} collective-permute-done((f32[192,256]{1,0:T(8,128)}, f32[192,256]{1,0:T(8,128)}, u32[]{:S(2)}, u32[]{:S(2)}) %collective-permute-start.16) | collective-permute-done | bytes 196640 | tf_op jit(solution)/shard_map/ppermute | solution.py:640
  393.0 22.0 %reduce-scatter.2.cloned.1.call-done = bf16[1,4096,192]{2,1,0:T(8,128)(2,1)} async-done(((bf16[8,4096,192]{2,1,0:T(8,128)(2,1)}), bf16[1,4096,192]{2,1,0:T(8,128)(2,1)}) %reduce-scatter.2.cloned.1.call-update) | async-done | bytes 1572880 | tf_op jit(solution)/shard_map/reduce_scatter | solution.py:725
  415.0 6.4 %fusion.2 = f32[4096,192]{1,0:T(8,128)} fusion(bf16[1,4096,192]{2,1,0:T(8,128)(2,1)} %reduce-scatter.2.cloned.1.call-done, bf16[4096,1536]{1,0:T(8,128)(2,1)} %param.35, s32[]{:T(128)S(6)} %select_n.122, f32[4096]{0:T(1024)S(1)} %copy-done.7, bf16[4096,1536]{1,0:T(8,128)(2,1)} %hidden_ref.3, f32[192]{0:T(256)S(1)} %copy-done.15, f32[4096]{0:T(1024)S(1)} %slice_reduce_fusion), kind=kLoop, calls=%fused_computation.3 | loop fusion | flops 7077888 | bytes 7897860 | tf_op jit(solution)/shard_map/add | solution.py:770
  421.4 5.3 %copy.86 = f32[4096,192]{0,1:T(8,128)} copy(f32[4096,192]{1,0:T(8,128)} %fusion.2) | data formatting | bytes 6291456
  (186 shorter events, 96.9 us)
Async XLA Ops:
  7.2 254.4 %all-gather.5.cloned.1.call-start = ((), (), s32[]{:S(2)}) async-start(), calls=%async_computation.4 | async-start | bytes 3538944 | tf_op jit(solution)/shard_map/all_gather | solution.py:680
  7.9 407.1 %reduce-scatter.2.cloned.1.call-start = ((), (), s32[]{:S(2)}) async-start(), calls=%async_computation.3 | async-start | bytes 18874368 | tf_op jit(solution)/shard_map/reduce_scatter | solution.py:725
  28.8 14.9 %collective-permute-start = (bf16[8,384]{1,0:T(8,128)(2,1)S(1)}, bf16[8,384]{1,0:T(8,128)(2,1)S(1)}, u32[]{:S(2)}, u32[]{:S(2)}) collective-permute-start(bf16[8,384]{1,0:T(8,128)(2,1)S(1)} %slice.188), channel_id=1, source_target_pairs={{0,8},{8,16},{16,24},{1,9},{9,17},{17,25},{2,10},{10,18},{18,26},{... | collective-permute-start | bytes 18440 | tf_op jit(solution)/shard_map/ppermute | solution.py:613
  82.5 4.5 %collective-permute-start.1 = (f32[2,4096]{1,0:T(2,128)}, f32[2,4096]{1,0:T(2,128)S(1)}, u32[]{:S(2)}, u32[]{:S(2)}) collective-permute-start(f32[2,4096]{1,0:T(2,128)} %get-tuple-element.75), channel_id=1, source_target_pairs={{0,1},{1,0},{2,3},{3,2},{4,5},{5,4},{6,7},{7,6},{8,9},{9,8},{10,11... | collective-permute-start | bytes 98312 | tf_op jit(solution)/shard_map/ppermute | solution.py:626
  147.2 4.6 %collective-permute-start.4 = (f32[8,384]{1,0:T(8,128)}, f32[8,384]{1,0:T(8,128)S(1)}, u32[]{:S(2)}, u32[]{:S(2)}) collective-permute-start(f32[8,384]{1,0:T(8,128)} %get-tuple-element.83), channel_id=1, source_target_pairs={{8,0},{16,8},{24,16},{9,1},{17,9},{25,17},{10,2},{18,10},{26,18},{... | collective-permute-start | bytes 36872 | tf_op jit(solution)/shard_map/ppermute | solution.py:613
  180.8 80.7 %all-to-all-start = ((bf16[8,512,128]{2,1,0:T(8,128)(2,1)}), bf16[8,512,128]{2,1,0:T(8,128)(2,1)S(1)}, u32[]{:S(2)}, u32[]{:S(2)}) async-start(bf16[8,512,128]{2,1,0:T(8,128)(2,1)} %bitcast.13), calls=%async_computation | async-start | bytes 2097152 | tf_op jit(solution)/shard_map/all_to_all | solution.py:704
  216.4 24.7 %collective-permute-start.5 = (f32[44,128]{1,0:T(8,128)S(1)}, f32[44,128]{1,0:T(8,128)S(1)}, u32[]{:S(2)}, u32[]{:S(2)}) collective-permute-start(f32[44,128]{1,0:T(8,128)S(1)} %maximum_bitcast_fusion), channel_id=1, source_target_pairs={{0,8},{8,0},{16,24},{24,16},{1,9},{9,1},{17,25},{25,17},{2,10},{10... | collective-permute-start | bytes 67592 | tf_op jit(solution)/shard_map/ppermute | solution.py:626
  218.5 24.3 %collective-permute-start.19 = (f32[2,1536]{1,0:T(2,128)S(1)}, f32[2,1536]{1,0:T(2,128)S(1)}, u32[]{:S(2)}, u32[]{:S(2)}) collective-permute-start(f32[2,1536]{1,0:T(2,128)S(1)} %bitcast.125), channel_id=1, source_target_pairs={{0,16},{8,24},{16,0},{24,8},{1,17},{9,25},{17,1},{25,9},{2,18},{10... | collective-permute-start | bytes 36872 | tf_op jit(solution)/shard_map/ppermute | solution.py:626
  218.6 66.5 %collective-permute-start.12 = (f32[1536,128]{1,0:T(8,128)}, f32[1536,128]{1,0:T(8,128)}, u32[]{:S(2)}, u32[]{:S(2)}) collective-permute-start(f32[1536,128]{1,0:T(8,128)} %slice.250), channel_id=1, source_target_pairs={{0,8},{8,0},{16,24},{24,16},{1,9},{9,1},{17,25},{25,17},{2,10},{10... | collective-permute-start | bytes 2359304 | tf_op jit(solution)/shard_map/ppermute | solution.py:626
  239.1 43.1 %collective-permute-start.14 = (f32[2,2,192,256]{3,2,1,0:T(8,128)}, f32[2,2,192,256]{3,2,1,0:T(8,128)}, u32[]{:S(2)}, u32[]{:S(2)}) collective-permute-start(f32[2,2,192,256]{3,2,1,0:T(8,128)} %dynamic-slice_bitcast_fusion), channel_id=1, source_target_pairs={{0,1},{1,0},{2,3},{3,2},{4,5},{5,4},{6,7},{7,6},{8,9},{9,8},{10,11... | collective-permute-start | bytes 2359304 | tf_op jit(solution)/shard_map/ppermute | solution.py:640
  240.4 47.2 %collective-permute-start.10 = (f32[1536,128]{1,0:T(8,128)}, f32[1536,128]{1,0:T(8,128)}, u32[]{:S(2)}, u32[]{:S(2)}) collective-permute-start(f32[1536,128]{1,0:T(8,128)} %fusion.24), channel_id=1, source_target_pairs={{0,8},{8,0},{16,24},{24,16},{1,9},{9,1},{17,25},{25,17},{2,10},{10... | collective-permute-start | bytes 2359304 | tf_op jit(solution)/shard_map/ppermute | solution.py:626
  241.2 48.4 %collective-permute-start.21 = (f32[128,1536]{1,0:T(8,128)}, f32[128,1536]{1,0:T(8,128)}, u32[]{:S(2)}, u32[]{:S(2)}) collective-permute-start(f32[128,1536]{1,0:T(8,128)} %fusion.26), channel_id=1, source_target_pairs={{0,16},{8,24},{16,0},{24,8},{1,17},{9,25},{17,1},{25,9},{2,18},{10... | collective-permute-start | bytes 2359304 | tf_op jit(solution)/shard_map/ppermute | solution.py:626
  242.8 18.3 %collective-permute-start.6 = (f32[44,128]{1,0:T(8,128)S(1)}, f32[44,128]{1,0:T(8,128)S(1)}, u32[]{:S(2)}, u32[]{:S(2)}) collective-permute-start(f32[44,128]{1,0:T(8,128)S(1)} %fusion.19), channel_id=1, source_target_pairs={{0,16},{8,24},{16,0},{24,8},{1,17},{9,25},{17,1},{25,9},{2,18},{10... | collective-permute-start | bytes 67592 | tf_op jit(solution)/shard_map/ppermute | solution.py:626
  261.1 18.9 %collective-permute-start.20 = (f32[2,1536]{1,0:T(2,128)S(1)}, f32[2,1536]{1,0:T(2,128)S(1)}, u32[]{:S(2)}, u32[]{:S(2)}) collective-permute-start(f32[2,1536]{1,0:T(2,128)S(1)} %bitcast_add_fusion.3), channel_id=1, source_target_pairs={{0,8},{8,0},{16,24},{24,16},{1,9},{9,1},{17,25},{25,17},{2,10},{10... | collective-permute-start | bytes 36872 | tf_op jit(solution)/shard_map/ppermute | solution.py:626
  274.0 117.7 %all-to-all-start.1 = ((bf16[8,512,192]{1,2,0:T(8,128)(2,1)}), bf16[8,512,192]{1,2,0:T(8,128)(2,1)S(1)}, u32[]{:S(2)}, u32[]{:S(2)}) async-start(bf16[8,512,192]{1,2,0:T(8,128)(2,1)} %copy.78), calls=%async_computation.1 | async-start | bytes 3145728 | tf_op jit(solution)/shard_map/all_to_all | solution.py:709
  282.2 72.5 %collective-permute-start.8 = (f32[76,128]{1,0:T(8,128)}, f32[76,128]{1,0:T(8,128)}, u32[]{:S(2)}, u32[]{:S(2)}) collective-permute-start(f32[76,128]{1,0:T(8,128)} %fusion.20), channel_id=1, source_target_pairs={{0,2},{1,3},{2,0},{3,1},{4,6},{5,7},{6,4},{7,5},{8,10},{9,11},{10,... | collective-permute-start | bytes 116744 | tf_op jit(solution)/shard_map/ppermute | solution.py:626
  283.5 64.8 %collective-permute-start.15 = (f32[2,192,256]{2,1,0:T(8,128)S(1)}, f32[2,192,256]{2,1,0:T(8,128)S(1)}, u32[]{:S(2)}, u32[]{:S(2)}) collective-permute-start(f32[2,192,256]{2,1,0:T(8,128)S(1)} %dynamic-slice_bitcast_fusion.1), channel_id=1, source_target_pairs={{0,2},{1,3},{2,0},{3,1},{4,6},{5,7},{6,4},{7,5},{8,10},{9,11},{10,... | collective-permute-start | bytes 1179656 | tf_op jit(solution)/shard_map/ppermute | solution.py:640
  286.5 97.9 %collective-permute-start.13 = (f32[1536,128]{1,0:T(8,128)S(1)}, f32[1536,128]{1,0:T(8,128)}, u32[]{:S(2)}, u32[]{:S(2)}) collective-permute-start(f32[1536,128]{1,0:T(8,128)S(1)} %slice_add_fusion.5), channel_id=1, source_target_pairs={{0,16},{8,24},{16,0},{24,8},{1,17},{9,25},{17,1},{25,9},{2,18},{10... | collective-permute-start | bytes 2359304 | tf_op jit(solution)/shard_map/ppermute | solution.py:626
  289.1 97.4 %collective-permute-start.11 = (f32[1536,128]{1,0:T(8,128)S(1)}, f32[1536,128]{1,0:T(8,128)}, u32[]{:S(2)}, u32[]{:S(2)}) collective-permute-start(f32[1536,128]{1,0:T(8,128)S(1)} %add.190), channel_id=1, source_target_pairs={{0,16},{8,24},{16,0},{24,8},{1,17},{9,25},{17,1},{25,9},{2,18},{10... | collective-permute-start | bytes 2359304 | tf_op jit(solution)/shard_map/ppermute | solution.py:626
  291.9 96.7 %collective-permute-start.22 = (f32[128,1536]{1,0:T(8,128)}, f32[128,1536]{1,0:T(8,128)}, u32[]{:S(2)}, u32[]{:S(2)}) collective-permute-start(f32[128,1536]{1,0:T(8,128)} %add.215), channel_id=1, source_target_pairs={{0,8},{8,0},{16,24},{24,16},{1,9},{9,1},{17,25},{25,17},{2,10},{10... | collective-permute-start | bytes 2359304 | tf_op jit(solution)/shard_map/ppermute | solution.py:626
  349.0 18.5 %collective-permute-start.16 = (f32[192,256]{1,0:T(8,128)}, f32[192,256]{1,0:T(8,128)}, u32[]{:S(2)}, u32[]{:S(2)}) collective-permute-start(f32[192,256]{1,0:T(8,128)} %dynamic-slice_bitcast_fusion.2), channel_id=1, source_target_pairs={{0,4},{1,5},{2,6},{3,7},{4,0},{5,1},{6,2},{7,3},{8,12},{9,13},{10,... | collective-permute-start | bytes 589832 | tf_op jit(solution)/shard_map/ppermute | solution.py:640
  356.1 19.2 %collective-permute-start.9 = (f32[76,128]{1,0:T(8,128)}, f32[76,128]{1,0:T(8,128)}, u32[]{:S(2)}, u32[]{:S(2)}) collective-permute-start(f32[76,128]{1,0:T(8,128)} %add.185), channel_id=1, source_target_pairs={{0,4},{1,5},{2,6},{3,7},{4,0},{5,1},{6,2},{7,3},{8,12},{9,13},{10,... | collective-permute-start | bytes 116744 | tf_op jit(solution)/shard_map/ppermute | solution.py:626
  369.2 6.9 %collective-permute-start.17 = (f32[192,256]{1,0:T(8,128)}, f32[192,256]{1,0:T(8,128)S(1)}, u32[]{:S(2)}, u32[]{:S(2)}) collective-permute-start(f32[192,256]{1,0:T(8,128)} %bitcast_add_fusion.2), channel_id=1, source_target_pairs={{0,16},{8,24},{16,0},{24,8},{1,17},{9,25},{17,1},{25,9},{2,18},{10... | collective-permute-start | bytes 589832 | tf_op jit(solution)/shard_map/ppermute | solution.py:626
  377.1 13.8 %collective-permute-start.18 = (f32[192,256]{1,0:T(8,128)S(1)}, f32[192,256]{1,0:T(8,128)S(1)}, u32[]{:S(2)}, u32[]{:S(2)}) collective-permute-start(f32[192,256]{1,0:T(8,128)S(1)} %add.211), channel_id=1, source_target_pairs={{0,8},{8,0},{16,24},{24,16},{1,9},{9,1},{17,25},{25,17},{2,10},{10... | collective-permute-start | bytes 589832 | tf_op jit(solution)/shard_map/ppermute | solution.py:626
  (28 other events, 301.0 us)
Sparse Core Ops, SparseCore 0:
  9.6 38.9 all-gather.4
  176.1 238.8 reduce-scatter.1

commit v2 on v1

v2 whole, which is shorter than its diff:
```python
from functools import partial

import jax
import jax.numpy as jnp
from jax import lax
from jax.experimental import pallas as pl
from jax.experimental.pallas import tpu as pltpu
from jax.experimental.layout import Layout, with_layout_constraint
from jax.sharding import PartitionSpec as P


SPAN = 256
epsilon = 1e-05
f32 = jnp.float32
bf16 = jnp.bfloat16


def mm(a, b):
    return jnp.dot(a, b, preferred_element_type=f32)


def mm_nt(a, b):
    return lax.dot_general(a, b, (((1,), (1,)), ((), ())), preferred_element_type=f32)


def mm_tn(a, b):
    return lax.dot_general(a, b, (((0,), (0,)), ((), ())), preferred_element_type=f32)


def halves(x):
    high = x.astype(bf16)
    return jnp.concatenate([high, (x - high.astype(f32)).astype(bf16)], axis=1)


def two(x):
    high = x.astype(bf16)
    return high, (x - high.astype(f32)).astype(bf16)


def left_terms(x, axis):
    high, low = two(x)
    return jnp.concatenate([high, high, low], axis=axis)


def right_terms(x):
    high, low = two(x)
    return jnp.concatenate([high, low, high], axis=0)


def wide_terms(x):
    high, low = two(x)
    return jnp.concatenate([high, low, high], axis=1)


def folded(x):
    width = x.shape[1] // 2
    return x[:, :width] + x[:, width:]


def logistic(x):
    return 0.5 + 0.5 * jnp.tanh(0.5 * x)


def softplus(x):
    return jnp.maximum(x, 0.0) + jnp.log1p(jnp.exp(-jnp.abs(x)))


def iota(shape, axis):
    return lax.broadcasted_iota(jnp.int32, shape, axis)


def params(mebibytes):
    return pltpu.CompilerParams(
        dimension_semantics=("arbitrary",), vmem_limit_bytes=mebibytes << 20
    )


def spec(shape, index):
    return pl.BlockSpec(shape, index)


def whole_block(array):
    rank = array.ndim
    return pl.BlockSpec(array.shape, lambda *i: (0,) * rank)


def project_kernel(
    hidden_ref, gain_ref, gate_ref, value_ref, state_ref, step_ref,
    projected_ref, gate_out, stream_out, step_out, scale_out, weights,
):
    @pl.when(pl.program_id(0) == 0)
    def _():
        weights[:, 0:128] = gate_ref[...]
        weights[:, 128:256] = value_ref[...]
        weights[:, 256:512] = state_ref[...]
        weights[:, 512:640] = step_ref[...]

    hidden = hidden_ref[...].astype(f32)
    scale = lax.rsqrt(jnp.mean(hidden * hidden, axis=1, keepdims=True) + epsilon)
    projected = (hidden * scale * gain_ref[...]).astype(bf16)
    projected_ref[...] = projected
    scale_out[...] = jnp.broadcast_to(scale, scale_out.shape)
    result = mm(projected, weights[...])
    gate_out[...] = result[:, 0:128]
    stream_out[...] = result[:, 128:512].astype(bf16)
    step_out[...] = result[:, 512:640]


def project(hidden_in, norm_gain, gate_proj, value_proj, state_proj, step_wide):
    rows, width = hidden_in.shape
    span = 512
    row = lambda i: (i, 0)
    gain = norm_gain[None, :]
    return pl.pallas_call(
        project_kernel,
        grid=(rows // span,),
        in_specs=[
            spec((span, width), row), whole_block(gain), whole_block(gate_proj),
            whole_block(value_proj), whole_block(state_proj), whole_block(step_wide),
        ],
        out_specs=[
            spec((span, width), row), spec((span, 128), row), spec((span, 384), row),
            spec((span, 128), row), spec((span, 128), row),
        ],
        out_shape=[
            jax.ShapeDtypeStruct((rows, width), bf16),
            jax.ShapeDtypeStruct((rows, 128), f32),
            jax.ShapeDtypeStruct((rows, 384), bf16),
            jax.ShapeDtypeStruct((rows, 128), f32),
            jax.ShapeDtypeStruct((rows, 128), f32),
        ],
        scratch_shapes=[pltpu.VMEM((width, 640), bf16)],
        compiler_params=params(56),
        cost_estimate=pl.CostEstimate(
            flops=2 * rows * width * 640, bytes_accessed=rows * width * 4, transcendentals=0
        ),
        name="project",
    )(hidden_in, gain, gate_proj, value_proj, state_proj, step_wide)


def convolved(ext, taps, bias):
    span = SPAN
    total = bias + taps[0:1] * ext[5 : 5 + span]
    for tap in range(1, 4):
        total = total + taps[tap : tap + 1] * ext[5 + tap : 5 + tap + span]
    return total


def running_sums(log_decay):
    span = log_decay.shape[0]
    lower = (iota((span, span), 0) >= iota((span, span), 1)).astype(bf16)
    return folded(mm(lower, halves(log_decay)))


def decay_matrix(running, running_rows, head):
    span = running.shape[0]
    at = 64 * head
    spread = running[:, at : at + 1] - running_rows[at : at + 1, :]
    return jnp.exp(jnp.where(iota((span, span), 0) >= iota((span, span), 1), spread, -jnp.inf))


def forward_kernel(
    stream_ref, edge_ref, step_ref, taps_ref, bias_ref, step_bias_ref, rate_ref, skip_ref,
    mixed_out, active_out, slope_out, reach_out, steps_out, states_out,
    ext, state, offset,
):
    span = SPAN
    first = pl.program_id(0) == 0

    @pl.when(first)
    def _():
        ext[0:8] = edge_ref[...].astype(f32)
        state[...] = jnp.zeros_like(state)
        offset[...] = jnp.zeros_like(offset)

    ext[8 : 8 + span] = stream_ref[...].astype(f32)
    conv = convolved(ext, taps_ref[...], bias_ref[...])
    ext[0:8] = ext[span : span + 8]
    chance = logistic(conv)
    active = conv * chance
    active_out[...] = active
    slope_out[...] = chance * (1.0 + conv * (1.0 - chance))
    values = active[:, 0:128]
    keys = active[:, 128:256]
    queries = active[:, 256:384]
    step = step_ref[...] + step_bias_ref[...]
    widths = softplus(step)
    running = running_sums(-rate_ref[...] * widths)
    steps_out[:, 0:128] = widths
    steps_out[:, 128:256] = running
    steps_out[:, 256:384] = logistic(step)
    running_rows = running.T
    last = running[span - 1 : span, :]
    fed = widths * values
    fed16 = fed.astype(bf16)
    query_terms = left_terms(queries, 1)
    scores = mm_nt(queries.astype(bf16), keys.astype(bf16))
    low = iota((span, 128), 1) < 64
    heads = [
        mm((scores * decay_matrix(running, running_rows, head)).astype(bf16), fed16)
        for head in range(2)
    ]
    before = state[...]
    mixed = jnp.where(low, heads[0], heads[1])
    mixed = mixed + jnp.exp(running) * mm_nt(query_terms, wide_terms(before))
    mixed_out[...] = mixed + skip_ref[...] * values
    reach_out[...] = running + offset[0:1]
    offset[...] = offset[...] + last
    tails = left_terms(jnp.exp(last - running) * fed, 0)
    after = jnp.exp(running_rows[:, span - 1 : span]) * before + mm_tn(tails, right_terms(keys))
    state[...] = after
    states_out[0] = after


def scan_forward(stream, edge, step, taps, bias, step_bias, rate, skip):
    rows = stream.shape[0]
    span = SPAN
    count = rows // span
    row = lambda i: (i, 0)
    narrow, full = spec((span, 128), row), spec((span, 384), row)
    return pl.pallas_call(
        forward_kernel,
        grid=(count,),
        in_specs=[
            full, whole_block(edge), narrow, whole_block(taps), whole_block(bias),
            whole_block(step_bias), whole_block(rate), whole_block(skip),
        ],
        out_specs=[
            narrow, full, full, narrow, full, spec((1, 128, 128), lambda i: (i, 0, 0)),
        ],
        out_shape=[
            jax.ShapeDtypeStruct((rows, 128), f32),
            jax.ShapeDtypeStruct((rows, 384), f32),
            jax.ShapeDtypeStruct((rows, 384), f32),
            jax.ShapeDtypeStruct((rows, 128), f32),
            jax.ShapeDtypeStruct((rows, 384), f32),
            jax.ShapeDtypeStruct((count, 128, 128), f32),
        ],
        scratch_shapes=[
            pltpu.VMEM((span + 8, 384), f32), pltpu.VMEM((128, 128), f32), pltpu.VMEM((8, 128), f32),
        ],
        compiler_params=params(56),
        cost_estimate=pl.CostEstimate(
            flops=count * 2 * span * span * 900, bytes_accessed=rows * 128 * 50, transcendentals=0
        ),
        name="scan_forward",
    )(stream, edge, step, taps, bias, step_bias, rate, skip)


def join_kernel(
    mixed_ref, query_ref, reach_ref, gate_ref, grad_ref, carried_ref, gain_ref, mixed_out, sums_out
):
    inner = mm_nt(left_terms(query_ref[...], 1), wide_terms(carried_ref[...]))
    mixed = mixed_ref[...] + jnp.exp(reach_ref[...]) * inner
    mixed_out[...] = mixed
    gate = gate_ref[...]
    gated = mixed * (gate * logistic(gate))
    at = 2 * pl.program_id(0)
    sums_out[pl.ds(at, 1), :] = jnp.sum((gated * gated).T, axis=0, keepdims=True)
    product = grad_ref[...] * gain_ref[...] * gated
    sums_out[pl.ds(at + 1, 1), :] = jnp.sum(product.T, axis=0, keepdims=True)


def join(mixed, active, reach, gate, grad, carried, gain):
    rows = mixed.shape[0]
    block = 1024
    sums = (2 * rows // block, block)
    blocks = spec((block, 128), lambda i: (i, 0))
    return pl.pallas_call(
        join_kernel,
        grid=(rows // block,),
        in_specs=[
            blocks, spec((block, 128), lambda i: (i, 2)), blocks, blocks, blocks,
            whole_block(carried), whole_block(gain),
        ],
        out_specs=[blocks, spec(sums, lambda i: (0, 0))],
        out_shape=[jax.ShapeDtypeStruct((rows, 128), f32), jax.ShapeDtypeStruct(sums, f32)],
        compiler_params=params(56),
        cost_estimate=pl.CostEstimate(
            flops=2 * rows * 128 * 128, bytes_accessed=rows * 128 * 22, transcendentals=0
        ),
        name="join",
    )(mixed, active, reach, gate, grad, carried, gain)


def gate_kernel(
    inner_width,
    mixed_ref, query_ref, reach_ref, gate_ref, grad_ref, sums_ref, gain_ref,
    rows_out, gate_out, mixed_grad_out, gain_out, incoming_out,
):
    @pl.when(pl.program_id(0) == 0)
    def _():
        gain_out[...] = jnp.zeros_like(gain_out)
        incoming_out[...] = jnp.zeros_like(incoming_out)

    block = mixed_ref.shape[0]
    at = 2 * pl.program_id(0)
    square = jnp.broadcast_to(sums_ref[pl.ds(at, 1), :], (128, block)).T
    product = jnp.broadcast_to(sums_ref[pl.ds(at + 1, 1), :], (128, block)).T
    scale = lax.rsqrt(square / inner_width + epsilon)
    gate = gate_ref[...]
    chance = logistic(gate)
    act = gate * chance
    mixed = mixed_ref[...]
    hat = mixed * act * scale
    rows_out[...] = (hat * gain_ref[...]).astype(bf16)
    grad = grad_ref[...]
    gain_out[...] += jnp.sum(grad * hat, axis=0, keepdims=True)
    pre = scale * (grad * gain_ref[...] - hat * (product * scale / inner_width))
    mixed_grad = pre * act
    mixed_grad_out[...] = mixed_grad
    gate_out[...] = (pre * mixed * (chance * (1.0 + gate * (1.0 - chance)))).astype(bf16)
    incoming_out[...] += mm_tn(
        left_terms(jnp.exp(reach_ref[...]) * mixed_grad, 0), right_terms(query_ref[...])
    )


def gate_step(mixed, active, reach, gate, grad, sums, gain, inner_width):
    rows = mixed.shape[0]
    block = sums.shape[1]
    blocks = spec((block, 128), lambda i: (i, 0))
    return pl.pallas_call(
        partial(gate_kernel, inner_width),
        grid=(rows // block,),
        in_specs=[
            blocks, spec((block, 128), lambda i: (i, 2)), blocks, blocks, blocks, whole_block(sums),
            whole_block(gain),
        ],
        out_specs=[
            blocks, blocks, blocks, spec((1, 128), lambda i: (0, 0)),
            spec((128, 128), lambda i: (0, 0)),
        ],
        out_shape=[
            jax.ShapeDtypeStruct((rows, 128), bf16),
            jax.ShapeDtypeStruct((rows, 128), bf16),
            jax.ShapeDtypeStruct((rows, 128), f32),
            jax.ShapeDtypeStruct((1, 128), f32),
            jax.ShapeDtypeStruct((128, 128), f32),
        ],
        compiler_params=params(56),
        cost_estimate=pl.CostEstimate(
            flops=2 * rows * 128 * 128, bytes_accessed=rows * 128 * 26, transcendentals=0
        ),
        name="gate_step",
    )(mixed, active, reach, gate, grad, sums, gain)


def head_sums(x):
    same = (iota((128, 128), 0) < 64) == (iota((128, 128), 1) < 64)
    ones = same.astype(bf16)
    high = x.astype(bf16)
    return mm(high, ones) + mm((x - high.astype(f32)).astype(bf16), ones)


def backward_kernel(
    first_chunk,
    stream_ref, before_ref, edge_ref, active_ref, slope_ref, steps_ref, taps_ref, rate_ref, skip_ref,
    mixed_ref, grad_ref, reach_ref, start_ref, end_ref, carried_ref, arriving_ref, next_ref,
    stream_grad_out, tail_out, head_out, sums_out, leaving_out,
    ext, grads, state_grad,
):
    span = SPAN
    chunk = first_chunk - pl.program_id(0)

    @pl.when(pl.program_id(0) == 0)
    def _():
        state_grad[...] = arriving_ref[...]
        grads[span : span + 8] = next_ref[...]
        sums_out[...] = jnp.zeros_like(sums_out)

    @pl.when(chunk == 0)
    def _():
        ext[0:8] = edge_ref[...].astype(f32)

    @pl.when(chunk > 0)
    def _():
        ext[0:8] = before_ref[8:16].astype(f32)

    ext[8 : 8 + span] = stream_ref[...].astype(f32)
    taps = taps_ref[...]
    values = active_ref[:, 0:128]
    keys = active_ref[:, 128:256]
    queries = active_ref[:, 256:384]
    keys16 = keys.astype(bf16)
    rate = rate_ref[...]
    widths = steps_ref[:, 0:128]
    running = steps_ref[:, 128:256]
    running_rows = running.T
    last = running[span - 1 : span, :]
    fed = widths * values
    fed16 = fed.astype(bf16)
    grad = grad_ref[...]
    grad16 = grad.astype(bf16)
    scores = mm_nt(queries.astype(bf16), keys16)
    low = iota((span, 128), 1) < 64
    grad_turned = pltpu.roll(grad, 64, 1)
    fed_turned = pltpu.roll(fed, 64, 1)
    score_grad = None
    fed_grads = []
    for head in range(2):
        decay = decay_matrix(running, running_rows, head)
        mine = low == (head == 0)
        grad_high, grad_low = two(jnp.where(mine, grad, grad_turned))
        left = [jnp.where(low, grad_high, grad_low), jnp.where(low, grad_high, 0)]
        right = two(jnp.where(mine, fed, fed_turned))
        part = mm_nt(jnp.concatenate(left, axis=1), jnp.concatenate(right, axis=1)) * decay
        score_grad = part if score_grad is None else score_grad + part
        fed_grads.append(mm_tn((scores * decay).astype(bf16), grad16))

    offset = (reach_ref[span - 8 : span, :] - running[span - 8 : span, :]).T[:, 7:8]
    carried = jnp.exp(offset) * carried_ref[...]
    before = jnp.where(chunk > 0, start_ref[0], 0.0) + carried
    last_rows = jnp.exp(running_rows[:, span - 1 : span])
    after = end_ref[0] + last_rows * carried
    after_grad = state_grad[...]
    tail = jnp.exp(last - running)
    reached = jnp.exp(running) * grad
    query_terms = right_terms(queries)
    fed_grad = jnp.where(low, fed_grads[0], fed_grads[1])
    fed_grad = fed_grad + tail * mm_nt(keys16, after_grad.astype(bf16))
    score_high, score_low = two(score_grad)
    query_grad = mm(
        jnp.concatenate([score_high, score_high, score_low], axis=1), right_terms(keys)
    ) + mm(left_terms(reached, 1), right_terms(before))
    key_grad = mm_tn(
        jnp.concatenate([score_high, score_high, score_low], axis=0), query_terms
    ) + mm(left_terms(tail * fed, 1), right_terms(after_grad))
    leaving = last_rows * after_grad + mm_tn(left_terms(reached, 0), query_terms)
    state_grad[...] = leaving
    leaving_out[...] = leaving
    value_grad = widths * fed_grad + skip_ref[...] * grad

    mixed = mixed_ref[...] - skip_ref[...] * values
    balance = head_sums(grad16.astype(f32) * mixed - fed16.astype(f32) * fed_grad)
    upper = (iota((span, span), 0) <= iota((span, span), 1)).astype(bf16)
    boundary = head_sums(
        jnp.broadcast_to(jnp.sum((after_grad * after).T, axis=0, keepdims=True), (8, 128))
    )
    decay_grad = folded(mm(upper, halves(balance))) + boundary[0:1]
    width_grad = head_sums(values * fed_grad) - rate * decay_grad
    step_grad = width_grad * steps_ref[:, 256:384]
    sums_out[0:1, 384:512] += jnp.sum(step_grad, axis=0, keepdims=True)
    sums_out[1:2, 384:512] += jnp.sum(-widths * decay_grad, axis=0, keepdims=True)
    sums_out[2:3, 384:512] += jnp.sum(grad * values, axis=0, keepdims=True)

    conv_grad = jnp.concatenate([value_grad, key_grad, query_grad], axis=1) * slope_ref[...]
    grads[0:span] = conv_grad
    for tap in range(4):
        sums_out[tap : tap + 1, 0:384] += jnp.sum(
            conv_grad * ext[5 + tap : 5 + tap + span], axis=0, keepdims=True
        )
    sums_out[4:5, 0:384] += jnp.sum(conv_grad, axis=0, keepdims=True)
    stream_grad = taps[3:4] * conv_grad
    for tap in range(3):
        stream_grad = stream_grad + taps[tap : tap + 1] * grads[3 - tap : 3 - tap + span]
    high = stream_grad.astype(bf16)
    stream_grad_out[:, 0:384] = high
    stream_grad_out[:, 384:512] = step_grad.astype(bf16)
    stream_grad_out[:, 512:768] = (stream_grad - high.astype(f32))[:, 128:384].astype(bf16)

    @pl.when(pl.program_id(0) == 0)
    def _():
        tail_out[...] = stream_grad[span - 8 :]

    head_out[...] = conv_grad[0:8]
    grads[span : span + 8] = conv_grad[0:8]


def scan_backward(
    late, stream, edge, active, slope, steps, taps, rate, skip, mixed, grad, reach, states, carried,
    arriving, next_rows,
):
    rows = stream.shape[0]
    span = SPAN
    count = rows // span // 2
    first = 2 * count - 1 if late else count - 1
    row = lambda i: (first - i, 0)
    fixed = lambda i: (0, 0)
    narrow, full = spec((span, 128), row), spec((span, 384), row)
    return pl.pallas_call(
        partial(backward_kernel, first),
        grid=(count,),
        in_specs=[
            full, spec((16, 384), lambda i: (jnp.maximum((first - i) * (span // 16) - 1, 0), 0)),
            whole_block(edge), full, full, full, whole_block(taps), whole_block(rate),
            whole_block(skip), narrow, narrow, narrow,
            spec((1, 128, 128), lambda i: (jnp.maximum(first - 1 - i, 0), 0, 0)),
            spec((1, 128, 128), lambda i: (first - i, 0, 0)),
            whole_block(carried), whole_block(arriving), whole_block(next_rows),
        ],
        out_specs=[
            spec((span, 768), lambda i: (count - 1 - i, 0)), spec((8, 384), fixed),
            spec((8, 384), fixed), spec((8, 512), fixed), spec((128, 128), fixed),
        ],
        out_shape=[
            jax.ShapeDtypeStruct((rows // 2, 768), bf16),
            jax.ShapeDtypeStruct((8, 384), f32),
            jax.ShapeDtypeStruct((8, 384), f32),
            jax.ShapeDtypeStruct((8, 512), f32),
            jax.ShapeDtypeStruct((128, 128), f32),
        ],
        scratch_shapes=[
            pltpu.VMEM((span + 8, 384), f32), pltpu.VMEM((span + 8, 384), f32),
            pltpu.VMEM((128, 128), f32),
        ],
        compiler_params=params(56),
        cost_estimate=pl.CostEstimate(
            flops=count * 2 * span * span * 1500, bytes_accessed=rows * 128 * 30, transcendentals=0
        ),
        name="scan_backward",
    )(
        stream, stream, edge, active, slope, steps, taps, rate, skip, mixed, grad, reach, states,
        states, carried, arriving, next_rows,
    )


def group_of(rows, index):
    half = rows // SPAN // 2
    if index == 0:
        return half // 2 - 1, lambda place: half + place
    return half // 2 + 1, lambda place: jnp.where(place < half, place, place + half - 2)


def parts_kernel(
    block_of, count, last_block, early_blocks,
    half_ref, gate_ref, early_ref, late_ref, weights_ref, hidden_ref, scale_ref, gain_ref, tail_ref,
    next_ref, taps_ref,
    parts_out, dots_out, sums_out,
    left, edge,
):
    at_block = block_of(half_ref[0] * count + pl.program_id(0))

    @pl.when(pl.program_id(0) == 0)
    def _():
        sums_out[...] = jnp.zeros_like(sums_out)

    block = left.shape[0]
    left[:, 0:128] = gate_ref[...]

    @pl.when(at_block < early_blocks)
    def _():
        left[:, 128:640] = early_ref[...]

    @pl.when(at_block >= early_blocks)
    def _():
        left[:, 128:640] = late_ref[...]

    @pl.when(at_block == last_block)
    def _():
        edge[0:8] = jnp.zeros_like(edge[0:8])
        edge[8:16] = next_ref[...]
        fixed = tail_ref[...]
        for tap in range(3):
            fixed = fixed + taps_ref[tap : tap + 1] * edge[3 - tap : 11 - tap]
        left[block - 8 :, 128:512] = fixed.astype(bf16)

    chips, _, share = parts_out.shape
    total = mm(left[...], weights_ref[...]).astype(bf16)
    scale = scale_ref[...]
    summed = None
    for at in range(0, total.shape[1], 128):
        lanes = slice(at, at + 128)
        product = total[:, lanes].astype(f32) * (hidden_ref[:, lanes].astype(f32) * scale)
        sums_out[0:1, lanes] += jnp.sum(product, axis=0, keepdims=True)
        product = product * gain_ref[:, lanes]
        summed = product if summed is None else summed + product
    dots_out[...] = jnp.sum(summed.T, axis=0, keepdims=True)
    for chip in range(chips):
        parts_out[chip] = total[:, chip * share : (chip + 1) * share]


def input_parts(
    index, half, gate16, early16, late16, weights, hidden_in, scale, gain, tail, next_head, taps, chips
):
    rows, width = hidden_in.shape
    block = SPAN
    count, block_of = group_of(rows, index)
    blocks = rows // block
    at = lambda i, half: block_of(half[0] * count + i)
    row = lambda i, half: (at(i, half), 0)
    share = width // chips
    return pl.pallas_call(
        partial(parts_kernel, block_of, count, blocks - 1, blocks // 2),
        grid_spec=pltpu.PrefetchScalarGridSpec(
            num_scalar_prefetch=1,
            grid=(count,),
            in_specs=[
                spec((block, 128), row),
                spec((block, 512), lambda i, half: (jnp.minimum(at(i, half), blocks // 2 - 1), 0)),
                spec((block, 512), lambda i, half: (jnp.maximum(at(i, half) - blocks // 2, 0), 0)),
                whole_block(weights), spec((block, width), row), spec((block, 128), row),
                whole_block(gain), whole_block(tail), whole_block(next_head), whole_block(taps),
            ],
            out_specs=[
                spec((chips, block, share), lambda i, half: (0, i, 0)),
                spec((1, block), lambda i, half: (0, i)),
                spec((1, width), lambda i, half: (0, 0)),
            ],
            scratch_shapes=[pltpu.VMEM((block, 640), bf16), pltpu.VMEM((16, 384), f32)],
        ),
        out_shape=[
            jax.ShapeDtypeStruct((chips, count * block, share), bf16),
            jax.ShapeDtypeStruct((1, count * block), f32),
            jax.ShapeDtypeStruct((1, width), f32),
        ],
        compiler_params=params(56),
        cost_estimate=pl.CostEstimate(
            flops=2 * count * block * width * 640, bytes_accessed=count * block * width * 5,
            transcendentals=0,
        ),
        name="input_parts",
    )(
        half.astype(jnp.int32)[None], gate16, early16, late16, weights, hidden_in, scale, gain, tail,
        next_head, taps,
    )


def output_kernel(at_ref, rows_ref, weights_ref, hidden_ref, parts_out):
    chips, _, _, share = parts_out.shape
    summed = None
    for group in range(rows_ref.shape[0]):
        term = mm(rows_ref[group], weights_ref[group]).astype(bf16).astype(f32)
        summed = term if summed is None else summed + term
    total = (hidden_ref[...].astype(f32) + summed).astype(bf16)
    for chip in range(chips):
        parts_out[chip, 0] = total[:, chip * share : (chip + 1) * share]


def output_rows(rows, weights, hidden, at, chips):
    groups, tokens, inner = rows.shape
    width = hidden.shape[1]
    block = tokens // 2
    share = width // chips
    return pl.pallas_call(
        output_kernel,
        grid_spec=pltpu.PrefetchScalarGridSpec(
            num_scalar_prefetch=1,
            grid=(2,),
            in_specs=[
                spec((groups, block, inner), lambda i, at: (0, i, 0)), whole_block(weights),
                spec((block, width), lambda i, at: (2 * at[0] + i, 0)),
            ],
            out_specs=spec((chips, 1, block, share), lambda i, at: (0, i, 0, 0)),
        ),
        out_shape=jax.ShapeDtypeStruct((chips, 2, block, share), bf16),
        compiler_params=params(56),
        cost_estimate=pl.CostEstimate(
            flops=2 * tokens * groups * inner * width, bytes_accessed=8 << 20, transcendentals=0
        ),
        name="output_rows",
    )(at, rows, weights, hidden)


def row_major(x):
    return with_layout_constraint(x, Layout(major_to_minor=(0, 1)))


def passed_along(block, axis, distance):
    devices = range(lax.axis_size(axis))
    route = [(i - distance, i) for i in devices if i - distance in devices]
    return lax.ppermute(block, axis, route)


def bits_of(axis):
    count = lax.axis_size(axis)
    assert count & (count - 1) == 0
    return [1 << n for n in range(count.bit_length() - 1)]


def summed_over(value, axis, turned=False):
    count = lax.axis_size(axis)
    bits = bits_of(axis)
    for bit in reversed(bits) if turned else bits:
        value = value + lax.ppermute(value, axis, [(i, i ^ bit) for i in range(count)])
    return value


def spread_sums(pair, axis):
    chips = pair.shape[0]
    mine = lax.axis_index(axis)
    spread = jnp.stack([pair, jnp.zeros_like(pair)], axis=1)
    spread = jnp.where(mine % 2 == 0, spread, spread[:, ::-1])
    spread = spread.reshape(2 * chips, *pair.shape[1:])
    return lax.psum_scatter(spread, axis, scatter_dimension=0, tiled=False).astype(f32)


def line_kernel(at_ref, up_own, up_got, down_own, down_got, *refs):
    up_out, down_out = refs[-2:]
    up = up_own[0].astype(f32) + up_got[0].astype(f32)
    down = down_own[0].astype(f32) + down_got[0].astype(f32)
    if len(refs) == 4:
        up, down = up + refs[0][...].astype(f32), down + refs[1][...].astype(f32)
    up_out[...] = up.astype(bf16)
    down_out[...] = down.astype(bf16)


def line_step(up_at, down_at, own, got, arrived):
    chips, rows, width = own.shape
    block = rows // 2
    at = jnp.stack([up_at, down_at]).astype(jnp.int32)
    at = jnp.clip(at, 0, chips - 1)
    blocks = [spec((1, block, width), lambda i, at, k=k: (at[k], i, 0)) for k in (0, 0, 1, 1)]
    plain = spec((block, width), lambda i, at: (i, 0))
    return pl.pallas_call(
        line_kernel,
        grid_spec=pltpu.PrefetchScalarGridSpec(
            num_scalar_prefetch=1,
            grid=(rows // block,),
            in_specs=blocks + [plain] * len(arrived),
            out_specs=[plain, plain],
        ),
        out_shape=[jax.ShapeDtypeStruct((rows, width), bf16)] * 2,
        compiler_params=params(56),
        cost_estimate=pl.CostEstimate(
            flops=rows * width * 4, bytes_accessed=rows * width * 16, transcendentals=0
        ),
        name="line_step",
    )(at, own, got, own, got, *arrived)


def line_sent(step, sent, axis):
    chips, cores = 4, 2
    last = chips * cores - 1
    up = lax.ppermute(sent[0], axis, [(i, i + cores) for i in range(cores * step)])
    down_route = [(last - i, last - i - cores) for i in range(cores * step)]
    down = lax.ppermute(sent[1], axis, down_route)
    return up, down


def line_terms(step, own, got, arrived, axis):
    chip = lax.axis_index(axis) // 2
    return line_step(4 + chip - step, step - 4 + chip, own, got, arrived)


after = lax.optimization_barrier


def finish_kernel(
    width,
    place_ref, own_ref, got_ref, up_ref, down_ref, hidden_ref, scale_ref, gain_ref, dots_ref,
    grad_ref, *refs,
):
    kept_out, sent_out = refs[-2:]
    total = own_ref[0].astype(f32) + got_ref[0].astype(f32)
    total = total + up_ref[...].astype(f32) + down_ref[...].astype(f32)
    share, block = kept_out.shape
    dot = jnp.broadcast_to(dots_ref[...], (128, block)).T * (1.0 / width)
    scale = scale_ref[...]
    parts = []
    for at in range(0, total.shape[1], 128):
        lanes = slice(at, at + 128)
        normal = hidden_ref[:, lanes].astype(f32) * scale
        unit = total[:, lanes] * gain_ref[:, lanes]
        parts.append(scale * (unit - normal * dot) + grad_ref[:, lanes].astype(f32))
    result = jnp.concatenate([part.T for part in parts], axis=0)
    second = place_ref[1] == 1
    kept_out[...] = jnp.where(second, result[share:], result[:share])
    sent_out[...] = jnp.where(second, result[:share], result[share:])


def finish(
    index, own, got, up, down, hidden_in, scale, gain, dots, out_grad, place, target
):
    rows, width = hidden_in.shape
    both = own.shape[2]
    block = SPAN
    count, block_of = group_of(rows, index)
    here = lambda i, at: (at[0], i, 0)
    local_row = lambda i, at: (i, 0)
    token = lambda i, at: (block_of(at[1] * count + i), 0)
    feature = lambda i, at: (block_of(at[1] * count + i), at[0])
    share = both // 2
    operands = [place, own, got, up, down, hidden_in, scale, gain, dots, out_grad]
    in_specs = [
        spec((1, block, both), here), spec((1, block, both), here),
        spec((block, both), local_row), spec((block, both), local_row),
        spec((block, both), feature), spec((block, 128), token),
        spec((1, both), lambda i, at: (0, at[0])), spec((1, block), lambda i, at: (0, i)),
        spec((block, both), feature),
    ]
    aliases = {}
    if target is not None:
        aliases = {len(operands): 0}
        operands.append(target)
        in_specs.append(pl.BlockSpec(memory_space=pl.ANY))
    return pl.pallas_call(
        partial(finish_kernel, width),
        grid_spec=pltpu.PrefetchScalarGridSpec(
            num_scalar_prefetch=1,
            grid=(count,),
            in_specs=in_specs,
            out_specs=[
                spec((share, block), lambda i, at: (0, block_of(at[1] * count + i))),
                spec((share, block), lambda i, at: (0, i)),
            ],
        ),
        out_shape=[
            jax.ShapeDtypeStruct((share, rows), f32),
            jax.ShapeDtypeStruct((share, count * block), f32),
        ],
        input_output_aliases=aliases,
        compiler_params=params(56),
        cost_estimate=pl.CostEstimate(
            flops=rows * both * 5, bytes_accessed=count * block * both * 16, transcendentals=0
        ),
        name="finish",
    )(*operands)


def place_kernel(place_ref, received_ref, target_ref, out_ref):
    out_ref[...] = received_ref[...]


def placed(received, target, place, block_at):
    block = SPAN
    share = received.shape[0]
    return pl.pallas_call(
        place_kernel,
        grid_spec=pltpu.PrefetchScalarGridSpec(
            num_scalar_prefetch=1,
            grid=(received.shape[1] // block,),
            in_specs=[
                spec((share, block), lambda i, at: (0, i)), pl.BlockSpec(memory_space=pl.ANY),
            ],
            out_specs=spec((share, block), lambda i, at: (0, block_at(i, 1 - at[1]))),
        ),
        out_shape=jax.ShapeDtypeStruct(target.shape, target.dtype),
        input_output_aliases={2: 0},
        compiler_params=params(56),
        name="placed",
    )(place, received, target)


def split_kernel(place_ref, rows_ref, kept_out, sent_out):
    share = kept_out.shape[0]
    rows = rows_ref[...].astype(f32).T
    second = place_ref[1] == 1
    kept_out[...] = jnp.where(second, rows[share:], rows[:share]).astype(bf16)
    sent_out[...] = jnp.where(second, rows[:share], rows[share:]).astype(bf16)


def split(rows, place, block_at):
    block = SPAN
    count, both = rows.shape
    share = both // 2
    return pl.pallas_call(
        split_kernel,
        grid_spec=pltpu.PrefetchScalarGridSpec(
            num_scalar_prefetch=1,
            grid=(count // block,),
            in_specs=[spec((block, both), lambda i, at: (i, 0))],
            out_specs=[
                spec((share, block), lambda i, at: (0, block_at(i, at[1]))),
                spec((share, block), lambda i, at: (0, i)),
            ],
        ),
        out_shape=[
            jax.ShapeDtypeStruct((share, 2 * count), bf16),
            jax.ShapeDtypeStruct((share, count), bf16),
        ],
        compiler_params=params(56),
        name="split",
    )(place, rows)


def swapped(mine, other_first, axis):
    count = lax.axis_size(axis)
    share = mine.shape[-1] // 2
    low, high = mine[..., :share], mine[..., share:]
    kept = jnp.where(other_first, high, low)
    sent = jnp.where(other_first, low, high).astype(bf16)
    got = lax.ppermute(sent, axis, [(i, i ^ 1) for i in range(count)]).astype(kept.dtype)
    at = mine.ndim - 2
    return jnp.where(
        other_first, jnp.stack([got, kept], axis=at), jnp.stack([kept, got], axis=at)
    )


def chained(states, decays, mine, backward):
    count = states.shape[0]
    order = range(count)
    if backward:
        order = reversed(order)
    total = jnp.zeros_like(states[0])
    for at in order:
        use = at > mine if backward else at < mine
        total = jnp.where(use, decays[at][:, None] * total + states[at], total)
    return total


def block(
    hidden_in, norm_gain, gate_proj, value_proj, state_proj, step_proj, conv_value,
    conv_value_bias, conv_state, conv_state_bias, step_bias, decay_rate, skip_gain, mix_gain,
    out_proj, out_grad,
):
    rows, width = hidden_in.shape
    groups = lax.axis_size("head")
    share = width // groups
    mine = lax.axis_index("head")
    first_col = mine * share
    chips = groups // 2
    core = mine % 2
    second = core == 1
    inner_local = gate_proj.shape[1]
    inner_width = inner_local * groups
    heads = step_proj.shape[1]
    head_size = inner_local // heads

    def wide(x):
        return jnp.repeat(x, head_size, axis=-1)

    step_wide = wide(step_proj)
    rate, skip, step_shift = (wide(x)[None, :] for x in (decay_rate, skip_gain, step_bias))
    taps = jnp.concatenate([conv_value, conv_state], axis=1)
    bias = jnp.concatenate([conv_value_bias, conv_state_bias])[None, :]
    gain = mix_gain[None, :]

    all_out_proj = lax.all_gather(out_proj, "head")
    projected, gate_in, stream, step, scale_in = project(
        hidden_in, norm_gain, gate_proj, value_proj, state_proj, step_wide
    )
    edge = passed_along(stream[rows - 8 :], "seq", 1)
    grad_gated = lax.dot_general(
        out_grad, out_proj, (((1,), (1,)), ((), ())), preferred_element_type=f32
    )
    partial_mixed, active, slope, reach, steps, states = scan_forward(
        stream, edge, step, taps, bias, step_shift, rate, skip
    )
    at_seq = lax.axis_index("seq")
    decay_here = jnp.exp(reach[rows - 1])
    packed = jnp.concatenate([states[-1], jnp.broadcast_to(decay_here[None, :], (8, 128))])
    gathered = lax.all_gather(packed, "seq")
    decays = gathered[:, 128]
    carried = chained(gathered[:, :128], decays, at_seq, False)
    mixed, sums = join(partial_mixed, active, reach, gate_in, grad_gated, carried, gain)
    sums = summed_over(sums, "head")
    gated_rows, grad_gate16, grad_mixed, grad_mix_gain, incoming = gate_step(
        mixed, active, reach, gate_in, grad_gated, sums, gain, inner_width
    )

    own_tokens = rows // groups
    group_rows = lax.all_to_all(
        gated_rows.reshape(groups, own_tokens, inner_local), "head", 0, 0, tiled=False
    )
    on_line = chips == 4 and 2 * share % 128 == 0 and own_tokens == 2 * SPAN
    partner = [(i, i ^ 1) for i in range(groups)]
    place = jnp.stack([mine // 2, core]).astype(jnp.int32)
    arriving = chained(lax.all_gather(incoming, "seq"), decays, at_seq, True)
    scan_args = (
        stream, edge, active, slope, steps, taps, rate, skip, mixed, grad_mixed, reach, states, carried
    )
    late16, tail, head, late_sums, arriving = scan_backward(
        True, *scan_args, arriving, jnp.zeros((8, stream.shape[1]), f32)
    )
    step_back = wide(step_proj).T * (1.0 / head_size)
    weights = jnp.concatenate(
        [gate_proj.T, value_proj.T, state_proj.T, step_back.astype(bf16)], axis=0
    )
    gain_in = norm_gain[None, :]

    def parts_of(index, half, early16, next_head, weights):
        return input_parts(
            index, half, grad_gate16, early16, late16, weights, hidden_in, scale_in, gain_in, tail,
            next_head, taps, chips,
        )

    def exchanged(other):
        return lax.ppermute(other, "head", partner)

    def both_halves(own, other):
        return jnp.concatenate(
            [jnp.where(second, other, own), jnp.where(second, own, other)], axis=0
        )

    other_0, other_dots, other_sums = parts_of(0, 1 - core, late16, head, weights)
    got_0 = exchanged(other_0)
    own_0, own_dots, own_sums = parts_of(0, core, late16, head, weights)
    norm_sums, dots_0 = other_sums + own_sums, both_halves(own_dots, other_dots)
    if on_line:
        line_0 = line_sent(1, line_terms(1, own_0, got_0, (), "head"), "head")
    early16, _, head, early_sums, _ = scan_backward(False, *scan_args, arriving, head)
    next_head = passed_along(head, "seq", -1)
    if on_line:
        line_0, _ = after((line_0, early16))
        sent, group_rows = after((line_terms(2, own_0, got_0, line_0, "head"), group_rows))
        line_0 = line_sent(2, sent, "head")
    out_parts = output_rows(
        group_rows, all_out_proj, hidden_in, mine.astype(jnp.int32)[None], chips
    )
    out_parts = out_parts.reshape(groups, own_tokens // 2, 2 * share)
    out_parts = lax.all_to_all(out_parts, "head", 0, 0, tiled=False)
    other_1, other_dots, other_sums = parts_of(1, 1 - core, early16, next_head, weights)
    got_1 = exchanged(other_1)
    if on_line:
        line_0, other_dots = after((line_0, other_dots))
        sent, weights = after((line_terms(3, own_0, got_0, line_0, "head"), weights))
        line_0 = line_sent(3, sent, "head")
    own_1, own_dots, own_sums = parts_of(1, core, early16, next_head, weights)
    norm_sums, dots_1 = norm_sums + other_sums + own_sums, both_halves(own_dots, other_dots)
    dots = jnp.concatenate([dots_0.reshape(-1, 128), dots_1.reshape(-1, 128)], axis=0)
    needs = (late16, next_head, projected, gated_rows)
    if on_line:
        sent, needs, dots = after((line_terms(1, own_1, got_1, (), "head"), needs, dots))
        line_1 = line_sent(1, sent, "head")
    sums = (late_sums + early_sums).at[5, :128].set(grad_mix_gain[0])
    headed = jnp.concatenate(
        [sums[:5, 128:384].reshape(-1, 128), norm_sums.reshape(-1, 128), dots], axis=0
    )
    headed = summed_over(headed, "head", False)
    unit_dot, headed = headed[-dots.shape[0] :], headed[: -dots.shape[0]]

    def dots_of(total):
        total = total.reshape(-1)
        return total[: dots_0.size].reshape(2, -1), total[dots_0.size :].reshape(2, -1)

    late_fixed, next_rows, projected, gated_rows = needs
    extra = [sum(taps[tap] * next_rows[row - tap] for tap in range(row + 1)) for row in range(3)]
    fixed = tail.at[5:].add(jnp.stack(extra))
    fixed16 = fixed.astype(bf16)
    low16 = (fixed - fixed16.astype(f32))[:, inner_local:].astype(bf16)
    late_fixed = lax.dynamic_update_slice(late_fixed, fixed16, (rows // 2 - 8, 0))
    late_fixed = lax.dynamic_update_slice(late_fixed, low16, (rows // 2 - 8, 512))
    contract = (((0,), (0,)), ((), ()))
    rest16 = jnp.concatenate([early16, late_fixed], axis=0)

    def product(left, right):
        return lax.dot_general(left, right, contract, preferred_element_type=f32)

    grad_rest = product(projected, rest16)
    state_part = row_major(grad_rest[:, 128:384] + grad_rest[:, 512:768])
    grad_value_proj = row_major(grad_rest[:, :128])
    step_sums = row_major(grad_rest[:, 384:512]).T[::head_size]
    if on_line:
        line_1, unit_dot, state_part = after((line_1, unit_dot, state_part))
        sent = line_terms(2, own_1, got_1, line_1, "head")
        sent, gated_rows, projected, sums = after((sent, gated_rows, projected, sums))
        line_1 = line_sent(2, sent, "head")
    grad_gate_proj = row_major(product(projected, grad_gate16))
    grad_out_proj = product(gated_rows, out_grad)
    grad_state_proj = lax.psum_scatter(state_part, "head", scatter_dimension=0, tiled=True)
    grad_state_proj = summed_over(grad_state_proj, "seq", False)
    grad_value_proj, grad_gate_proj = (
        total.astype(f32)
        for total in lax.psum((grad_value_proj.astype(bf16), grad_gate_proj.astype(bf16)), "seq")
    )
    grad_out_proj = summed_over(grad_out_proj, "seq", True)

    small = jnp.concatenate(
        [sums.reshape(-1, 128), step_sums.reshape(-1, 128), headed.reshape(-1, 128)], axis=0
    )
    small = summed_over(small, "seq", False).reshape(-1)
    at = sums.size
    sums, small = small[:at].reshape(8, 512), small[at:]
    grad_step_proj, small = small[: heads * width].reshape(heads, width).T, small[heads * width :]
    state_sums, norm_sums = small[: 5 * 256].reshape(5, 256), small[5 * 256 :]
    grad_norm_gain = lax.dynamic_slice_in_dim(norm_sums, first_col, share, 0)
    if on_line:
        sent = line_terms(3, own_1, got_1, line_1, "head")
        sent, own_0, out_parts = after((sent, own_0, out_parts))
        line_1 = line_sent(3, sent, "head")
        own_block = lambda i, core: 2 * i + core
        block_out, out_sent = split(out_parts.reshape(rows // 2, 2 * share), place, own_block)
        received = lax.ppermute(out_sent, "head", partner)
        block_out = placed(received, block_out, place, own_block).T
        line_dots = dots_of(unit_dot)
        grad_input = None
        for index, own, got, (up, down), dots in (
            (0, own_0, got_0, line_0, line_dots[0]), (1, own_1, got_1, line_1, line_dots[1])
        ):
            count, block_of = group_of(rows, index)
            own_dots = jnp.where(second, dots[1:], dots[:1])
            grad_input, sent = finish(
                index, own, got, up, down, hidden_in, scale_in, gain_in, own_dots, out_grad, place,
                grad_input,
            )
            received = lax.ppermute(sent, "head", partner)
            grad_input = placed(
                received, grad_input, place,
                lambda i, core, count=count, block_of=block_of: block_of(core * count + i),
            )
        grad_input = grad_input.T
    else:
        block_out = swapped(out_parts, second, "head").reshape(rows, share)
        pieces = []
        for own, got in ((own_0, got_0), (own_1, got_1)):
            pair = (own.astype(f32) + got.astype(f32)).astype(bf16)
            both = swapped(spread_sums(pair, "head")[None], second, "head")
            pieces.append(both.reshape(-1, share))
        cut = rows // 2
        grad_projected = jnp.concatenate([pieces[1][:cut], pieces[0], pieces[1][cut:]])
        first, second_dots = (dots.reshape(-1) for dots in dots_of(unit_dot))
        unit_dot = jnp.concatenate([second_dots[:cut], first, second_dots[cut:]])
        hidden_own = lax.dynamic_slice_in_dim(hidden_in, first_col, share, 1).astype(f32)
        gain_own = lax.dynamic_slice_in_dim(norm_gain, first_col, share, 0)
        scale_col = scale_in[:, :1]
        normal_own = hidden_own * scale_col
        grad_unit = grad_projected * gain_own[None, :]
        grad_input = scale_col * (grad_unit - normal_own * (unit_dot / width)[:, None])
        out_grad_own = lax.dynamic_slice_in_dim(out_grad, first_col, share, 1)
        grad_input = grad_input + out_grad_own.astype(f32)

    head_rows = sums[:3, 384:512].reshape(3, heads, head_size)
    return (
        block_out,
        grad_input,
        grad_norm_gain,
        grad_gate_proj,
        grad_value_proj,
        grad_state_proj,
        grad_step_proj,
        sums[:4, :128],
        sums[4, :128],
        state_sums[:4],
        state_sums[4],
        head_rows[0, :, 0],
        head_rows[1, :, 0],
        jnp.sum(head_rows[2], axis=1),
        sums[5, :128],
        grad_out_proj,
    )


def solution(mesh):
    in_specs = (
        P("seq", None), P(), P(None, "head"), P(None, "head"), P(), P(None, "head"),
        P(None, "head"), P("head"), P(), P(), P("head"), P("head"), P("head"), P("head"),
        P("head", None), P("seq", None),
    )
    out_specs = (
        P("seq", "head"), P("seq", "head"), P("head"), P(None, "head"), P(None, "head"),
        P("head", None), P(None, "head"), P(None, "head"), P("head"), P(), P(), P("head"),
        P("head"), P("head"), P("head"), P("head", None),
    )
    return jax.shard_map(block, mesh=mesh, in_specs=in_specs, out_specs=out_specs, check_vma=False)
```

time: 436 us -> 481 us (1.10)
  the two profiles are of different devices: /device:TPU:9 before, /device:TPU:0 now
where the time goes in v2:
time: 481 us; the launch traced here: 477 us
  Pallas kernels  175 us (36%)
  waiting for transfers between devices  112 us (23%)
  starting transfers between devices  66.5 us (14%)
  matrix products  35.4 us (7%)
  local copies, waits for them, and re-layouts  35 us (7%)
  other arithmetic  18.7 us (4%)
  blocking collectives  17.8 us (4%)
  between operations  16.3 us (3%)
    ppermute x6, waiting for transfers between devices, line_sent(): lax.ppermute(sent[0], axis, [(i, i + cores) for i in range(cores * step)])  43.8 us
    ppermute x12, waiting for transfers between devices, summed_over(): lax.ppermute(value, axis, [(i, i ^ bit) for i in range(count)])  43.4 us
    pallas_call x4, Pallas kernels, input_parts(): pl.pallas_call(partial(parts_kernel, block_of, count, blocks - 1, blocks...  32.1 us
    pallas_call x2, Pallas kernels, scan_backward(): pl.pallas_call(partial(backward_kernel, first), grid=(count,), in_specs=[...  29.7 us
    ppermute x6, starting transfers between devices, line_sent(): lax.ppermute(sent[0], axis, [(i, i + cores) for i in range(cores * step)])  29.2 us
    dot_general x3, matrix products, product(): return lax.dot_general(left, right, contract, preferred_element_type=f32)  27.7 us
    pallas_call x6, Pallas kernels, line_step(): pl.pallas_call(line_kernel, grid_spec=pltpu.PrefetchScalarGridSpec(num_sc...  23.5 us
    psum x1, waiting for transfers between devices, block(): lax.psum((grad_value_proj.astype(bf16), grad_gate_proj.astype(bf16)), 'seq')  20.3 us
  transfers between devices with their start and end apart: 36, of which 13 were waited for; matrix products, arithmetic and copies ran while one was open for 14% of the time, Pallas kernels for 21%

profile of v2, /device:TPU:0, one launch (start us, length us, event | category | flops | bytes accessed | tf_op | source)
XLA Modules:
  0.0 477.1 jit_solution(881419962057249668)
XLA Ops:
  11.0 17.1 %project.1 = (bf16[4096,1536]{1,0:T(8,128)(2,1)}, f32[4096,128]{1,0:T(8,128)}, bf16[4096,384]{1,0:T(8,128)(2,1)}, f32[4096,128]{1,0:T(8,128)}, f32[4096,128]{1,0:T(8,128)}) custom-call(bf16[4096,1536]{1,0:T(8,128)(2,1)} %hidden_ref.15, f32[1,1536]{1,0:T(1,128)} %broadcast_in_dim.43.gain_ref, bf16[1536,128]{1,0:T(8,128)(2,1)} %gate_ref.1, ...), custom_call_target="tpu_custom_call" | custom-call | flops 8053063680 | bytes 25165824 | tf_op jit(solution)/shard_map/project/pallas_call | solution.py:114
  33.8 7.7 %fusion.22.grad_ref = f32[4096,128]{1,0:T(8,128)} fusion(bf16[4096,1536]{1,0:T(8,128)(2,1)} %grad_ref.3, bf16[128,1536]{1,0:T(8,128)(2,1)S(1)} %copy-done.5), kind=kOutput, calls=%fused_computation.77 | convolution fusion | flops 1610612736 | bytes 15073280 | tf_op jit(solution)/shard_map/dot_general | solution.py:923
  44.7 18.9 %scan_forward.1 = (f32[4096,128]{1,0:T(8,128)}, f32[4096,384]{1,0:T(8,128)}, f32[4096,384]{1,0:T(8,128)}, f32[4096,128]{1,0:T(8,128)}, f32[4096,384]{1,0:T(8,128)}, /*index=5*/f32[16,128,128]{2,1,0:T(8,128)}) custom-call(bf16[4096,384]{1,0:T(8,128)(2,1)} %get-tuple-element.127.stream_ref.before_ref, bf16[8,384]{1,0:T(8,128)(2,1)} %copy-done.27, ...), custom_call_target="tpu_custom_call" | custom-call | flops 1887436800 | bytes 26214400 | tf_op jit(solution)/shard_map/scan_forward/pallas_call | solution.py:221
  65.2 9.4 %all-gather = f32[544,128]{1,0:T(8,128)S(1)} all-gather(f32[136,128]{1,0:T(8,128)S(1)} %pad_maximum_fusion.1), channel_id=2, replica_groups=mesh['seq'=4,'head'=8] {'seq'}, dimensions={0}, use_global_device_ids=true | all-gather | bytes 348160 | tf_op jit(solution)/shard_map/all_gather | solution.py:932
  75.3 6.8 %join.1 = (f32[4096,128]{1,0:T(8,128)}, f32[8,1024]{1,0:T(8,128)}) custom-call(f32[4096,128]{1,0:T(8,128)} %get-tuple-element.129.mixed_ref, f32[4096,384]{1,0:T(8,128)} %get-tuple-element.130.query_ref.active_ref, f32[4096,128]{1,0:T(8,128)} %get-tuple-element.131.reach_ref, f32[4096,128]{1,0:T(8,128)} %get-tuple-element.132.gate_ref, ...), custom_call_target="tpu_custom_call" | custom-call | flops 134217728 | bytes 11534336 | tf_op jit(solution)/shard_map/join/pallas_call | solution.py:269
  93.6 7.8 %gate_step.1 = (bf16[4096,128]{1,0:T(8,128)(2,1)}, bf16[4096,128]{1,0:T(8,128)(2,1)}, f32[4096,128]{1,0:T(8,128)}, f32[1,128]{1,0:T(1,128)}, f32[128,128]{1,0:T(8,128)}) custom-call(f32[4096,128]{1,0:T(8,128)} %get-tuple-element.134.mixed_ref, f32[4096,384]{1,0:T(8,128)} %get-tuple-element.130.query_ref.active_ref, ...), custom_call_target="tpu_custom_call" | custom-call | flops 134217728 | bytes 13631488 | tf_op jit(solution)/shard_map/gate_step/pallas_call | solution.py:322
  101.4 8.5 %all-gather.1 = f32[512,128]{1,0:T(8,128)S(1)} all-gather(f32[128,128]{1,0:T(8,128)} %get-tuple-element.140), channel_id=3, replica_groups=mesh['seq'=4,'head'=8] {'seq'}, dimensions={0}, use_global_device_ids=true | all-gather | bytes 327680 | tf_op jit(solution)/shard_map/all_gather | solution.py:948
  111.2 14.8 %scan_backward.2 = (bf16[2048,768]{1,0:T(8,128)(2,1)}, f32[8,384]{1,0:T(8,128)}, f32[8,384]{1,0:T(8,128)}, f32[8,512]{1,0:T(8,128)}, f32[128,128]{1,0:T(8,128)}) custom-call(bf16[4096,384]{1,0:T(8,128)(2,1)} %get-tuple-element.127.stream_ref.before_ref, bf16[4096,384]{1,0:T(8,128)(2,1)} %get-tuple-element.127.stream_ref.before_ref, ...), custom_call_target="tpu_custom_call" | custom-call | flops 1572864000 | bytes 15728640 | tf_op jit(solution)/shard_map/scan_backward/pallas_call | solution.py:480
  132.8 14.9 %scan_backward.3 = (bf16[2048,768]{1,0:T(8,128)(2,1)}, f32[8,384]{1,0:T(8,128)}, f32[8,384]{1,0:T(8,128)}, f32[8,512]{1,0:T(8,128)}, f32[128,128]{1,0:T(8,128)}) custom-call(bf16[4096,384]{1,0:T(8,128)(2,1)} %get-tuple-element.127.stream_ref.before_ref, bf16[4096,384]{1,0:T(8,128)(2,1)} %get-tuple-element.127.stream_ref.before_ref, ...), custom_call_target="tpu_custom_call" | custom-call | flops 1572864000 | bytes 15728640 | tf_op jit(solution)/shard_map/scan_backward/pallas_call | solution.py:480
  154.1 9.4 %input_parts.6 = (bf16[4,1280,384]{2,1,0:T(8,128)(2,1)}, f32[1,1280]{1,0:T(1,128)}, f32[1,1536]{1,0:T(1,128)}) custom-call(s32[1]{0:T(128)} %bitcast.21.half_ref, bf16[4096,128]{1,0:T(8,128)(2,1)} %get-tuple-element.136.gate_ref, bf16[2048,768]{1,0:T(8,128)(2,1)} %get-tuple-element.143.early_ref, bf16[2048,768]{1,0:T(8,128)(2,1)} %get-tuple-element.185.early_ref.late_ref, ...), custom_call_target="tpu_custom_call" | custom-call | flops 2516582400 | bytes 9830400 | tf_op jit(solution)/shard_map/input_parts/pallas_call | solution.py:582
  186.1 13.5 %collective-permute-done.5.refs_0_ = bf16[768,384]{1,0:T(8,128)(2,1)S(1)} collective-permute-done((bf16[768,384]{1,0:T(8,128)(2,1)}, bf16[768,384]{1,0:T(8,128)(2,1)S(1)}, u32[]{:S(2)}, u32[]{:S(2)}) %collective-permute-start.5) | collective-permute-done | bytes 589856 | tf_op jit(solution)/shard_map/ppermute | solution.py:724
  210.8 11.3 %collective-permute-done.7.refs_0_ = bf16[768,384]{1,0:T(8,128)(2,1)S(1)} collective-permute-done((bf16[768,384]{1,0:T(8,128)(2,1)}, bf16[768,384]{1,0:T(8,128)(2,1)S(1)}, u32[]{:S(2)}, u32[]{:S(2)}) %collective-permute-start.7) | collective-permute-done | bytes 589856 | tf_op jit(solution)/shard_map/ppermute | solution.py:724
  226.7 9.4 %input_parts.7 = (bf16[4,1280,384]{2,1,0:T(8,128)(2,1)}, f32[1,1280]{1,0:T(1,128)}, f32[1,1536]{1,0:T(1,128)}) custom-call(s32[1]{0:T(128)} %bitcast.1.half_ref, bf16[4096,128]{1,0:T(8,128)(2,1)} %get-tuple-element.136.gate_ref, bf16[2048,768]{1,0:T(8,128)(2,1)} %get-tuple-element.143.early_ref, bf16[2048,768]{1,0:T(8,128)(2,1)} %get-tuple-element.185.early_ref.late_ref, ...), custom_call_target="tpu_custom_call" | custom-call | flops 2516582400 | bytes 9830400 | tf_op jit(solution)/shard_map/input_parts/pallas_call | solution.py:582
  241.7 8.1 %collective-permute-start.11 = (bf16[1280,384]{1,0:T(8,128)(2,1)}, bf16[1280,384]{1,0:T(8,128)(2,1)}, u32[]{:S(2)}, u32[]{:S(2)}) collective-permute-start(bf16[1280,384]{1,0:T(8,128)(2,1)} %get-tuple-element.174), channel_id=1, source_target_pairs={{0,2},{1,3},{8,10},{9,11},{16,18},{17,19},{24,26},{25,27}} | collective-permute-start | bytes 2949128 | tf_op jit(solution)/shard_map/ppermute | solution.py:724
  252.8 7.0 %output_rows.1 = bf16[4,2,256,384]{3,2,1,0:T(8,128)(2,1)} custom-call(s32[1]{0:T(128)} %bitcast.27.at_ref, bf16[8,512,128]{2,1,0:T(8,128)(2,1)} %copy-done.3, bf16[8,128,1536]{2,1,0:T(8,128)(2,1)} %bitcast.107, bf16[4096,1536]{1,0:T(8,128)(2,1)} %hidden_ref.15), custom_call_target="tpu_custom_call" | custom-call | flops 1610612736 | bytes 8388608 | tf_op jit(solution)/shard_map/output_rows/pallas_call | solution.py:634
  264.1 13.7 %fusion = f32[1536,768]{1,0:T(8,128)S(1)} fusion(bf16[4096,1536]{1,0:T(8,128)(2,1)} %get-tuple-element.211, bf16[2048,768]{1,0:T(8,128)(2,1)S(1)} %fusion.17, bf16[2048,768]{1,0:T(8,128)(2,1)} %get-tuple-element.143.early_ref), kind=kOutput, calls=%fused_computation | convolution fusion | flops 9676259328 | bytes 23592960 | tf_op jit(solution)/shard_map/dot_general | solution.py:1027
  282.0 21.0 %collective-permute-done.15 = f32[54,128]{1,0:T(8,128)S(1)} collective-permute-done((f32[54,128]{1,0:T(8,128)S(1)}, f32[54,128]{1,0:T(8,128)S(1)}, u32[]{:S(2)}, u32[]{:S(2)}) %collective-permute-start.15) | collective-permute-done | bytes 27680 | tf_op jit(solution)/shard_map/ppermute | solution.py:674
  325.8 11.8 %collective-permute-done.16.refs_0_ = bf16[1280,384]{1,0:T(8,128)(2,1)S(1)} collective-permute-done((bf16[1280,384]{1,0:T(8,128)(2,1)}, bf16[1280,384]{1,0:T(8,128)(2,1)S(1)}, u32[]{:S(2)}, u32[]{:S(2)}) %collective-permute-start.16) | collective-permute-done | bytes 983072 | tf_op jit(solution)/shard_map/ppermute | solution.py:724
  344.1 7.6 %collective-permute-start.19 = (bf16[1280,384]{1,0:T(8,128)(2,1)}, bf16[1280,384]{1,0:T(8,128)(2,1)S(1)}, u32[]{:S(2)}, u32[]{:S(2)}) collective-permute-start(bf16[1280,384]{1,0:T(8,128)(2,1)} %get-tuple-element.200), channel_id=1, source_target_pairs={{0,2},{1,3},{2,4},{3,5},{4,6},{5,7},{8,10},{9,11},{10,12},{11,13},... | collective-permute-start | bytes 2949128 | tf_op jit(solution)/shard_map/ppermute | solution.py:724
  364.4 6.7 %fusion.23 = f32[128,1536]{1,0:T(8,128)S(1)} fusion(bf16[4096,128]{1,0:T(8,128)(2,1)} %get-tuple-element.213, bf16[4096,1536]{1,0:T(8,128)(2,1)} %grad_ref.3), kind=kOutput, calls=%fused_computation.78 | convolution fusion | flops 1610612736 | bytes 14417920 | tf_op jit(solution)/shard_map/dot_general | solution.py:1027
  380.6 7.1 %finish.3 = (f32[192,4096]{1,0:T(8,128)}, f32[192,1280]{1,0:T(8,128)}) custom-call(s32[2]{0:T(128)} %pad_add_fusion.place_ref, bf16[4,1280,384]{2,1,0:T(8,128)(2,1)} %get-tuple-element.165.up_own.down_own.own_ref, bf16[4,1280,384]{2,1,0:T(8,128)(2,1)} %collective-permute-done.10.up_got.down_got.got_ref, ...), custom_call_target="tpu_custom_call", output_to_operand_aliasing={{0}: (10, {})} | custom-call | flops 7864320 | bytes 7864320 | tf_op jit(solution)/shard_map/finish/pallas_call | solution.py:786
  387.8 7.2 %convolution_convert_fusion = bf16[1536,128]{1,0:T(8,128)(2,1)} fusion(bf16[4096,1536]{1,0:T(8,128)(2,1)} %get-tuple-element.211, bf16[4096,128]{1,0:T(8,128)(2,1)S(1)} %copy-done.2), kind=kOutput, calls=%fused_computation.4 | convolution fusion | flops 1610809344 | bytes 14024704 | tf_op jit(solution)/shard_map/dot_general | solution.py:1027
  409.4 18.5 %collective-permute-done.27 = f32[192,256]{1,0:T(8,128)S(1)} collective-permute-done((f32[192,256]{1,0:T(8,128)}, f32[192,256]{1,0:T(8,128)S(1)}, u32[]{:S(2)}, u32[]{:S(2)}) %collective-permute-start.27) | collective-permute-done | bytes 196640 | tf_op jit(solution)/shard_map/ppermute | solution.py:674
  431.0 20.3 %all-reduce.3.cloned.1.call-done = (bf16[1536,128]{1,0:T(8,128)(2,1)}, bf16[1536,128]{1,0:T(8,128)(2,1)}) async-done(((bf16[1536,128]{1,0:T(8,128)(2,1)}, bf16[1536,128]{1,0:T(8,128)(2,1)}), (bf16[1536,128]{1,0:T(8,128)(2,1)}, bf16[1536,128]{1,0:T(8,128)(2,1)})) %all-reduce.3.cloned.1.call-update) | async-done | bytes 786448 | tf_op jit(solution)/shard_map/psum | solution.py:1044
  (266 shorter events, 182.4 us)
Async XLA Ops:
  8.0 244.8 %all-gather.5.cloned.1.call-start = ((), (), s32[]{:S(2)}) async-start(), calls=%async_computation.4 | async-start | bytes 3538944 | tf_op jit(solution)/shard_map/all_gather | solution.py:918
  132.7 43.5 %collective-permute-start.4 = (bf16[4,768,384]{2,1,0:T(8,128)(2,1)}, bf16[4,768,384]{2,1,0:T(8,128)(2,1)S(1)}, u32[]{:S(2)}, u32[]{:S(2)}) collective-permute-start(bf16[4,768,384]{2,1,0:T(8,128)(2,1)} %get-tuple-element.148), channel_id=1, source_target_pairs={{0,1},{1,0},{2,3},{3,2},{4,5},{5,4},{6,7},{7,6},{8,9},{9,8},{10,11... | collective-permute-start | bytes 7077896 | tf_op jit(solution)/shard_map/ppermute | solution.py:968
  163.5 74.1 %collective-permute-start.10 = (bf16[4,1280,384]{2,1,0:T(8,128)(2,1)}, bf16[4,1280,384]{2,1,0:T(8,128)(2,1)}, u32[]{:S(2)}, u32[]{:S(2)}) collective-permute-start(bf16[4,1280,384]{2,1,0:T(8,128)(2,1)} %get-tuple-element.166), channel_id=1, source_target_pairs={{0,1},{1,0},{2,3},{3,2},{4,5},{5,4},{6,7},{7,6},{8,9},{9,8},{10,11... | collective-permute-start | bytes 11796488 | tf_op jit(solution)/shard_map/ppermute | solution.py:968
  163.6 41.2 %all-to-all-start = ((bf16[8,512,128]{2,1,0:T(8,128)(2,1)}), bf16[8,512,128]{2,1,0:T(8,128)(2,1)S(1)}, u32[]{:S(2)}, u32[]{:S(2)}) async-start(bf16[8,512,128]{2,1,0:T(8,128)(2,1)} %bitcast.26), calls=%async_computation | async-start | bytes 2097152 | tf_op jit(solution)/shard_map/all_to_all | solution.py:942
  241.7 61.9 %collective-permute-start.11 = (bf16[1280,384]{1,0:T(8,128)(2,1)}, bf16[1280,384]{1,0:T(8,128)(2,1)}, u32[]{:S(2)}, u32[]{:S(2)}) collective-permute-start(bf16[1280,384]{1,0:T(8,128)(2,1)} %get-tuple-element.174), channel_id=1, source_target_pairs={{0,2},{1,3},{8,10},{9,11},{16,18},{17,19},{24,26},{25,27}} | collective-permute-start | bytes 2949128 | tf_op jit(solution)/shard_map/ppermute | solution.py:724
  249.8 53.8 %collective-permute-start.12 = (bf16[1280,384]{1,0:T(8,128)(2,1)}, bf16[1280,384]{1,0:T(8,128)(2,1)}, u32[]{:S(2)}, u32[]{:S(2)}) collective-permute-start(bf16[1280,384]{1,0:T(8,128)(2,1)} %get-tuple-element.175), channel_id=1, source_target_pairs={{7,5},{6,4},{15,13},{14,12},{23,21},{22,20},{31,29},{30,28}} | collective-permute-start | bytes 2949128 | tf_op jit(solution)/shard_map/ppermute | solution.py:726
  252.7 25.2 %collective-permute-start.14 = (f32[54,128]{1,0:T(8,128)S(1)}, f32[54,128]{1,0:T(8,128)S(1)}, u32[]{:S(2)}, u32[]{:S(2)}) collective-permute-start(f32[54,128]{1,0:T(8,128)S(1)} %fusion.31), channel_id=1, source_target_pairs={{0,2},{1,3},{2,0},{3,1},{4,6},{5,7},{6,4},{7,5},{8,10},{9,11},{10,... | collective-permute-start | bytes 82952 | tf_op jit(solution)/shard_map/ppermute | solution.py:674
  259.8 84.3 %all-to-all-start.1 = ((bf16[8,256,384]{2,1,0:T(8,128)(2,1)}), bf16[8,256,384]{2,1,0:T(8,128)(2,1)}, u32[]{:S(2)}, u32[]{:S(2)}) async-start(bf16[8,256,384]{2,1,0:T(8,128)(2,1)} %bitcast.105), calls=%async_computation.1 | async-start | bytes 3145728 | tf_op jit(solution)/shard_map/all_to_all | solution.py:991
  264.1 144.3 %reduce-scatter.2.cloned.1.call-start = ((), (), s32[]{:S(2)}) async-start(), calls=%async_computation.3 | async-start | bytes 1769472 | tf_op jit(solution)/shard_map/reduce_scatter | solution.py:1040
  277.9 25.1 %collective-permute-start.15 = (f32[54,128]{1,0:T(8,128)S(1)}, f32[54,128]{1,0:T(8,128)S(1)}, u32[]{:S(2)}, u32[]{:S(2)}) collective-permute-start(f32[54,128]{1,0:T(8,128)S(1)} %add.157), channel_id=1, source_target_pairs={{0,4},{1,5},{2,6},{3,7},{4,0},{5,1},{6,2},{7,3},{8,12},{9,13},{10,... | collective-permute-start | bytes 82952 | tf_op jit(solution)/shard_map/ppermute | solution.py:674
  308.1 29.4 %collective-permute-start.16 = (bf16[1280,384]{1,0:T(8,128)(2,1)}, bf16[1280,384]{1,0:T(8,128)(2,1)S(1)}, u32[]{:S(2)}, u32[]{:S(2)}) collective-permute-start(bf16[1280,384]{1,0:T(8,128)(2,1)} %get-tuple-element.192), channel_id=1, source_target_pairs={{0,2},{1,3},{2,4},{3,5},{8,10},{9,11},{10,12},{11,13},{16,18},{17,... | collective-permute-start | bytes 2949128 | tf_op jit(solution)/shard_map/ppermute | solution.py:724
  309.5 28.1 %collective-permute-start.17 = (bf16[1280,384]{1,0:T(8,128)(2,1)}, bf16[1280,384]{1,0:T(8,128)(2,1)S(1)}, u32[]{:S(2)}, u32[]{:S(2)}) collective-permute-start(bf16[1280,384]{1,0:T(8,128)(2,1)} %get-tuple-element.193), channel_id=1, source_target_pairs={{7,5},{6,4},{5,3},{4,2},{15,13},{14,12},{13,11},{12,10},{23,21},{2... | collective-permute-start | bytes 2949128 | tf_op jit(solution)/shard_map/ppermute | solution.py:726
  310.8 48.4 %collective-permute-start.21 = (bf16[768,384]{1,0:T(8,128)(2,1)}, bf16[768,384]{1,0:T(8,128)(2,1)}, u32[]{:S(2)}, u32[]{:S(2)}) collective-permute-start(bf16[768,384]{1,0:T(8,128)(2,1)} %get-tuple-element.204), channel_id=1, source_target_pairs={{0,2},{1,3},{2,4},{3,5},{4,6},{5,7},{8,10},{9,11},{10,12},{11,13},... | collective-permute-start | bytes 1769480 | tf_op jit(solution)/shard_map/ppermute | solution.py:724
  314.8 44.5 %collective-permute-start.22 = (bf16[768,384]{1,0:T(8,128)(2,1)}, bf16[768,384]{1,0:T(8,128)(2,1)}, u32[]{:S(2)}, u32[]{:S(2)}) collective-permute-start(bf16[768,384]{1,0:T(8,128)(2,1)} %get-tuple-element.205), channel_id=1, source_target_pairs={{7,5},{6,4},{5,3},{4,2},{3,1},{2,0},{15,13},{14,12},{13,11},{12,10... | collective-permute-start | bytes 1769480 | tf_op jit(solution)/shard_map/ppermute | solution.py:726
  318.0 133.2 %all-reduce.3.cloned.1.call-start = ((), (), s32[]{:S(2)}) async-start(), calls=%async_computation.5 | async-start | bytes 1572864 | tf_op jit(solution)/shard_map/psum | solution.py:1044
  323.9 49.0 %collective-permute-start.25 = (f32[78,128]{1,0:T(8,128)S(1)}, f32[78,128]{1,0:T(8,128)S(1)}, u32[]{:S(2)}, u32[]{:S(2)}) collective-permute-start(f32[78,128]{1,0:T(8,128)S(1)} %pad_maximum_fusion.2), channel_id=1, source_target_pairs={{0,8},{8,0},{16,24},{24,16},{1,9},{9,1},{17,25},{25,17},{2,10},{10... | collective-permute-start | bytes 119816 | tf_op jit(solution)/shard_map/ppermute | solution.py:674
  344.1 35.2 %collective-permute-start.19 = (bf16[1280,384]{1,0:T(8,128)(2,1)}, bf16[1280,384]{1,0:T(8,128)(2,1)S(1)}, u32[]{:S(2)}, u32[]{:S(2)}) collective-permute-start(bf16[1280,384]{1,0:T(8,128)(2,1)} %get-tuple-element.200), channel_id=1, source_target_pairs={{0,2},{1,3},{2,4},{3,5},{4,6},{5,7},{8,10},{9,11},{10,12},{11,13},... | collective-permute-start | bytes 2949128 | tf_op jit(solution)/shard_map/ppermute | solution.py:724
  351.7 27.6 %collective-permute-start.20 = (bf16[1280,384]{1,0:T(8,128)(2,1)}, bf16[1280,384]{1,0:T(8,128)(2,1)S(1)}, u32[]{:S(2)}, u32[]{:S(2)}) collective-permute-start(bf16[1280,384]{1,0:T(8,128)(2,1)} %get-tuple-element.201), channel_id=1, source_target_pairs={{7,5},{6,4},{5,3},{4,2},{3,1},{2,0},{15,13},{14,12},{13,11},{12,10... | collective-permute-start | bytes 2949128 | tf_op jit(solution)/shard_map/ppermute | solution.py:726
  371.8 25.2 %collective-permute-start.29 = (f32[128,1536]{1,0:T(8,128)S(1)}, f32[128,1536]{1,0:T(8,128)S(1)}, u32[]{:S(2)}, u32[]{:S(2)}) collective-permute-start(f32[128,1536]{1,0:T(8,128)S(1)} %fusion.23), channel_id=1, source_target_pairs={{0,16},{8,24},{16,0},{24,8},{1,17},{9,25},{17,1},{25,9},{2,18},{10... | collective-permute-start | bytes 2359304 | tf_op jit(solution)/shard_map/ppermute | solution.py:674
  372.9 22.2 %collective-permute-start.26 = (f32[78,128]{1,0:T(8,128)S(1)}, f32[78,128]{1,0:T(8,128)S(1)}, u32[]{:S(2)}, u32[]{:S(2)}) collective-permute-start(f32[78,128]{1,0:T(8,128)S(1)} %fusion.20), channel_id=1, source_target_pairs={{0,16},{8,24},{16,0},{24,8},{1,17},{9,25},{17,1},{25,9},{2,18},{10... | collective-permute-start | bytes 119816 | tf_op jit(solution)/shard_map/ppermute | solution.py:674
  387.7 76.6 %collective-permute-start.24 = (f32[192,1280]{1,0:T(8,128)}, f32[192,1280]{1,0:T(8,128)S(1)}, u32[]{:S(2)}, u32[]{:S(2)}) collective-permute-start(f32[192,1280]{1,0:T(8,128)} %get-tuple-element.208), channel_id=1, source_target_pairs={{0,1},{1,0},{2,3},{3,2},{4,5},{5,4},{6,7},{7,6},{8,9},{9,8},{10,11... | collective-permute-start | bytes 2949128 | tf_op jit(solution)/shard_map/ppermute | solution.py:1076
  397.1 58.0 %collective-permute-start.30 = (f32[128,1536]{1,0:T(8,128)S(1)}, f32[128,1536]{1,0:T(8,128)S(1)}, u32[]{:S(2)}, u32[]{:S(2)}) collective-permute-start(f32[128,1536]{1,0:T(8,128)S(1)} %add.169), channel_id=1, source_target_pairs={{0,8},{8,0},{16,24},{24,16},{1,9},{9,1},{17,25},{25,17},{2,10},{10... | collective-permute-start | bytes 2359304 | tf_op jit(solution)/shard_map/ppermute | solution.py:674
  405.8 51.9 %collective-permute-start.18 = (bf16[192,2048]{1,0:T(8,128)(2,1)}, bf16[192,2048]{1,0:T(8,128)(2,1)S(1)}, u32[]{:S(2)}, u32[]{:S(2)}) collective-permute-start(bf16[192,2048]{1,0:T(8,128)(2,1)} %get-tuple-element.198), channel_id=1, source_target_pairs={{0,1},{1,0},{2,3},{3,2},{4,5},{5,4},{6,7},{7,6},{8,9},{9,8},{10,11... | collective-permute-start | bytes 2359304 | tf_op jit(solution)/shard_map/ppermute | solution.py:1063
  428.8 27.3 %collective-permute-start.28 = (f32[192,256]{1,0:T(8,128)S(1)}, f32[192,256]{1,0:T(8,128)}, u32[]{:S(2)}, u32[]{:S(2)}) collective-permute-start(f32[192,256]{1,0:T(8,128)S(1)} %add.167), channel_id=1, source_target_pairs={{0,16},{8,24},{16,0},{24,8},{1,17},{9,25},{17,1},{25,9},{2,18},{10... | collective-permute-start | bytes 589832 | tf_op jit(solution)/shard_map/ppermute | solution.py:674
  (57 other events, 577.7 us)
Sparse Core Ops, SparseCore 0:
  133.0 38.8 all-gather.4
  318.1 41.7 reduce-scatter.1
Sparse Core Ops, SparseCore 1:
  395.1 56.1 all-reduce.2

commit v3 on v2

--- a/solution.py
+++ b/solution.py
@@ -10,6 +10,7 @@
 
 
 SPAN = 256
+BLOCK = 512
 epsilon = 1e-05
 f32 = jnp.float32
 bf16 = jnp.bfloat16
@@ -86,7 +87,7 @@
 
 def project_kernel(
     hidden_ref, gain_ref, gate_ref, value_ref, state_ref, step_ref,
-    projected_ref, gate_out, stream_out, step_out, scale_out, weights,
+    projected_ref, gate_out, stream_out, step_out, scale_out, scale_row_out, weights,
 ):
     @pl.when(pl.program_id(0) == 0)
     def _():
@@ -99,7 +100,9 @@
     scale = lax.rsqrt(jnp.mean(hidden * hidden, axis=1, keepdims=True) + epsilon)
     projected = (hidden * scale * gain_ref[...]).astype(bf16)
     projected_ref[...] = projected
-    scale_out[...] = jnp.broadcast_to(scale, scale_out.shape)
+    wide_scale = jnp.broadcast_to(scale, scale_out.shape)
+    scale_out[...] = wide_scale
+    scale_row_out[...] = wide_scale.T[0:1]
     result = mm(projected, weights[...])
     gate_out[...] = result[:, 0:128]
     stream_out[...] = result[:, 128:512].astype(bf16)
@@ -120,7 +123,7 @@
         ],
         out_specs=[
             spec((span, width), row), spec((span, 128), row), spec((span, 384), row),
-            spec((span, 128), row), spec((span, 128), row),
+            spec((span, 128), row), spec((span, 128), row), spec((1, span), lambda i: (0, i)),
         ],
         out_shape=[
             jax.ShapeDtypeStruct((rows, width), bf16),
@@ -128,13 +131,13 @@
             jax.ShapeDtypeStruct((rows, 384), bf16),
             jax.ShapeDtypeStruct((rows, 128), f32),
             jax.ShapeDtypeStruct((rows, 128), f32),
+            jax.ShapeDtypeStruct((1, rows), f32),
         ],
         scratch_shapes=[pltpu.VMEM((width, 640), bf16)],
         compiler_params=params(56),
         cost_estimate=pl.CostEstimate(
             flops=2 * rows * width * 640, bytes_accessed=rows * width * 4, transcendentals=0
         ),
-        name="project",
     )(hidden_in, gain, gate_proj, value_proj, state_proj, step_wide)
 
 
@@ -243,7 +246,6 @@
         cost_estimate=pl.CostEstimate(
             flops=count * 2 * span * span * 900, bytes_accessed=rows * 128 * 50, transcendentals=0
         ),
-        name="scan_forward",
     )(stream, edge, step, taps, bias, step_bias, rate, skip)
 
 
@@ -279,7 +281,6 @@
         cost_estimate=pl.CostEstimate(
             flops=2 * rows * 128 * 128, bytes_accessed=rows * 128 * 22, transcendentals=0
         ),
-        name="join",
     )(mixed, active, reach, gate, grad, carried, gain)
 
 
@@ -341,7 +342,6 @@
         cost_estimate=pl.CostEstimate(
             flops=2 * rows * 128 * 128, bytes_accessed=rows * 128 * 26, transcendentals=0
         ),
-        name="gate_step",
     )(mixed, active, reach, gate, grad, sums, gain)
 
 
@@ -507,7 +507,6 @@
         cost_estimate=pl.CostEstimate(
             flops=count * 2 * span * span * 1500, bytes_accessed=rows * 128 * 30, transcendentals=0
         ),
-        name="scan_backward",
     )(
         stream, stream, edge, active, slope, steps, taps, rate, skip, mixed, grad, reach, states,
         states, carried, arriving, next_rows,
@@ -515,20 +514,20 @@
 
 
 def group_of(rows, index):
-    half = rows // SPAN // 2
+    half = rows // BLOCK // 2
     if index == 0:
-        return half // 2 - 1, lambda place: half + place
-    return half // 2 + 1, lambda place: jnp.where(place < half, place, place + half - 2)
+        return half - 1, lambda place: half + place
+    return half + 1, lambda place: jnp.where(place < half, place, place + half - 1)
 
 
 def parts_kernel(
-    block_of, count, last_block, early_blocks,
-    half_ref, gate_ref, early_ref, late_ref, weights_ref, hidden_ref, scale_ref, gain_ref, tail_ref,
+    block_of, last_block, early_blocks,
+    place_ref, gate_ref, early_ref, late_ref, weights_ref, hidden_ref, scale_ref, gain_ref, tail_ref,
     next_ref, taps_ref,
-    parts_out, dots_out, sums_out,
+    own_out, other_out, dots_out, sums_out,
     left, edge,
 ):
-    at_block = block_of(half_ref[0] * count + pl.program_id(0))
+    at_block = block_of(pl.program_id(0))
 
     @pl.when(pl.program_id(0) == 0)
     def _():
@@ -554,52 +553,61 @@
             fixed = fixed + taps_ref[tap : tap + 1] * edge[3 - tap : 11 - tap]
         left[block - 8 :, 128:512] = fixed.astype(bf16)
 
-    chips, _, share = parts_out.shape
+    chips, share, _ = own_out.shape
     total = mm(left[...], weights_ref[...]).astype(bf16)
     scale = scale_ref[...]
     summed = None
+    turned = []
     for at in range(0, total.shape[1], 128):
         lanes = slice(at, at + 128)
-        product = total[:, lanes].astype(f32) * (hidden_ref[:, lanes].astype(f32) * scale)
+        part = total[:, lanes].astype(f32)
+        turned.append(part.T)
+        product = part * (hidden_ref[:, lanes].astype(f32) * scale)
         sums_out[0:1, lanes] += jnp.sum(product, axis=0, keepdims=True)
         product = product * gain_ref[:, lanes]
         summed = product if summed is None else summed + product
     dots_out[...] = jnp.sum(summed.T, axis=0, keepdims=True)
+    turned = jnp.concatenate(turned, axis=0)
+    second = place_ref[1] == 1
     for chip in range(chips):
-        parts_out[chip] = total[:, chip * share : (chip + 1) * share]
+        low = turned[2 * chip * share : (2 * chip + 1) * share]
+        high = turned[(2 * chip + 1) * share : (2 * chip + 2) * share]
+        own_out[chip] = jnp.where(second, high, low).astype(bf16)
+        other_out[chip] = jnp.where(second, low, high).astype(bf16)
 
 
 def input_parts(
-    index, half, gate16, early16, late16, weights, hidden_in, scale, gain, tail, next_head, taps, chips
+    index, place, gate16, early16, late16, weights, hidden_in, scale, gain, tail, next_head, taps,
+    chips,
 ):
     rows, width = hidden_in.shape
-    block = SPAN
+    block = BLOCK
     count, block_of = group_of(rows, index)
     blocks = rows // block
-    at = lambda i, half: block_of(half[0] * count + i)
-    row = lambda i, half: (at(i, half), 0)
-    share = width // chips
+    row = lambda i, at: (block_of(i), 0)
+    share = width // chips // 2
+    turned = spec((chips, share, block), lambda i, at: (0, 0, i))
     return pl.pallas_call(
-        partial(parts_kernel, block_of, count, blocks - 1, blocks // 2),
+        partial(parts_kernel, block_of, blocks - 1, blocks // 2),
         grid_spec=pltpu.PrefetchScalarGridSpec(
             num_scalar_prefetch=1,
             grid=(count,),
             in_specs=[
                 spec((block, 128), row),
-                spec((block, 512), lambda i, half: (jnp.minimum(at(i, half), blocks // 2 - 1), 0)),
-                spec((block, 512), lambda i, half: (jnp.maximum(at(i, half) - blocks // 2, 0), 0)),
+                spec((block, 512), lambda i, at: (jnp.minimum(block_of(i), blocks // 2 - 1), 0)),
+                spec((block, 512), lambda i, at: (jnp.maximum(block_of(i) - blocks // 2, 0), 0)),
                 whole_block(weights), spec((block, width), row), spec((block, 128), row),
                 whole_block(gain), whole_block(tail), whole_block(next_head), whole_block(taps),
             ],
             out_specs=[
-                spec((chips, block, share), lambda i, half: (0, i, 0)),
-                spec((1, block), lambda i, half: (0, i)),
-                spec((1, width), lambda i, half: (0, 0)),
+                turned, turned, spec((1, block), lambda i, at: (0, i)),
+                spec((1, width), lambda i, at: (0, 0)),
             ],
             scratch_shapes=[pltpu.VMEM((block, 640), bf16), pltpu.VMEM((16, 384), f32)],
         ),
         out_shape=[
-            jax.ShapeDtypeStruct((chips, count * block, share), bf16),
+            jax.ShapeDtypeStruct((chips, share, count * block), bf16),
+            jax.ShapeDtypeStruct((chips, share, count * block), bf16),
             jax.ShapeDtypeStruct((1, count * block), f32),
             jax.ShapeDtypeStruct((1, width), f32),
         ],
@@ -608,47 +616,65 @@
             flops=2 * count * block * width * 640, bytes_accessed=count * block * width * 5,
             transcendentals=0,
         ),
-        name="input_parts",
     )(
-        half.astype(jnp.int32)[None], gate16, early16, late16, weights, hidden_in, scale, gain, tail,
-        next_head, taps,
+        place, gate16, early16, late16, weights, hidden_in, scale, gain, tail, next_head, taps
     )
 
 
 def output_kernel(at_ref, rows_ref, weights_ref, hidden_ref, parts_out):
-    chips, _, _, share = parts_out.shape
+    groups, share, _ = parts_out.shape
     summed = None
     for group in range(rows_ref.shape[0]):
         term = mm(rows_ref[group], weights_ref[group]).astype(bf16).astype(f32)
         summed = term if summed is None else summed + term
-    total = (hidden_ref[...].astype(f32) + summed).astype(bf16)
-    for chip in range(chips):
-        parts_out[chip, 0] = total[:, chip * share : (chip + 1) * share]
-
-
-def output_rows(rows, weights, hidden, at, chips):
+    total = hidden_ref[...].astype(f32) + summed
+    turned = [total[:, at : at + 128].T for at in range(0, total.shape[1], 128)]
+    turned = jnp.concatenate(turned, axis=0)
+    for group in range(groups):
+        parts_out[group] = turned[group * share : (group + 1) * share].astype(bf16)
+
+
+def output_rows(rows, weights, hidden, at):
     groups, tokens, inner = rows.shape
     width = hidden.shape[1]
-    block = tokens // 2
-    share = width // chips
+    block = min(tokens, SPAN)
+    steps = tokens // block
+    share = width // groups
     return pl.pallas_call(
         output_kernel,
         grid_spec=pltpu.PrefetchScalarGridSpec(
             num_scalar_prefetch=1,
-            grid=(2,),
+            grid=(steps,),
             in_specs=[
                 spec((groups, block, inner), lambda i, at: (0, i, 0)), whole_block(weights),
-                spec((block, width), lambda i, at: (2 * at[0] + i, 0)),
+                spec((block, width), lambda i, at: (steps * at[0] + i, 0)),
             ],
-            out_specs=spec((chips, 1, block, share), lambda i, at: (0, i, 0, 0)),
-        ),
-        out_shape=jax.ShapeDtypeStruct((chips, 2, block, share), bf16),
+            out_specs=spec((groups, share, block), lambda i, at: (0, 0, i)),
+        ),
+        out_shape=jax.ShapeDtypeStruct((groups, share, tokens), bf16),
         compiler_params=params(56),
         cost_estimate=pl.CostEstimate(
             flops=2 * tokens * groups * inner * width, bytes_accessed=8 << 20, transcendentals=0
         ),
-        name="output_rows",
     )(at, rows, weights, hidden)
+
+
+def side_kernel(blocks_ref, out_ref):
+    tokens = blocks_ref.shape[2]
+    for at in range(blocks_ref.shape[0]):
+        out_ref[:, at * tokens : (at + 1) * tokens] = blocks_ref[at]
+
+
+def side_by_side(blocks):
+    count, share, tokens = blocks.shape
+    return pl.pallas_call(
+        side_kernel,
+        grid=(count // 2,),
+        in_specs=[spec((2, share, tokens), lambda i: (i, 0, 0))],
+        out_specs=spec((share, 2 * tokens), lambda i: (0, i)),
+        out_shape=jax.ShapeDtypeStruct((share, count * tokens), blocks.dtype),
+        compiler_params=params(56),
+    )(blocks)
 
 
 def row_major(x):
@@ -695,26 +721,25 @@
 
 
 def line_step(up_at, down_at, own, got, arrived):
-    chips, rows, width = own.shape
-    block = rows // 2
+    chips, share, tokens = own.shape
+    block = tokens // 2
     at = jnp.stack([up_at, down_at]).astype(jnp.int32)
     at = jnp.clip(at, 0, chips - 1)
-    blocks = [spec((1, block, width), lambda i, at, k=k: (at[k], i, 0)) for k in (0, 0, 1, 1)]
-    plain = spec((block, width), lambda i, at: (i, 0))
+    blocks = [spec((1, share, block), lambda i, at, k=k: (at[k], 0, i)) for k in (0, 0, 1, 1)]
+    plain = spec((share, block), lambda i, at: (0, i))
     return pl.pallas_call(
         line_kernel,
         grid_spec=pltpu.PrefetchScalarGridSpec(
             num_scalar_prefetch=1,
-            grid=(rows // block,),
+            grid=(2,),
             in_specs=blocks + [plain] * len(arrived),
             out_specs=[plain, plain],
         ),
-        out_shape=[jax.ShapeDtypeStruct((rows, width), bf16)] * 2,
+        out_shape=[jax.ShapeDtypeStruct((share, tokens), bf16)] * 2,
         compiler_params=params(56),
         cost_estimate=pl.CostEstimate(
-            flops=rows * width * 4, bytes_accessed=rows * width * 16, transcendentals=0
-        ),
-        name="line_step",
+            flops=share * tokens * 4, bytes_accessed=share * tokens * 16, transcendentals=0
+        ),
     )(at, own, got, own, got, *arrived)
 
 
@@ -735,48 +760,44 @@
 after = lax.optimization_barrier
 
 
+def own_features(rows, second):
+    share = rows.shape[1] // 2
+    turned = [rows[:, at : at + 128].T for at in range(0, 2 * share, 128)]
+    turned = jnp.concatenate(turned, axis=0)
+    return jnp.where(second, turned[share:], turned[:share])
+
+
 def finish_kernel(
     width,
     place_ref, own_ref, got_ref, up_ref, down_ref, hidden_ref, scale_ref, gain_ref, dots_ref,
     grad_ref, *refs,
 ):
-    kept_out, sent_out = refs[-2:]
+    out_ref = refs[-1]
+    second = place_ref[1] == 1
     total = own_ref[0].astype(f32) + got_ref[0].astype(f32)
     total = total + up_ref[...].astype(f32) + down_ref[...].astype(f32)
-    share, block = kept_out.shape
-    dot = jnp.broadcast_to(dots_ref[...], (128, block)).T * (1.0 / width)
+    gain = jnp.broadcast_to(gain_ref[...], (8, gain_ref.shape[1]))
+    gain = own_features(gain, second)[:, 0:1]
     scale = scale_ref[...]
-    parts = []
-    for at in range(0, total.shape[1], 128):
-        lanes = slice(at, at + 128)
-        normal = hidden_ref[:, lanes].astype(f32) * scale
-        unit = total[:, lanes] * gain_ref[:, lanes]
-        parts.append(scale * (unit - normal * dot) + grad_ref[:, lanes].astype(f32))
-    result = jnp.concatenate([part.T for part in parts], axis=0)
-    second = place_ref[1] == 1
-    kept_out[...] = jnp.where(second, result[share:], result[:share])
-    sent_out[...] = jnp.where(second, result[:share], result[share:])
-
-
-def finish(
-    index, own, got, up, down, hidden_in, scale, gain, dots, out_grad, place, target
-):
+    dot = dots_ref[...] * (1.0 / width) * (scale * scale)
+    normal = own_features(hidden_ref[...].astype(f32), second)
+    base = own_features(grad_ref[...].astype(f32), second) - normal * dot
+    out_ref[...] = base + total * (gain * scale)
+
+
+def finish(index, own, got, up, down, hidden_in, scale, gain, dots, out_grad, place, target):
     rows, width = hidden_in.shape
-    both = own.shape[2]
-    block = SPAN
+    share = own.shape[1]
+    both = 2 * share
+    block = BLOCK
     count, block_of = group_of(rows, index)
-    here = lambda i, at: (at[0], i, 0)
-    local_row = lambda i, at: (i, 0)
-    token = lambda i, at: (block_of(at[1] * count + i), 0)
-    feature = lambda i, at: (block_of(at[1] * count + i), at[0])
-    share = both // 2
+    here = spec((1, share, block), lambda i, at: (at[0], 0, i))
+    plain = spec((share, block), lambda i, at: (0, i))
+    feature = spec((block, both), lambda i, at: (block_of(i), at[0]))
     operands = [place, own, got, up, down, hidden_in, scale, gain, dots, out_grad]
     in_specs = [
-        spec((1, block, both), here), spec((1, block, both), here),
-        spec((block, both), local_row), spec((block, both), local_row),
-        spec((block, both), feature), spec((block, 128), token),
-        spec((1, both), lambda i, at: (0, at[0])), spec((1, block), lambda i, at: (0, i)),
-        spec((block, both), feature),
+        here, here, plain, plain, feature, spec((1, block), lambda i, at: (0, block_of(i))),
+        spec((1, both), lambda i, at: (0, at[0])), spec((1, block), lambda i, at: (0, i)), feature,
     ]
     aliases = {}
     if target is not None:
@@ -789,91 +810,15 @@
             num_scalar_prefetch=1,
             grid=(count,),
             in_specs=in_specs,
-            out_specs=[
-                spec((share, block), lambda i, at: (0, block_of(at[1] * count + i))),
-                spec((share, block), lambda i, at: (0, i)),
-            ],
-        ),
-        out_shape=[
-            jax.ShapeDtypeStruct((share, rows), f32),
-            jax.ShapeDtypeStruct((share, count * block), f32),
-        ],
+            out_specs=spec((share, block), lambda i, at: (0, block_of(i))),
+        ),
+        out_shape=jax.ShapeDtypeStruct((share, rows), f32),
         input_output_aliases=aliases,
         compiler_params=params(56),
         cost_estimate=pl.CostEstimate(
-            flops=rows * both * 5, bytes_accessed=count * block * both * 16, transcendentals=0
-        ),
-        name="finish",
+            flops=rows * both * 5, bytes_accessed=count * block * both * 12, transcendentals=0
+        ),
     )(*operands)
-
-
-def place_kernel(place_ref, received_ref, target_ref, out_ref):
-    out_ref[...] = received_ref[...]
-
-
-def placed(received, target, place, block_at):
-    block = SPAN
-    share = received.shape[0]
-    return pl.pallas_call(
-        place_kernel,
-        grid_spec=pltpu.PrefetchScalarGridSpec(
-            num_scalar_prefetch=1,
-            grid=(received.shape[1] // block,),
-            in_specs=[
-                spec((share, block), lambda i, at: (0, i)), pl.BlockSpec(memory_space=pl.ANY),
-            ],
-            out_specs=spec((share, block), lambda i, at: (0, block_at(i, 1 - at[1]))),
-        ),
-        out_shape=jax.ShapeDtypeStruct(target.shape, target.dtype),
-        input_output_aliases={2: 0},
-        compiler_params=params(56),
-        name="placed",
-    )(place, received, target)
-
-
-def split_kernel(place_ref, rows_ref, kept_out, sent_out):
-    share = kept_out.shape[0]
-    rows = rows_ref[...].astype(f32).T
-    second = place_ref[1] == 1
-    kept_out[...] = jnp.where(second, rows[share:], rows[:share]).astype(bf16)
-    sent_out[...] = jnp.where(second, rows[:share], rows[share:]).astype(bf16)
-
-
-def split(rows, place, block_at):
-    block = SPAN
-    count, both = rows.shape
-    share = both // 2
-    return pl.pallas_call(
-        split_kernel,
-        grid_spec=pltpu.PrefetchScalarGridSpec(
-            num_scalar_prefetch=1,
-            grid=(count // block,),
-            in_specs=[spec((block, both), lambda i, at: (i, 0))],
-            out_specs=[
-                spec((share, block), lambda i, at: (0, block_at(i, at[1]))),
-                spec((share, block), lambda i, at: (0, i)),
-            ],
-        ),
-        out_shape=[
-            jax.ShapeDtypeStruct((share, 2 * count), bf16),
-            jax.ShapeDtypeStruct((share, count), bf16),
-        ],
-        compiler_params=params(56),
-        name="split",
-    )(place, rows)
-
-
-def swapped(mine, other_first, axis):
-    count = lax.axis_size(axis)
-    share = mine.shape[-1] // 2
-    low, high = mine[..., :share], mine[..., share:]
-    kept = jnp.where(other_first, high, low)
-    sent = jnp.where(other_first, low, high).astype(bf16)
-    got = lax.ppermute(sent, axis, [(i, i ^ 1) for i in range(count)]).astype(kept.dtype)
-    at = mine.ndim - 2
-    return jnp.where(
-        other_first, jnp.stack([got, kept], axis=at), jnp.stack([kept, got], axis=at)
-    )
 
 
 def chained(states, decays, mine, backward):
@@ -900,7 +845,6 @@
     first_col = mine * share
     chips = groups // 2
     core = mine % 2
-    second = core == 1
     inner_local = gate_proj.shape[1]
     inner_width = inner_local * groups
     heads = step_proj.shape[1]
@@ -916,7 +860,7 @@
     gain = mix_gain[None, :]
 
     all_out_proj = lax.all_gather(out_proj, "head")
-    projected, gate_in, stream, step, scale_in = project(
+    projected, gate_in, stream, step, scale_in, scale_row = project(
         hidden_in, norm_gain, gate_proj, value_proj, state_proj, step_wide
     )
     edge = passed_along(stream[rows - 8 :], "seq", 1)
@@ -942,7 +886,7 @@
     group_rows = lax.all_to_all(
         gated_rows.reshape(groups, own_tokens, inner_local), "head", 0, 0, tiled=False
     )
-    on_line = chips == 4 and 2 * share % 128 == 0 and own_tokens == 2 * SPAN
+    on_line = chips == 4 and 2 * share % 128 == 0
     partner = [(i, i ^ 1) for i in range(groups)]
     place = jnp.stack([mine // 2, core]).astype(jnp.int32)
     arriving = chained(lax.all_gather(incoming, "seq"), decays, at_seq, True)
@@ -958,50 +902,42 @@
     )
     gain_in = norm_gain[None, :]
 
-    def parts_of(index, half, early16, next_head, weights):
+    def parts_of(index, early16, next_head):
         return input_parts(
-            index, half, grad_gate16, early16, late16, weights, hidden_in, scale_in, gain_in, tail,
+            index, place, grad_gate16, early16, late16, weights, hidden_in, scale_in, gain_in, tail,
             next_head, taps, chips,
         )
 
-    def exchanged(other):
-        return lax.ppermute(other, "head", partner)
-
-    def both_halves(own, other):
-        return jnp.concatenate(
-            [jnp.where(second, other, own), jnp.where(second, own, other)], axis=0
-        )
-
-    other_0, other_dots, other_sums = parts_of(0, 1 - core, late16, head, weights)
-    got_0 = exchanged(other_0)
-    own_0, own_dots, own_sums = parts_of(0, core, late16, head, weights)
-    norm_sums, dots_0 = other_sums + own_sums, both_halves(own_dots, other_dots)
+    own_0, other_0, dots_0, norm_sums = parts_of(0, late16, head)
+    got_0 = lax.ppermute(other_0, "head", partner)
+    out_parts = output_rows(group_rows, all_out_proj, hidden_in, mine.astype(jnp.int32)[None])
     if on_line:
-        line_0 = line_sent(1, line_terms(1, own_0, got_0, (), "head"), "head")
+        line_0 = line_terms(1, own_0, got_0, (), "head")
+        line_0 = line_sent(1, line_0, "head")
+    out_parts = lax.all_to_all(out_parts, "head", 0, 0, tiled=False)
     early16, _, head, early_sums, _ = scan_backward(False, *scan_args, arriving, head)
     next_head = passed_along(head, "seq", -1)
+    contract = (((0,), (0,)), ((), ()))
+
+    def product(left, right):
+        return lax.dot_general(left, right, contract, preferred_element_type=f32)
+
+    gated_rows, _ = after((gated_rows, early16))
+    grad_out_proj = product(gated_rows, out_grad)
+    own_1, other_1, dots_1, more_sums = parts_of(1, early16, next_head)
+    norm_sums = norm_sums + more_sums
+    got_1 = lax.ppermute(other_1, "head", partner)
+    dots = jnp.concatenate([dots_0.reshape(-1, 128), dots_1.reshape(-1, 128)], axis=0)
+    needs = (late16, next_head, projected)
     if on_line:
-        line_0, _ = after((line_0, early16))
-        sent, group_rows = after((line_terms(2, own_0, got_0, line_0, "head"), group_rows))
-        line_0 = line_sent(2, sent, "head")
-    out_parts = output_rows(
-        group_rows, all_out_proj, hidden_in, mine.astype(jnp.int32)[None], chips
-    )
-    out_parts = out_parts.reshape(groups, own_tokens // 2, 2 * share)
-    out_parts = lax.all_to_all(out_parts, "head", 0, 0, tiled=False)
-    other_1, other_dots, other_sums = parts_of(1, 1 - core, early16, next_head, weights)
-    got_1 = exchanged(other_1)
-    if on_line:
-        line_0, other_dots = after((line_0, other_dots))
-        sent, weights = after((line_terms(3, own_0, got_0, line_0, "head"), weights))
-        line_0 = line_sent(3, sent, "head")
-    own_1, own_dots, own_sums = parts_of(1, core, early16, next_head, weights)
-    norm_sums, dots_1 = norm_sums + other_sums + own_sums, both_halves(own_dots, other_dots)
-    dots = jnp.concatenate([dots_0.reshape(-1, 128), dots_1.reshape(-1, 128)], axis=0)
-    needs = (late16, next_head, projected, gated_rows)
-    if on_line:
-        sent, needs, dots = after((line_terms(1, own_1, got_1, (), "head"), needs, dots))
+        line_0, dots = after((line_0, dots))
+        line_0 = line_terms(2, own_0, got_0, line_0, "head")
+        line_0 = line_sent(2, line_0, "head")
+        sent = line_terms(1, own_1, got_1, (), "head")
+        sent, needs, dots = after((sent, needs, dots))
         line_1 = line_sent(1, sent, "head")
+        line_0 = line_terms(3, own_0, got_0, line_0, "head")
+        line_0 = line_sent(3, line_0, "head")
     sums = (late_sums + early_sums).at[5, :128].set(grad_mix_gain[0])
     headed = jnp.concatenate(
         [sums[:5, 128:384].reshape(-1, 128), norm_sums.reshape(-1, 128), dots], axis=0
@@ -1009,41 +945,29 @@
     headed = summed_over(headed, "head", False)
     unit_dot, headed = headed[-dots.shape[0] :], headed[: -dots.shape[0]]
 
-    def dots_of(total):
-        total = total.reshape(-1)
-        return total[: dots_0.size].reshape(2, -1), total[dots_0.size :].reshape(2, -1)
-
-    late_fixed, next_rows, projected, gated_rows = needs
+    late_fixed, next_rows, projected = needs
     extra = [sum(taps[tap] * next_rows[row - tap] for tap in range(row + 1)) for row in range(3)]
     fixed = tail.at[5:].add(jnp.stack(extra))
     fixed16 = fixed.astype(bf16)
     low16 = (fixed - fixed16.astype(f32))[:, inner_local:].astype(bf16)
     late_fixed = lax.dynamic_update_slice(late_fixed, fixed16, (rows // 2 - 8, 0))
     late_fixed = lax.dynamic_update_slice(late_fixed, low16, (rows // 2 - 8, 512))
-    contract = (((0,), (0,)), ((), ()))
     rest16 = jnp.concatenate([early16, late_fixed], axis=0)
-
-    def product(left, right):
-        return lax.dot_general(left, right, contract, preferred_element_type=f32)
-
     grad_rest = product(projected, rest16)
     state_part = row_major(grad_rest[:, 128:384] + grad_rest[:, 512:768])
     grad_value_proj = row_major(grad_rest[:, :128])
     step_sums = row_major(grad_rest[:, 384:512]).T[::head_size]
     if on_line:
-        line_1, unit_dot, state_part = after((line_1, unit_dot, state_part))
+        line_1, state_part = after((line_1, state_part))
         sent = line_terms(2, own_1, got_1, line_1, "head")
-        sent, gated_rows, projected, sums = after((sent, gated_rows, projected, sums))
+        sent, projected, sums = after((sent, projected, sums))
         line_1 = line_sent(2, sent, "head")
     grad_gate_proj = row_major(product(projected, grad_gate16))
-    grad_out_proj = product(gated_rows, out_grad)
     grad_state_proj = lax.psum_scatter(state_part, "head", scatter_dimension=0, tiled=True)
     grad_state_proj = summed_over(grad_state_proj, "seq", False)
-    grad_value_proj, grad_gate_proj = (
-        total.astype(f32)
-        for total in lax.psum((grad_value_proj.astype(bf16), grad_gate_proj.astype(bf16)), "seq")
-    )
-    grad_out_proj = summed_over(grad_out_proj, "seq", True)
+    grad_value_proj = summed_over(grad_value_proj, "seq", False)
+    grad_gate_proj = summed_over(grad_gate_proj, "seq", True)
+    grad_out_proj = summed_over(grad_out_proj, "seq", False)
 
     small = jnp.concatenate(
         [sums.reshape(-1, 128), step_sums.reshape(-1, 128), headed.reshape(-1, 128)], axis=0
@@ -1054,42 +978,33 @@
     grad_step_proj, small = small[: heads * width].reshape(heads, width).T, small[heads * width :]
     state_sums, norm_sums = small[: 5 * 256].reshape(5, 256), small[5 * 256 :]
     grad_norm_gain = lax.dynamic_slice_in_dim(norm_sums, first_col, share, 0)
+    unit_dot = unit_dot.reshape(1, -1)
+    dots_0, dots_1 = unit_dot[:, : dots_0.size], unit_dot[:, dots_0.size :]
+
     if on_line:
         sent = line_terms(3, own_1, got_1, line_1, "head")
         sent, own_0, out_parts = after((sent, own_0, out_parts))
         line_1 = line_sent(3, sent, "head")
-        own_block = lambda i, core: 2 * i + core
-        block_out, out_sent = split(out_parts.reshape(rows // 2, 2 * share), place, own_block)
-        received = lax.ppermute(out_sent, "head", partner)
-        block_out = placed(received, block_out, place, own_block).T
-        line_dots = dots_of(unit_dot)
+    block_out = side_by_side(out_parts).T
+    if on_line:
         grad_input = None
         for index, own, got, (up, down), dots in (
-            (0, own_0, got_0, line_0, line_dots[0]), (1, own_1, got_1, line_1, line_dots[1])
+            (0, own_0, got_0, line_0, dots_0), (1, own_1, got_1, line_1, dots_1)
         ):
-            count, block_of = group_of(rows, index)
-            own_dots = jnp.where(second, dots[1:], dots[:1])
-            grad_input, sent = finish(
-                index, own, got, up, down, hidden_in, scale_in, gain_in, own_dots, out_grad, place,
+            grad_input = finish(
+                index, own, got, up, down, hidden_in, scale_row, gain_in, dots, out_grad, place,
                 grad_input,
-            )
-            received = lax.ppermute(sent, "head", partner)
-            grad_input = placed(
-                received, grad_input, place,
-                lambda i, core, count=count, block_of=block_of: block_of(core * count + i),
             )
         grad_input = grad_input.T
     else:
-        block_out = swapped(out_parts, second, "head").reshape(rows, share)
         pieces = []
         for own, got in ((own_0, got_0), (own_1, got_1)):
             pair = (own.astype(f32) + got.astype(f32)).astype(bf16)
-            both = swapped(spread_sums(pair, "head")[None], second, "head")
-            pieces.append(both.reshape(-1, share))
+            pieces.append(spread_sums(pair, "head").T)
         cut = rows // 2
         grad_projected = jnp.concatenate([pieces[1][:cut], pieces[0], pieces[1][cut:]])
-        first, second_dots = (dots.reshape(-1) for dots in dots_of(unit_dot))
-        unit_dot = jnp.concatenate([second_dots[:cut], first, second_dots[cut:]])
+        dots_0, dots_1 = dots_0.reshape(-1), dots_1.reshape(-1)
+        unit_dot = jnp.concatenate([dots_1[:cut], dots_0, dots_1[cut:]])
         hidden_own = lax.dynamic_slice_in_dim(hidden_in, first_col, share, 1).astype(f32)
         gain_own = lax.dynamic_slice_in_dim(norm_gain, first_col, share, 0)
         scale_col = scale_in[:, :1]

time: 481 us -> 450 us (0.936)
  Pallas kernels: 175 us -> 155 us
  local copies, waits for them, and re-layouts: 35 us -> 25.5 us
  waiting for transfers between devices: 112 us -> 104 us
  other arithmetic: 18.7 us -> 23.7 us
    ppermute x12 -> x16, waiting for transfers between devices: 43.4 us -> 69.6 us  [summed_over(): lax.ppermute(value, axis, [(i, i ^ bit) for i in range(count)])]
    pallas_call x8 -> x3, Pallas kernels: 52.4 us -> 30.2 us  [the longest x2 26.6 us: input_parts(): pl.pallas_call(partial(parts_kernel, block_of, blocks - 1, blocks // 2),...]
    psum x1 -> x0, waiting for transfers between devices: 20.3 us -> none  [block(): lax.psum((grad_value_proj.astype(bf16), grad_gate_proj.astype(bf16)), 'seq')]
    ppermute x6, waiting for transfers between devices: 43.8 us -> 26.1 us  [line_sent(): lax.ppermute(sent[0], axis, [(i, i + cores) for i in range(cores * step)])]
    add x12 -> x16, other arithmetic: 5.07 us -> 15.4 us  [summed_over(): value + lax.ppermute(value, axis, [(i, i ^ bit) for i in range(count)])]
    ppermute x12 -> x16, starting transfers between devices: 14.5 us -> 24.1 us  [summed_over(): lax.ppermute(value, axis, [(i, i ^ bit) for i in range(count)])]
    ppermute x6, starting transfers between devices: 29.2 us -> 20.5 us  [line_sent(): lax.ppermute(sent[0], axis, [(i, i + cores) for i in range(cores * step)])]
    unnamed x98 -> x74, local copies, waits for them, and re-layouts: 14.8 us -> 6.36 us
  transfers between devices with their start and end apart: 36 -> 36, of which waited for: 13 -> 12; matrix products, arithmetic and copies ran while one was open for 14% -> 16% of each run, Pallas kernels for 21% -> 11%
where the time goes in v3:
time: 450 us; the launch traced here: 447 us
  Pallas kernels  155 us (34%)
  waiting for transfers between devices  104 us (23%)
  starting transfers between devices  70 us (16%)
  matrix products  36.6 us (8%)
  local copies, waits for them, and re-layouts  25.5 us (6%)
  other arithmetic  23.7 us (5%)
  blocking collectives  17.7 us (4%)
  between operations  14.7 us (3%)
    ppermute x16, waiting for transfers between devices, summed_over(): lax.ppermute(value, axis, [(i, i ^ bit) for i in range(count)])  69.6 us
    pallas_call x2, Pallas kernels, scan_backward(): pl.pallas_call(partial(backward_kernel, first), grid=(count,), in_specs=[...  29.6 us
    dot_general x3, matrix products, product(): return lax.dot_general(left, right, contract, preferred_element_type=f32)  28.9 us
    pallas_call x2, Pallas kernels, input_parts(): pl.pallas_call(partial(parts_kernel, block_of, blocks - 1, blocks // 2),...  26.6 us
    ppermute x6, waiting for transfers between devices, line_sent(): lax.ppermute(sent[0], axis, [(i, i + cores) for i in range(cores * step)])  26.1 us
    ppermute x16, starting transfers between devices, summed_over(): lax.ppermute(value, axis, [(i, i ^ bit) for i in range(count)])  24.1 us
    pallas_call x6, Pallas kernels, line_step(): pl.pallas_call(line_kernel, grid_spec=pltpu.PrefetchScalarGridSpec(num_sc...  23.9 us
    ppermute x6, starting transfers between devices, line_sent(): lax.ppermute(sent[0], axis, [(i, i + cores) for i in range(cores * step)])  20.5 us
  transfers between devices with their start and end apart: 36, of which 12 were waited for; matrix products, arithmetic and copies ran while one was open for 16% of the time, Pallas kernels for 11%

profile of v3, /device:TPU:0, one launch (start us, length us, event | category | flops | bytes accessed | tf_op | source)
XLA Modules:
  0.0 447.3 jit_solution(13711778092742932446)
XLA Ops:
  10.2 17.1 %shard_map.279 = (bf16[4096,1536]{1,0:T(8,128)(2,1)}, f32[4096,128]{1,0:T(8,128)}, bf16[4096,384]{1,0:T(8,128)(2,1)}, f32[4096,128]{1,0:T(8,128)}, f32[4096,128]{1,0:T(8,128)}, /*index=5*/f32[1,4096]{1,0:T(1,128)}) custom-call(bf16[4096,1536]{1,0:T(8,128)(2,1)} %hidden_ref.11, f32[1,1536]{1,0:T(1,128)} %broadcast_in_dim.37.gain_ref, ...), custom_call_target="tpu_custom_call" | custom-call | flops 8053063680 | bytes 25165824 | tf_op jit(solution)/shard_map/pallas_call | solution.py:117
  28.0 4.9 %collective-permute-start = (bf16[8,384]{1,0:T(8,128)(2,1)S(1)}, bf16[8,384]{1,0:T(8,128)(2,1)S(1)}, u32[]{:S(2)}, u32[]{:S(2)}) collective-permute-start(bf16[8,384]{1,0:T(8,128)(2,1)S(1)} %slice.218), channel_id=1, source_target_pairs={{0,8},{8,16},{16,24},{1,9},{9,17},{17,25},{2,10},{10,18},{18,26},{... | collective-permute-start | bytes 18440 | tf_op jit(solution)/shard_map/ppermute | solution.py:687
  32.9 7.7 %fusion.22.grad_ref = f32[4096,128]{1,0:T(8,128)} fusion(bf16[4096,1536]{1,0:T(8,128)(2,1)} %grad_ref.3, bf16[128,1536]{1,0:T(8,128)(2,1)S(1)} %copy-done.5), kind=kOutput, calls=%fused_computation.66 | convolution fusion | flops 1610612736 | bytes 15073280 | tf_op jit(solution)/shard_map/dot_general | solution.py:867
  43.9 18.9 %shard_map.280 = (f32[4096,128]{1,0:T(8,128)}, f32[4096,384]{1,0:T(8,128)}, f32[4096,384]{1,0:T(8,128)}, f32[4096,128]{1,0:T(8,128)}, f32[4096,384]{1,0:T(8,128)}, /*index=5*/f32[16,128,128]{2,1,0:T(8,128)}) custom-call(bf16[4096,384]{1,0:T(8,128)(2,1)} %get-tuple-element.108.stream_ref.before_ref, bf16[8,384]{1,0:T(8,128)(2,1)} %copy-done.17, ...), custom_call_target="tpu_custom_call" | custom-call | flops 1887436800 | bytes 26214400 | tf_op jit(solution)/shard_map/pallas_call | solution.py:224
  64.3 9.4 %all-gather = f32[544,128]{1,0:T(8,128)S(1)} all-gather(f32[136,128]{1,0:T(8,128)S(1)} %pad_maximum_fusion.1), channel_id=2, replica_groups=mesh['seq'=4,'head'=8] {'seq'}, dimensions={0}, use_global_device_ids=true | all-gather | bytes 348160 | tf_op jit(solution)/shard_map/all_gather | solution.py:876
  74.4 6.7 %shard_map.281 = (f32[4096,128]{1,0:T(8,128)}, f32[8,1024]{1,0:T(8,128)}) custom-call(f32[4096,128]{1,0:T(8,128)} %get-tuple-element.110.mixed_ref, f32[4096,384]{1,0:T(8,128)} %get-tuple-element.111.query_ref.active_ref, f32[4096,128]{1,0:T(8,128)} %get-tuple-element.112.reach_ref, f32[4096,128]{1,0:T(8,128)} %get-tuple-element.113.gate_ref, ...), custom_call_target="tpu_custom_call" | custom-call | flops 134217728 | bytes 11534336 | tf_op jit(solution)/shard_map/pallas_call | solution.py:271
  92.8 7.7 %shard_map.282 = (bf16[4096,128]{1,0:T(8,128)(2,1)}, bf16[4096,128]{1,0:T(8,128)(2,1)}, f32[4096,128]{1,0:T(8,128)}, f32[1,128]{1,0:T(1,128)}, f32[128,128]{1,0:T(8,128)}) custom-call(f32[4096,128]{1,0:T(8,128)} %get-tuple-element.115.mixed_ref, f32[4096,384]{1,0:T(8,128)} %get-tuple-element.111.query_ref.active_ref, ...), custom_call_target="tpu_custom_call" | custom-call | flops 134217728 | bytes 13631488 | tf_op jit(solution)/shard_map/pallas_call | solution.py:323
  100.5 8.3 %all-gather.1 = f32[512,128]{1,0:T(8,128)S(1)} all-gather(f32[128,128]{1,0:T(8,128)} %get-tuple-element.121), channel_id=3, replica_groups=mesh['seq'=4,'head'=8] {'seq'}, dimensions={0}, use_global_device_ids=true | all-gather | bytes 327680 | tf_op jit(solution)/shard_map/all_gather | solution.py:892
  110.2 14.8 %shard_map.283 = (bf16[2048,768]{1,0:T(8,128)(2,1)}, f32[8,384]{1,0:T(8,128)}, f32[8,384]{1,0:T(8,128)}, f32[8,512]{1,0:T(8,128)}, f32[128,128]{1,0:T(8,128)}) custom-call(bf16[4096,384]{1,0:T(8,128)(2,1)} %get-tuple-element.108.stream_ref.before_ref, bf16[4096,384]{1,0:T(8,128)(2,1)} %get-tuple-element.108.stream_ref.before_ref, bf16[8,384]{1,0:T(8,128)(2,1)} %copy-done.17, ...), custom_call_target="tpu_custom_call" | custom-call | flops 1572864000 | bytes 15728640 | tf_op jit(solution)/shard_map/pallas_call | solution.py:480
  125.0 14.8 %shard_map.284 = (bf16[2048,768]{1,0:T(8,128)(2,1)}, f32[8,384]{1,0:T(8,128)}, f32[8,384]{1,0:T(8,128)}, f32[8,512]{1,0:T(8,128)}, f32[128,128]{1,0:T(8,128)}) custom-call(bf16[4096,384]{1,0:T(8,128)(2,1)} %get-tuple-element.108.stream_ref.before_ref, bf16[4096,384]{1,0:T(8,128)(2,1)} %get-tuple-element.108.stream_ref.before_ref, bf16[8,384]{1,0:T(8,128)(2,1)} %copy-done.17, ...), custom_call_target="tpu_custom_call" | custom-call | flops 1572864000 | bytes 15728640 | tf_op jit(solution)/shard_map/pallas_call | solution.py:480
  146.2 15.5 %shard_map.285 = (bf16[4,192,2560]{2,1,0:T(8,128)(2,1)}, bf16[4,192,2560]{2,1,0:T(8,128)(2,1)}, f32[1,2560]{1,0:T(1,128)}, f32[1,1536]{1,0:T(1,128)}) custom-call(s32[2]{0:T(128)} %pad_add_fusion.place_ref, bf16[4096,128]{1,0:T(8,128)(2,1)} %get-tuple-element.117.gate_ref, bf16[2048,768]{1,0:T(8,128)(2,1)} %get-tuple-element.124.early_ref, ...), custom_call_target="tpu_custom_call" | custom-call | flops 5033164800 | bytes 19660800 | tf_op jit(solution)/shard_map/pallas_call | solution.py:590
  161.8 11.1 %shard_map.287 = (bf16[4,192,1536]{2,1,0:T(8,128)(2,1)}, bf16[4,192,1536]{2,1,0:T(8,128)(2,1)}, f32[1,1536]{1,0:T(1,128)}, f32[1,1536]{1,0:T(1,128)}) custom-call(s32[2]{0:T(128)} %pad_add_fusion.place_ref, bf16[4096,128]{1,0:T(8,128)(2,1)} %get-tuple-element.117.gate_ref, bf16[2048,768]{1,0:T(8,128)(2,1)} %get-tuple-element.144.late_ref.early_ref, ...), custom_call_target="tpu_custom_call" | custom-call | flops 3019898880 | bytes 11796480 | tf_op jit(solution)/shard_map/pallas_call | solution.py:590
  186.8 7.7 %fusion.24 = f32[128,1536]{1,0:T(8,128)} fusion(bf16[4096,128]{1,0:T(8,128)(2,1)} %get-tuple-element.175, bf16[4096,1536]{1,0:T(8,128)(2,1)} %grad_ref.3), kind=kOutput, calls=%fused_computation.68 | convolution fusion | flops 1610612736 | bytes 14417920 | tf_op jit(solution)/shard_map/dot_general | solution.py:923
  201.4 11.1 %collective-permute-done.7.refs_0_ = bf16[192,1536]{1,0:T(8,128)(2,1)S(1)} collective-permute-done((bf16[192,1536]{1,0:T(8,128)(2,1)}, bf16[192,1536]{1,0:T(8,128)(2,1)S(1)}, u32[]{:S(2)}, u32[]{:S(2)}) %collective-permute-start.7) | collective-permute-done | bytes 589856 | tf_op jit(solution)/shard_map/ppermute | solution.py:749
  220.4 5.3 %collective-permute-start.9 = (bf16[192,2560]{1,0:T(8,128)(2,1)}, bf16[192,2560]{1,0:T(8,128)(2,1)}, u32[]{:S(2)}, u32[]{:S(2)}) collective-permute-start(bf16[192,2560]{1,0:T(8,128)(2,1)} %get-tuple-element.141), channel_id=1, source_target_pairs={{0,2},{1,3},{8,10},{9,11},{16,18},{17,19},{24,26},{25,27}} | collective-permute-start | bytes 2949128 | tf_op jit(solution)/shard_map/ppermute | solution.py:749
  225.7 13.7 %fusion = f32[1536,768]{1,0:T(8,128)S(1)} fusion(bf16[4096,1536]{1,0:T(8,128)(2,1)} %get-tuple-element.173, bf16[2048,768]{1,0:T(8,128)(2,1)S(1)} %fusion.17, bf16[2048,768]{1,0:T(8,128)(2,1)} %get-tuple-element.124.early_ref), kind=kOutput, calls=%fused_computation | convolution fusion | flops 9676259328 | bytes 23592960 | tf_op jit(solution)/shard_map/dot_general | solution.py:923
  243.9 14.9 %collective-permute-done.9.refs_0_ = bf16[192,2560]{1,0:T(8,128)(2,1)} collective-permute-done((bf16[192,2560]{1,0:T(8,128)(2,1)}, bf16[192,2560]{1,0:T(8,128)(2,1)}, u32[]{:S(2)}, u32[]{:S(2)}) %collective-permute-start.9) | collective-permute-done | bytes 983072 | tf_op jit(solution)/shard_map/ppermute | solution.py:749
  263.5 7.2 %shard_map.291 = bf16[8,192,512]{2,1,0:T(8,128)(2,1)} custom-call(s32[1]{0:T(128)} %bitcast.25.at_ref, bf16[8,512,128]{2,1,0:T(8,128)(2,1)} %all-to-all-done.rows_ref, bf16[8,128,1536]{2,1,0:T(8,128)(2,1)} %bitcast.94, bf16[4096,1536]{1,0:T(8,128)(2,1)} %hidden_ref.11), custom_call_target="tpu_custom_call" | custom-call | flops 1610612736 | bytes 8388608 | tf_op jit(solution)/shard_map/pallas_call | solution.py:643
  270.7 6.0 %all-to-all-start.1 = ((bf16[8,192,512]{2,1,0:T(8,128)(2,1)}), bf16[8,192,512]{2,1,0:T(8,128)(2,1)S(1)}, u32[]{:S(2)}, u32[]{:S(2)}) async-start(bf16[8,192,512]{2,1,0:T(8,128)(2,1)} %shard_map.291), calls=%async_computation.1 | async-start | bytes 3145728 | tf_op jit(solution)/shard_map/all_to_all | solution.py:917
  276.7 7.5 %fusion.23 = f32[1536,128]{1,0:T(8,128)} fusion(bf16[4096,1536]{1,0:T(8,128)(2,1)} %get-tuple-element.173, bf16[4096,128]{1,0:T(8,128)(2,1)S(1)} %copy-done.4), kind=kOutput, calls=%fused_computation.67 | convolution fusion | flops 1610612736 | bytes 14417920 | tf_op jit(solution)/shard_map/dot_general | solution.py:923
  291.3 44.6 %collective-permute-done.16 = f32[54,128]{1,0:T(8,128)S(1)} collective-permute-done((f32[54,128]{1,0:T(8,128)S(1)}, f32[54,128]{1,0:T(8,128)S(1)}, u32[]{:S(2)}, u32[]{:S(2)}) %collective-permute-start.16) | collective-permute-done | bytes 27680 | tf_op jit(solution)/shard_map/ppermute | solution.py:700
  346.9 18.0 %collective-permute-done.17 = f32[54,128]{1,0:T(8,128)S(1)} collective-permute-done((f32[54,128]{1,0:T(8,128)S(1)}, f32[54,128]{1,0:T(8,128)S(1)}, u32[]{:S(2)}, u32[]{:S(2)}) %collective-permute-start.17) | collective-permute-done | bytes 27680 | tf_op jit(solution)/shard_map/ppermute | solution.py:700
  426.4 5.6 %shard_map.295.refs_0_ = f32[192,4096]{1,0:T(8,128)} custom-call(s32[2]{0:T(128)} %pad_add_fusion.place_ref, bf16[4,192,1536]{2,1,0:T(8,128)(2,1)} %get-tuple-element.165.up_own.down_own.own_ref, bf16[4,192,1536]{2,1,0:T(8,128)(2,1)} %copy-done, bf16[192,1536]{1,0:T(8,128)(2,1)} %copy-done.10, bf16[192,1536]{1,0:T(8,128)(2,1)} %copy-done.11, ...), custom_call_target="tpu_custom_call" | custom-call | flops 7864320 | bytes 7077888 | tf_op jit(solution)/shard_map/pallas_call | solution.py:807
  432.7 7.7 %shard_map.296 = f32[192,4096]{1,0:T(8,128)} custom-call(s32[2]{0:T(128)} %pad_add_fusion.place_ref, bf16[4,192,2560]{2,1,0:T(8,128)(2,1)} %get-tuple-element.129.up_own.down_own.own_ref, bf16[4,192,2560]{2,1,0:T(8,128)(2,1)} %collective-permute-done.5.up_got.down_got.got_ref, ...), custom_call_target="tpu_custom_call", output_to_operand_aliasing={{}: (10, {})} | custom-call | flops 7864320 | bytes 11796480 | tf_op jit(solution)/shard_map/pallas_call | solution.py:807
  (233 shorter events, 146.3 us)
Async XLA Ops:
  7.2 256.3 %all-gather.5.cloned.1.call-start = ((), (), s32[]{:S(2)}) async-start(), calls=%async_computation.4 | async-start | bytes 3538944 | tf_op jit(solution)/shard_map/all_gather | solution.py:862
  161.7 50.8 %collective-permute-start.5 = (bf16[4,192,2560]{2,1,0:T(8,128)(2,1)}, bf16[4,192,2560]{2,1,0:T(8,128)(2,1)}, u32[]{:S(2)}, u32[]{:S(2)}) collective-permute-start(bf16[4,192,2560]{2,1,0:T(8,128)(2,1)} %get-tuple-element.130), channel_id=1, source_target_pairs={{0,1},{1,0},{2,3},{3,2},{4,5},{5,4},{6,7},{7,6},{8,9},{9,8},{10,11... | collective-permute-start | bytes 11796488 | tf_op jit(solution)/shard_map/ppermute | solution.py:929
  182.4 30.1 %collective-permute-start.7 = (bf16[192,1536]{1,0:T(8,128)(2,1)}, bf16[192,1536]{1,0:T(8,128)(2,1)S(1)}, u32[]{:S(2)}, u32[]{:S(2)}) collective-permute-start(bf16[192,1536]{1,0:T(8,128)(2,1)} %get-tuple-element.136), channel_id=1, source_target_pairs={{0,2},{1,3},{8,10},{9,11},{16,18},{17,19},{24,26},{25,27}} | collective-permute-start | bytes 1769480 | tf_op jit(solution)/shard_map/ppermute | solution.py:749
  186.0 26.6 %collective-permute-start.8 = (bf16[192,1536]{1,0:T(8,128)(2,1)}, bf16[192,1536]{1,0:T(8,128)(2,1)S(1)}, u32[]{:S(2)}, u32[]{:S(2)}) collective-permute-start(bf16[192,1536]{1,0:T(8,128)(2,1)} %get-tuple-element.137), channel_id=1, source_target_pairs={{7,5},{6,4},{15,13},{14,12},{23,21},{22,20},{31,29},{30,28}} | collective-permute-start | bytes 1769480 | tf_op jit(solution)/shard_map/ppermute | solution.py:751
  194.6 143.0 %collective-permute-start.30 = (f32[128,1536]{1,0:T(8,128)}, f32[128,1536]{1,0:T(8,128)}, u32[]{:S(2)}, u32[]{:S(2)}) collective-permute-start(f32[128,1536]{1,0:T(8,128)} %fusion.24), channel_id=1, source_target_pairs={{0,8},{8,0},{16,24},{24,16},{1,9},{9,1},{17,25},{25,17},{2,10},{10... | collective-permute-start | bytes 2359304 | tf_op jit(solution)/shard_map/ppermute | solution.py:700
  196.8 66.7 %all-to-all-start = ((bf16[8,512,128]{2,1,0:T(8,128)(2,1)}), bf16[8,512,128]{2,1,0:T(8,128)(2,1)}, u32[]{:S(2)}, u32[]{:S(2)}) async-start(bf16[8,512,128]{2,1,0:T(8,128)(2,1)} %bitcast.26), calls=%async_computation | async-start | bytes 2097152 | tf_op jit(solution)/shard_map/all_to_all | solution.py:886
  201.0 201.0 %reduce-scatter.2.cloned.1.call-start = ((), (), s32[]{:S(2)}) async-start(), calls=%async_computation.3 | async-start | bytes 1769472 | tf_op jit(solution)/shard_map/reduce_scatter | solution.py:966
  218.8 25.1 %collective-permute-start.10 = (bf16[192,2560]{1,0:T(8,128)(2,1)}, bf16[192,2560]{1,0:T(8,128)(2,1)}, u32[]{:S(2)}, u32[]{:S(2)}) collective-permute-start(bf16[192,2560]{1,0:T(8,128)(2,1)} %get-tuple-element.142), channel_id=1, source_target_pairs={{7,5},{6,4},{15,13},{14,12},{23,21},{22,20},{31,29},{30,28}} | collective-permute-start | bytes 2949128 | tf_op jit(solution)/shard_map/ppermute | solution.py:751
  220.4 38.5 %collective-permute-start.9 = (bf16[192,2560]{1,0:T(8,128)(2,1)}, bf16[192,2560]{1,0:T(8,128)(2,1)}, u32[]{:S(2)}, u32[]{:S(2)}) collective-permute-start(bf16[192,2560]{1,0:T(8,128)(2,1)} %get-tuple-element.141), channel_id=1, source_target_pairs={{0,2},{1,3},{8,10},{9,11},{16,18},{17,19},{24,26},{25,27}} | collective-permute-start | bytes 2949128 | tf_op jit(solution)/shard_map/ppermute | solution.py:749
  240.5 125.9 %collective-permute-start.26 = (f32[1536,128]{1,0:T(8,128)}, f32[1536,128]{1,0:T(8,128)}, u32[]{:S(2)}, u32[]{:S(2)}) collective-permute-start(f32[1536,128]{1,0:T(8,128)} %slice.295), channel_id=1, source_target_pairs={{0,8},{8,0},{16,24},{24,16},{1,9},{9,1},{17,25},{25,17},{2,10},{10... | collective-permute-start | bytes 2359304 | tf_op jit(solution)/shard_map/ppermute | solution.py:700
  270.7 115.4 %all-to-all-start.1 = ((bf16[8,192,512]{2,1,0:T(8,128)(2,1)}), bf16[8,192,512]{2,1,0:T(8,128)(2,1)S(1)}, u32[]{:S(2)}, u32[]{:S(2)}) async-start(bf16[8,192,512]{2,1,0:T(8,128)(2,1)} %shard_map.291), calls=%async_computation.1 | async-start | bytes 3145728 | tf_op jit(solution)/shard_map/all_to_all | solution.py:917
  284.2 84.3 %collective-permute-start.24 = (f32[1536,128]{1,0:T(8,128)}, f32[1536,128]{1,0:T(8,128)S(1)}, u32[]{:S(2)}, u32[]{:S(2)}) collective-permute-start(f32[1536,128]{1,0:T(8,128)} %fusion.23), channel_id=1, source_target_pairs={{0,16},{8,24},{16,0},{24,8},{1,17},{9,25},{17,1},{25,9},{2,18},{10... | collective-permute-start | bytes 2359304 | tf_op jit(solution)/shard_map/ppermute | solution.py:700
  286.0 86.8 %collective-permute-start.11 = (bf16[192,2560]{1,0:T(8,128)(2,1)}, bf16[192,2560]{1,0:T(8,128)(2,1)}, u32[]{:S(2)}, u32[]{:S(2)}) collective-permute-start(bf16[192,2560]{1,0:T(8,128)(2,1)} %get-tuple-element.153), channel_id=1, source_target_pairs={{0,2},{1,3},{2,4},{3,5},{8,10},{9,11},{10,12},{11,13},{16,18},{17,... | collective-permute-start | bytes 2949128 | tf_op jit(solution)/shard_map/ppermute | solution.py:749
  290.6 45.3 %collective-permute-start.16 = (f32[54,128]{1,0:T(8,128)S(1)}, f32[54,128]{1,0:T(8,128)S(1)}, u32[]{:S(2)}, u32[]{:S(2)}) collective-permute-start(f32[54,128]{1,0:T(8,128)S(1)} %fusion.32), channel_id=1, source_target_pairs={{0,2},{1,3},{2,0},{3,1},{4,6},{5,7},{6,4},{7,5},{8,10},{9,11},{10,... | collective-permute-start | bytes 82952 | tf_op jit(solution)/shard_map/ppermute | solution.py:700
  335.9 42.0 %collective-permute-start.12 = (bf16[192,2560]{1,0:T(8,128)(2,1)}, bf16[192,2560]{1,0:T(8,128)(2,1)}, u32[]{:S(2)}, u32[]{:S(2)}) collective-permute-start(bf16[192,2560]{1,0:T(8,128)(2,1)} %get-tuple-element.154), channel_id=1, source_target_pairs={{7,5},{6,4},{5,3},{4,2},{15,13},{14,12},{13,11},{12,10},{23,21},{2... | collective-permute-start | bytes 2949128 | tf_op jit(solution)/shard_map/ppermute | solution.py:751
  337.5 27.3 %collective-permute-start.17 = (f32[54,128]{1,0:T(8,128)S(1)}, f32[54,128]{1,0:T(8,128)S(1)}, u32[]{:S(2)}, u32[]{:S(2)}) collective-permute-start(f32[54,128]{1,0:T(8,128)S(1)} %add.162), channel_id=1, source_target_pairs={{0,4},{1,5},{2,6},{3,7},{4,0},{5,1},{6,2},{7,3},{8,12},{9,13},{10,... | collective-permute-start | bytes 82952 | tf_op jit(solution)/shard_map/ppermute | solution.py:700
  364.8 21.3 %collective-permute-start.31 = (f32[128,1536]{1,0:T(8,128)S(1)}, f32[128,1536]{1,0:T(8,128)}, u32[]{:S(2)}, u32[]{:S(2)}) collective-permute-start(f32[128,1536]{1,0:T(8,128)S(1)} %add.173), channel_id=1, source_target_pairs={{0,16},{8,24},{16,0},{24,8},{1,17},{9,25},{17,1},{25,9},{2,18},{10... | collective-permute-start | bytes 2359304 | tf_op jit(solution)/shard_map/ppermute | solution.py:700
  366.3 20.5 %collective-permute-start.18 = (bf16[192,1536]{1,0:T(8,128)(2,1)}, bf16[192,1536]{1,0:T(8,128)(2,1)}, u32[]{:S(2)}, u32[]{:S(2)}) collective-permute-start(bf16[192,1536]{1,0:T(8,128)(2,1)} %get-tuple-element.168), channel_id=1, source_target_pairs={{0,2},{1,3},{2,4},{3,5},{8,10},{9,11},{10,12},{11,13},{16,18},{17,... | collective-permute-start | bytes 1769480 | tf_op jit(solution)/shard_map/ppermute | solution.py:749
  368.5 22.2 %collective-permute-start.19 = (bf16[192,1536]{1,0:T(8,128)(2,1)}, bf16[192,1536]{1,0:T(8,128)(2,1)}, u32[]{:S(2)}, u32[]{:S(2)}) collective-permute-start(bf16[192,1536]{1,0:T(8,128)(2,1)} %get-tuple-element.169), channel_id=1, source_target_pairs={{7,5},{6,4},{5,3},{4,2},{15,13},{14,12},{13,11},{12,10},{23,21},{2... | collective-permute-start | bytes 1769480 | tf_op jit(solution)/shard_map/ppermute | solution.py:751
  372.8 31.9 %collective-permute-start.27 = (f32[1536,128]{1,0:T(8,128)}, f32[1536,128]{1,0:T(8,128)}, u32[]{:S(2)}, u32[]{:S(2)}) collective-permute-start(f32[1536,128]{1,0:T(8,128)} %get-tuple-element.178), channel_id=1, source_target_pairs={{0,16},{8,24},{16,0},{24,8},{1,17},{9,25},{17,1},{25,9},{2,18},{10... | collective-permute-start | bytes 2359304 | tf_op jit(solution)/shard_map/ppermute | solution.py:700
  386.2 27.5 %collective-permute-start.25 = (f32[1536,128]{1,0:T(8,128)S(1)}, f32[1536,128]{1,0:T(8,128)}, u32[]{:S(2)}, u32[]{:S(2)}) collective-permute-start(f32[1536,128]{1,0:T(8,128)S(1)} %add.167), channel_id=1, source_target_pairs={{0,8},{8,0},{16,24},{24,16},{1,9},{9,1},{17,25},{25,17},{2,10},{10... | collective-permute-start | bytes 2359304 | tf_op jit(solution)/shard_map/ppermute | solution.py:700
  386.9 45.8 %collective-permute-start.13 = (bf16[192,2560]{1,0:T(8,128)(2,1)}, bf16[192,2560]{1,0:T(8,128)(2,1)}, u32[]{:S(2)}, u32[]{:S(2)}) collective-permute-start(bf16[192,2560]{1,0:T(8,128)(2,1)} %get-tuple-element.159), channel_id=1, source_target_pairs={{0,2},{1,3},{2,4},{3,5},{4,6},{5,7},{8,10},{9,11},{10,12},{11,13},... | collective-permute-start | bytes 2949128 | tf_op jit(solution)/shard_map/ppermute | solution.py:749
  389.4 43.3 %collective-permute-start.14 = (bf16[192,2560]{1,0:T(8,128)(2,1)}, bf16[192,2560]{1,0:T(8,128)(2,1)}, u32[]{:S(2)}, u32[]{:S(2)}) collective-permute-start(bf16[192,2560]{1,0:T(8,128)(2,1)} %get-tuple-element.160), channel_id=1, source_target_pairs={{7,5},{6,4},{5,3},{4,2},{3,1},{2,0},{15,13},{14,12},{13,11},{12,10... | collective-permute-start | bytes 2949128 | tf_op jit(solution)/shard_map/ppermute | solution.py:751
  404.7 19.1 %collective-permute-start.20 = (bf16[192,1536]{1,0:T(8,128)(2,1)}, bf16[192,1536]{1,0:T(8,128)(2,1)S(1)}, u32[]{:S(2)}, u32[]{:S(2)}) collective-permute-start(bf16[192,1536]{1,0:T(8,128)(2,1)} %get-tuple-element.170), channel_id=1, source_target_pairs={{0,2},{1,3},{2,4},{3,5},{4,6},{5,7},{8,10},{9,11},{10,12},{11,13},... | collective-permute-start | bytes 1769480 | tf_op jit(solution)/shard_map/ppermute | solution.py:749
  (46 other events, 407.7 us)
Sparse Core Ops, SparseCore 0:
  173.6 56.1 all-gather.4
  263.6 46.5 reduce-scatter.1

commit v4 on v3

--- a/solution.py
+++ b/solution.py
@@ -472,8 +472,9 @@
 ):
     rows = stream.shape[0]
     span = SPAN
-    count = rows // span // 2
-    first = 2 * count - 1 if late else count - 1
+    early = rows // span // 4
+    count = 3 * early if late else early
+    first = 4 * early - 1 if late else early - 1
     row = lambda i: (first - i, 0)
     fixed = lambda i: (0, 0)
     narrow, full = spec((span, 128), row), spec((span, 384), row)
@@ -493,7 +494,7 @@
             spec((8, 384), fixed), spec((8, 512), fixed), spec((128, 128), fixed),
         ],
         out_shape=[
-            jax.ShapeDtypeStruct((rows // 2, 768), bf16),
+            jax.ShapeDtypeStruct((count * span, 768), bf16),
             jax.ShapeDtypeStruct((8, 384), f32),
             jax.ShapeDtypeStruct((8, 384), f32),
             jax.ShapeDtypeStruct((8, 512), f32),
@@ -514,10 +515,11 @@
 
 
 def group_of(rows, index):
-    half = rows // BLOCK // 2
+    early = rows // BLOCK // 4
+    late = 3 * early - 1
     if index == 0:
-        return half - 1, lambda place: half + place
-    return half + 1, lambda place: jnp.where(place < half, place, place + half - 1)
+        return late, lambda place: early + place
+    return early + 1, lambda place: jnp.where(place < early, place, place + late)
 
 
 def parts_kernel(
@@ -588,14 +590,14 @@
     share = width // chips // 2
     turned = spec((chips, share, block), lambda i, at: (0, 0, i))
     return pl.pallas_call(
-        partial(parts_kernel, block_of, blocks - 1, blocks // 2),
+        partial(parts_kernel, block_of, blocks - 1, blocks // 4),
         grid_spec=pltpu.PrefetchScalarGridSpec(
             num_scalar_prefetch=1,
             grid=(count,),
             in_specs=[
                 spec((block, 128), row),
-                spec((block, 512), lambda i, at: (jnp.minimum(block_of(i), blocks // 2 - 1), 0)),
-                spec((block, 512), lambda i, at: (jnp.maximum(block_of(i) - blocks // 2, 0), 0)),
+                spec((block, 512), lambda i, at: (jnp.minimum(block_of(i), blocks // 4 - 1), 0)),
+                spec((block, 512), lambda i, at: (jnp.maximum(block_of(i) - blocks // 4, 0), 0)),
                 whole_block(weights), spec((block, width), row), spec((block, 128), row),
                 whole_block(gain), whole_block(tail), whole_block(next_head), whole_block(taps),
             ],
@@ -693,11 +695,13 @@
     return [1 << n for n in range(count.bit_length() - 1)]
 
 
-def summed_over(value, axis, turned=False):
+def summed_over(value, axis, turned=False, bits=None, dtype=f32):
     count = lax.axis_size(axis)
-    bits = bits_of(axis)
+    bits = bits_of(axis) if bits is None else bits
     for bit in reversed(bits) if turned else bits:
-        value = value + lax.ppermute(value, axis, [(i, i ^ bit) for i in range(count)])
+        value = value.astype(dtype)
+        sent = lax.ppermute(value, axis, [(i, i ^ bit) for i in range(count)])
+        value = value.astype(f32) + sent.astype(f32)
     return value
 
 
@@ -877,7 +881,7 @@
     decays = gathered[:, 128]
     carried = chained(gathered[:, :128], decays, at_seq, False)
     mixed, sums = join(partial_mixed, active, reach, gate_in, grad_gated, carried, gain)
-    sums = summed_over(sums, "head")
+    sums = summed_over(sums, "head", False)
     gated_rows, grad_gate16, grad_mixed, grad_mix_gain, incoming = gate_step(
         mixed, active, reach, gate_in, grad_gated, sums, gain, inner_width
     )
@@ -908,66 +912,71 @@
             next_head, taps, chips,
         )
 
+    group_rows, late16 = after((group_rows, late16))
+    out_parts = output_rows(group_rows, all_out_proj, hidden_in, mine.astype(jnp.int32)[None])
+    out_parts = lax.all_to_all(out_parts, "head", 0, 0, tiled=False)
     own_0, other_0, dots_0, norm_sums = parts_of(0, late16, head)
     got_0 = lax.ppermute(other_0, "head", partner)
-    out_parts = output_rows(group_rows, all_out_proj, hidden_in, mine.astype(jnp.int32)[None])
+    early16, _, head, early_sums, _ = scan_backward(False, *scan_args, arriving, head)
+    next_head = passed_along(head, "seq", -1)
     if on_line:
         line_0 = line_terms(1, own_0, got_0, (), "head")
         line_0 = line_sent(1, line_0, "head")
-    out_parts = lax.all_to_all(out_parts, "head", 0, 0, tiled=False)
-    early16, _, head, early_sums, _ = scan_backward(False, *scan_args, arriving, head)
-    next_head = passed_along(head, "seq", -1)
     contract = (((0,), (0,)), ((), ()))
 
     def product(left, right):
         return lax.dot_general(left, right, contract, preferred_element_type=f32)
 
-    gated_rows, _ = after((gated_rows, early16))
-    grad_out_proj = product(gated_rows, out_grad)
     own_1, other_1, dots_1, more_sums = parts_of(1, early16, next_head)
     norm_sums = norm_sums + more_sums
     got_1 = lax.ppermute(other_1, "head", partner)
+    grad_out_proj = product(gated_rows, out_grad)
     dots = jnp.concatenate([dots_0.reshape(-1, 128), dots_1.reshape(-1, 128)], axis=0)
     needs = (late16, next_head, projected)
     if on_line:
-        line_0, dots = after((line_0, dots))
-        line_0 = line_terms(2, own_0, got_0, line_0, "head")
-        line_0 = line_sent(2, line_0, "head")
         sent = line_terms(1, own_1, got_1, (), "head")
         sent, needs, dots = after((sent, needs, dots))
         line_1 = line_sent(1, sent, "head")
-        line_0 = line_terms(3, own_0, got_0, line_0, "head")
-        line_0 = line_sent(3, line_0, "head")
+        line_0 = line_terms(2, own_0, got_0, line_0, "head")
+        line_0 = line_sent(2, line_0, "head")
     sums = (late_sums + early_sums).at[5, :128].set(grad_mix_gain[0])
     headed = jnp.concatenate(
         [sums[:5, 128:384].reshape(-1, 128), norm_sums.reshape(-1, 128), dots], axis=0
     )
-    headed = summed_over(headed, "head", False)
-    unit_dot, headed = headed[-dots.shape[0] :], headed[: -dots.shape[0]]
+    head_bits, seq_bits = bits_of("head"), bits_of("seq")
+    headed = summed_over(headed, "head", False, head_bits[:2])
+    grad_out_proj = summed_over(grad_out_proj, "seq", False, seq_bits[:1], bf16)
 
     late_fixed, next_rows, projected = needs
     extra = [sum(taps[tap] * next_rows[row - tap] for tap in range(row + 1)) for row in range(3)]
     fixed = tail.at[5:].add(jnp.stack(extra))
     fixed16 = fixed.astype(bf16)
     low16 = (fixed - fixed16.astype(f32))[:, inner_local:].astype(bf16)
-    late_fixed = lax.dynamic_update_slice(late_fixed, fixed16, (rows // 2 - 8, 0))
-    late_fixed = lax.dynamic_update_slice(late_fixed, low16, (rows // 2 - 8, 512))
+    late_fixed = lax.dynamic_update_slice(late_fixed, fixed16, (rows - rows // 4 - 8, 0))
+    late_fixed = lax.dynamic_update_slice(late_fixed, low16, (rows - rows // 4 - 8, 512))
     rest16 = jnp.concatenate([early16, late_fixed], axis=0)
     grad_rest = product(projected, rest16)
     state_part = row_major(grad_rest[:, 128:384] + grad_rest[:, 512:768])
-    grad_value_proj = row_major(grad_rest[:, :128])
-    step_sums = row_major(grad_rest[:, 384:512]).T[::head_size]
     if on_line:
         line_1, state_part = after((line_1, state_part))
         sent = line_terms(2, own_1, got_1, line_1, "head")
-        sent, projected, sums = after((sent, projected, sums))
+        sent, headed = after((sent, headed))
         line_1 = line_sent(2, sent, "head")
+        sent = line_terms(3, own_0, got_0, line_0, "head")
+        sent, projected, sums, grad_rest, grad_out_proj = after(
+            (sent, projected, sums, grad_rest, grad_out_proj)
+        )
+        line_0 = line_sent(3, sent, "head")
+    headed = summed_over(headed, "head", False, head_bits[2:])
+    unit_dot, headed = headed[-dots.shape[0] :], headed[: -dots.shape[0]]
+    grad_value_proj = row_major(grad_rest[:, :128])
+    step_sums = row_major(grad_rest[:, 384:512]).T[::head_size]
     grad_gate_proj = row_major(product(projected, grad_gate16))
     grad_state_proj = lax.psum_scatter(state_part, "head", scatter_dimension=0, tiled=True)
     grad_state_proj = summed_over(grad_state_proj, "seq", False)
-    grad_value_proj = summed_over(grad_value_proj, "seq", False)
-    grad_gate_proj = summed_over(grad_gate_proj, "seq", True)
-    grad_out_proj = summed_over(grad_out_proj, "seq", False)
+    grad_value_proj = summed_over(grad_value_proj, "seq", False, None, bf16)
+    grad_gate_proj = summed_over(grad_gate_proj, "seq", True, None, bf16)
+    grad_out_proj = summed_over(grad_out_proj, "seq", False, seq_bits[1:], bf16)
 
     small = jnp.concatenate(
         [sums.reshape(-1, 128), step_sums.reshape(-1, 128), headed.reshape(-1, 128)], axis=0
@@ -1001,7 +1010,7 @@
         for own, got in ((own_0, got_0), (own_1, got_1)):
             pair = (own.astype(f32) + got.astype(f32)).astype(bf16)
             pieces.append(spread_sums(pair, "head").T)
-        cut = rows // 2
+        cut = rows // 4
         grad_projected = jnp.concatenate([pieces[1][:cut], pieces[0], pieces[1][cut:]])
         dots_0, dots_1 = dots_0.reshape(-1), dots_1.reshape(-1)
         unit_dot = jnp.concatenate([dots_1[:cut], dots_0, dots_1[cut:]])

time: 450 us -> 429 us (0.953)
  waiting for transfers between devices: 104 us -> 78.9 us
  local copies, waits for them, and re-layouts: 25.5 us -> 30.9 us
    ppermute x16, waiting for transfers between devices: 69.6 us -> 51 us  [summed_over(): sent = lax.ppermute(value, axis, [(i, i ^ bit) for i in range(count)])]
    unnamed x74 -> x88, local copies, waits for them, and re-layouts: 6.36 us -> 12.4 us
    add x16 -> x14, other arithmetic: 15.4 us -> 9.73 us  [summed_over(): value = value.astype(f32) + sent.astype(f32)]
  transfers between devices with their start and end apart: 36 -> 36, of which waited for: 12 -> 9; matrix products, arithmetic and copies ran while one was open for 16% -> 17% of each run, Pallas kernels for 11% -> 20%
where the time goes in v4:
time: 429 us; the launch traced here: 424 us
  Pallas kernels  155 us (36%)
  waiting for transfers between devices  78.9 us (18%)
  starting transfers between devices  68.8 us (16%)
  matrix products  36.7 us (9%)
  local copies, waits for them, and re-layouts  30.9 us (7%)
  other arithmetic  21.7 us (5%)
  blocking collectives  17.3 us (4%)
  between operations  14.9 us (3%)
    ppermute x16, waiting for transfers between devices, summed_over(): sent = lax.ppermute(value, axis, [(i, i ^ bit) for i in range(count)])  51 us
    pallas_call x2, Pallas kernels, scan_backward(): pl.pallas_call(partial(backward_kernel, first), grid=(count,), in_specs=[...  29.6 us
    dot_general x3, matrix products, product(): return lax.dot_general(left, right, contract, preferred_element_type=f32)  29 us
    pallas_call x2, Pallas kernels, input_parts(): pl.pallas_call(partial(parts_kernel, block_of, blocks - 1, blocks // 4),...  26.8 us
    pallas_call x6, Pallas kernels, line_step(): pl.pallas_call(line_kernel, grid_spec=pltpu.PrefetchScalarGridSpec(num_sc...  24.3 us
    ppermute x6, starting transfers between devices, line_sent(): lax.ppermute(sent[0], axis, [(i, i + cores) for i in range(cores * step)])  23.7 us
    ppermute x6, waiting for transfers between devices, line_sent(): lax.ppermute(sent[0], axis, [(i, i + cores) for i in range(cores * step)])  23.2 us
    ppermute x16, starting transfers between devices, summed_over(): sent = lax.ppermute(value, axis, [(i, i ^ bit) for i in range(count)])  20.5 us
  transfers between devices with their start and end apart: 36, of which 9 were waited for; matrix products, arithmetic and copies ran while one was open for 17% of the time, Pallas kernels for 20%

profile of v4, /device:TPU:0, one launch (start us, length us, event | category | flops | bytes accessed | tf_op | source)
XLA Modules:
  0.0 424.3 jit_solution(16963804241255782252)
XLA Ops:
  10.1 17.1 %shard_map.279 = (bf16[4096,1536]{1,0:T(8,128)(2,1)}, f32[4096,128]{1,0:T(8,128)}, bf16[4096,384]{1,0:T(8,128)(2,1)}, f32[4096,128]{1,0:T(8,128)}, f32[4096,128]{1,0:T(8,128)}, /*index=5*/f32[1,4096]{1,0:T(1,128)}) custom-call(bf16[4096,1536]{1,0:T(8,128)(2,1)} %hidden_ref.11, f32[1,1536]{1,0:T(1,128)} %broadcast_in_dim.37.gain_ref, ...), custom_call_target="tpu_custom_call" | custom-call | flops 8053063680 | bytes 25165824 | tf_op jit(solution)/shard_map/pallas_call | solution.py:117
  27.9 4.9 %collective-permute-start = (bf16[8,384]{1,0:T(8,128)(2,1)S(1)}, bf16[8,384]{1,0:T(8,128)(2,1)S(1)}, u32[]{:S(2)}, u32[]{:S(2)}) collective-permute-start(bf16[8,384]{1,0:T(8,128)(2,1)S(1)} %slice.218), channel_id=1, source_target_pairs={{0,8},{8,16},{16,24},{1,9},{9,17},{17,25},{2,10},{10,18},{18,26},{... | collective-permute-start | bytes 18440 | tf_op jit(solution)/shard_map/ppermute | solution.py:689
  32.9 7.7 %fusion.22.grad_ref = f32[4096,128]{1,0:T(8,128)} fusion(bf16[4096,1536]{1,0:T(8,128)(2,1)} %grad_ref.3, bf16[128,1536]{1,0:T(8,128)(2,1)S(1)} %copy-done.8), kind=kOutput, calls=%fused_computation.74 | convolution fusion | flops 1610612736 | bytes 15073280 | tf_op jit(solution)/shard_map/dot_general | solution.py:871
  43.8 18.8 %shard_map.280 = (f32[4096,128]{1,0:T(8,128)}, f32[4096,384]{1,0:T(8,128)}, f32[4096,384]{1,0:T(8,128)}, f32[4096,128]{1,0:T(8,128)}, f32[4096,384]{1,0:T(8,128)}, /*index=5*/f32[16,128,128]{2,1,0:T(8,128)}) custom-call(bf16[4096,384]{1,0:T(8,128)(2,1)} %get-tuple-element.111.stream_ref.before_ref, bf16[8,384]{1,0:T(8,128)(2,1)} %copy-done.24, ...), custom_call_target="tpu_custom_call" | custom-call | flops 1887436800 | bytes 26214400 | tf_op jit(solution)/shard_map/pallas_call | solution.py:224
  64.1 9.4 %all-gather = f32[544,128]{1,0:T(8,128)S(1)} all-gather(f32[136,128]{1,0:T(8,128)S(1)} %pad_maximum_fusion.1), channel_id=2, replica_groups=mesh['seq'=4,'head'=8] {'seq'}, dimensions={0}, use_global_device_ids=true | all-gather | bytes 348160 | tf_op jit(solution)/shard_map/all_gather | solution.py:880
  74.3 6.6 %shard_map.281 = (f32[4096,128]{1,0:T(8,128)}, f32[8,1024]{1,0:T(8,128)}) custom-call(f32[4096,128]{1,0:T(8,128)} %get-tuple-element.113.mixed_ref, f32[4096,384]{1,0:T(8,128)} %get-tuple-element.114.query_ref.active_ref, f32[4096,128]{1,0:T(8,128)} %get-tuple-element.115.reach_ref, f32[4096,128]{1,0:T(8,128)} %get-tuple-element.116.gate_ref, ...), custom_call_target="tpu_custom_call" | custom-call | flops 134217728 | bytes 11534336 | tf_op jit(solution)/shard_map/pallas_call | solution.py:271
  92.5 7.8 %shard_map.282 = (bf16[4096,128]{1,0:T(8,128)(2,1)}, bf16[4096,128]{1,0:T(8,128)(2,1)}, f32[4096,128]{1,0:T(8,128)}, f32[1,128]{1,0:T(1,128)}, f32[128,128]{1,0:T(8,128)}) custom-call(f32[4096,128]{1,0:T(8,128)} %get-tuple-element.118.mixed_ref, f32[4096,384]{1,0:T(8,128)} %get-tuple-element.114.query_ref.active_ref, ...), custom_call_target="tpu_custom_call" | custom-call | flops 134217728 | bytes 13631488 | tf_op jit(solution)/shard_map/pallas_call | solution.py:323
  100.3 5.2 %all-to-all-start = ((bf16[8,512,128]{2,1,0:T(8,128)(2,1)}), bf16[8,512,128]{2,1,0:T(8,128)(2,1)S(1)}, u32[]{:S(2)}, u32[]{:S(2)}) async-start(bf16[8,512,128]{2,1,0:T(8,128)(2,1)} %bitcast.93), calls=%async_computation | async-start | bytes 2097152 | tf_op jit(solution)/shard_map/all_to_all | solution.py:890
  109.4 7.9 %all-gather.1 = f32[512,128]{1,0:T(8,128)S(1)} all-gather(f32[128,128]{1,0:T(8,128)S(1)} %copy-done.23), channel_id=3, replica_groups=mesh['seq'=4,'head'=8] {'seq'}, dimensions={0}, use_global_device_ids=true | all-gather | bytes 327680 | tf_op jit(solution)/shard_map/all_gather | solution.py:896
  118.7 21.0 %shard_map.283 = (bf16[3072,768]{1,0:T(8,128)(2,1)}, f32[8,384]{1,0:T(8,128)}, f32[8,384]{1,0:T(8,128)}, f32[8,512]{1,0:T(8,128)}, f32[128,128]{1,0:T(8,128)}) custom-call(bf16[4096,384]{1,0:T(8,128)(2,1)} %get-tuple-element.111.stream_ref.before_ref, bf16[4096,384]{1,0:T(8,128)(2,1)} %get-tuple-element.111.stream_ref.before_ref, bf16[8,384]{1,0:T(8,128)(2,1)} %copy-done.24, ...), custom_call_target="tpu_custom_call" | custom-call | flops 2359296000 | bytes 15728640 | tf_op jit(solution)/shard_map/pallas_call | solution.py:481
  139.7 15.4 %shard_map.287 = (bf16[4,192,2560]{2,1,0:T(8,128)(2,1)}, bf16[4,192,2560]{2,1,0:T(8,128)(2,1)}, f32[1,2560]{1,0:T(1,128)}, f32[1,1536]{1,0:T(1,128)}) custom-call(s32[2]{0:T(128)} %pad_add_fusion.place_ref, bf16[4096,128]{1,0:T(8,128)(2,1)} %get-tuple-element.120.gate_ref, bf16[3072,768]{1,0:T(8,128)(2,1)} %get-tuple-element.144.late_ref.early_ref, ...), custom_call_target="tpu_custom_call" | custom-call | flops 5033164800 | bytes 19660800 | tf_op jit(solution)/shard_map/pallas_call | solution.py:592
  155.2 8.6 %shard_map.284 = (bf16[1024,768]{1,0:T(8,128)(2,1)}, f32[8,384]{1,0:T(8,128)}, f32[8,384]{1,0:T(8,128)}, f32[8,512]{1,0:T(8,128)}, f32[128,128]{1,0:T(8,128)}) custom-call(bf16[4096,384]{1,0:T(8,128)(2,1)} %get-tuple-element.111.stream_ref.before_ref, bf16[4096,384]{1,0:T(8,128)(2,1)} %get-tuple-element.111.stream_ref.before_ref, bf16[8,384]{1,0:T(8,128)(2,1)} %copy-done.24, ...), custom_call_target="tpu_custom_call" | custom-call | flops 786432000 | bytes 15728640 | tf_op jit(solution)/shard_map/pallas_call | solution.py:481
  170.2 11.4 %shard_map.285 = (bf16[4,192,1536]{2,1,0:T(8,128)(2,1)}, bf16[4,192,1536]{2,1,0:T(8,128)(2,1)}, f32[1,1536]{1,0:T(1,128)}, f32[1,1536]{1,0:T(1,128)}) custom-call(s32[2]{0:T(128)} %pad_add_fusion.place_ref, bf16[4096,128]{1,0:T(8,128)(2,1)} %get-tuple-element.120.gate_ref, bf16[1024,768]{1,0:T(8,128)(2,1)} %get-tuple-element.127.early_ref, ...), custom_call_target="tpu_custom_call" | custom-call | flops 3019898880 | bytes 11796480 | tf_op jit(solution)/shard_map/pallas_call | solution.py:592
  183.0 7.2 %convolution_convert_fusion = bf16[128,1536]{1,0:T(8,128)(2,1)} fusion(bf16[4096,128]{1,0:T(8,128)(2,1)S(1)} %copy-done.2, bf16[4096,1536]{1,0:T(8,128)(2,1)} %grad_ref.3), kind=kOutput, calls=%fused_computation.4 | convolution fusion | flops 1610809344 | bytes 14024704 | tf_op jit(solution)/shard_map/dot_general | solution.py:928
  213.7 14.6 %fusion = f32[1536,768]{1,0:T(8,128)} fusion(bf16[4096,1536]{1,0:T(8,128)(2,1)} %get-tuple-element.179, bf16[3072,768]{1,0:T(8,128)(2,1)S(1)} %copy-done.1, bf16[1024,768]{1,0:T(8,128)(2,1)S(1)} %copy-done.7), kind=kOutput, calls=%fused_computation | convolution fusion | flops 9676259328 | bytes 23592960 | tf_op jit(solution)/shard_map/dot_general | solution.py:928
  228.2 23.2 %collective-permute-done.16.refs_0_ = bf16[192,2560]{1,0:T(8,128)(2,1)S(1)} collective-permute-done((bf16[192,2560]{1,0:T(8,128)(2,1)}, bf16[192,2560]{1,0:T(8,128)(2,1)S(1)}, u32[]{:S(2)}, u32[]{:S(2)}) %collective-permute-start.16) | collective-permute-done | bytes 983072 | tf_op jit(solution)/shard_map/ppermute | solution.py:753
  253.1 4.6 %shard_map.293 = (bf16[192,2560]{1,0:T(8,128)(2,1)}, bf16[192,2560]{1,0:T(8,128)(2,1)}) custom-call(s32[2]{0:T(128)} %add_clamp_fusion.1.at_ref, bf16[4,192,2560]{2,1,0:T(8,128)(2,1)} %get-tuple-element.167.up_own.down_own.own_ref, bf16[4,192,2560]{2,1,0:T(8,128)(2,1)} %collective-permute-done.15.up_got.down_got.got_ref, ...), custom_call_target="tpu_custom_call" | custom-call | flops 1966080 | bytes 7864320 | tf_op jit(solution)/shard_map/pallas_call | solution.py:734
  279.6 37.1 %collective-permute-done.14 = f32[54,128]{1,0:T(8,128)S(1)} collective-permute-done((f32[54,128]{1,0:T(8,128)S(1)}, f32[54,128]{1,0:T(8,128)S(1)}, u32[]{:S(2)}, u32[]{:S(2)}) %collective-permute-start.14) | collective-permute-done | bytes 27680 | tf_op jit(solution)/shard_map/ppermute | solution.py:703
  323.3 4.6 %shard_map.294 = (bf16[192,2560]{1,0:T(8,128)(2,1)}, bf16[192,2560]{1,0:T(8,128)(2,1)}) custom-call(s32[2]{0:T(128)} %add_clamp_fusion.at_ref, bf16[4,192,2560]{2,1,0:T(8,128)(2,1)} %get-tuple-element.167.up_own.down_own.own_ref, bf16[4,192,2560]{2,1,0:T(8,128)(2,1)} %collective-permute-done.15.up_got.down_got.got_ref, ...), custom_call_target="tpu_custom_call" | custom-call | flops 1966080 | bytes 7864320 | tf_op jit(solution)/shard_map/pallas_call | solution.py:734
  333.2 7.2 %shard_map.290 = bf16[8,192,512]{2,1,0:T(8,128)(2,1)} custom-call(s32[1]{0:T(128)} %bitcast.26.at_ref, bf16[8,512,128]{2,1,0:T(8,128)(2,1)} %copy-done.6, bf16[8,128,1536]{2,1,0:T(8,128)(2,1)} %bitcast.95, bf16[4096,1536]{1,0:T(8,128)(2,1)} %hidden_ref.11), custom_call_target="tpu_custom_call" | custom-call | flops 1610612736 | bytes 8388608 | tf_op jit(solution)/shard_map/pallas_call | solution.py:645
  345.2 4.8 %collective-permute-start.21 = (bf16[192,2560]{1,0:T(8,128)(2,1)}, bf16[192,2560]{1,0:T(8,128)(2,1)}, u32[]{:S(2)}, u32[]{:S(2)}) collective-permute-start(bf16[192,2560]{1,0:T(8,128)(2,1)} %get-tuple-element.175), channel_id=1, source_target_pairs={{0,2},{1,3},{2,4},{3,5},{4,6},{5,7},{8,10},{9,11},{10,12},{11,13},... | collective-permute-start | bytes 2949128 | tf_op jit(solution)/shard_map/ppermute | solution.py:753
  353.2 7.2 %convolution_convert_fusion.1 = bf16[1536,128]{1,0:T(8,128)(2,1)} fusion(bf16[4096,1536]{1,0:T(8,128)(2,1)} %get-tuple-element.179, bf16[4096,128]{1,0:T(8,128)(2,1)S(1)} %copy-done.5), kind=kOutput, calls=%fused_computation.5 | convolution fusion | flops 1610809344 | bytes 14024704 | tf_op jit(solution)/shard_map/dot_general | solution.py:928
  402.5 7.7 %shard_map.295.refs_0_ = f32[192,4096]{1,0:T(8,128)} custom-call(s32[2]{0:T(128)} %pad_add_fusion.place_ref, bf16[4,192,2560]{2,1,0:T(8,128)(2,1)} %get-tuple-element.167.up_own.down_own.own_ref, bf16[4,192,2560]{2,1,0:T(8,128)(2,1)} %collective-permute-done.15.up_got.down_got.got_ref, bf16[192,2560]{1,0:T(8,128)(2,1)} %collective-permute-done.21.up_ref, ...), custom_call_target="tpu_custom_call" | custom-call | flops 7864320 | bytes 11796480 | tf_op jit(solution)/shard_map/pallas_call | solution.py:811
  411.9 5.5 %shard_map.296 = f32[192,4096]{1,0:T(8,128)} custom-call(s32[2]{0:T(128)} %pad_add_fusion.place_ref, bf16[4,192,1536]{2,1,0:T(8,128)(2,1)} %get-tuple-element.134.up_own.down_own.own_ref, bf16[4,192,1536]{2,1,0:T(8,128)(2,1)} %copy-done, bf16[192,1536]{1,0:T(8,128)(2,1)} %copy-done.15, ...), custom_call_target="tpu_custom_call", output_to_operand_aliasing={{}: (10, {})} | custom-call | flops 7864320 | bytes 7077888 | tf_op jit(solution)/shard_map/pallas_call | solution.py:811
  (248 shorter events, 143.8 us)
Async XLA Ops:
  27.9 15.3 %collective-permute-start = (bf16[8,384]{1,0:T(8,128)(2,1)S(1)}, bf16[8,384]{1,0:T(8,128)(2,1)S(1)}, u32[]{:S(2)}, u32[]{:S(2)}) collective-permute-start(bf16[8,384]{1,0:T(8,128)(2,1)S(1)} %slice.218), channel_id=1, source_target_pairs={{0,8},{8,16},{16,24},{1,9},{9,17},{17,25},{2,10},{10,18},{18,26},{... | collective-permute-start | bytes 18440 | tf_op jit(solution)/shard_map/ppermute | solution.py:689
  100.3 39.4 %all-to-all-start = ((bf16[8,512,128]{2,1,0:T(8,128)(2,1)}), bf16[8,512,128]{2,1,0:T(8,128)(2,1)S(1)}, u32[]{:S(2)}, u32[]{:S(2)}) async-start(bf16[8,512,128]{2,1,0:T(8,128)(2,1)} %bitcast.93), calls=%async_computation | async-start | bytes 2097152 | tf_op jit(solution)/shard_map/all_to_all | solution.py:890
  105.5 227.6 %all-gather.5.cloned.1.call-start = ((), (), s32[]{:S(2)}) async-start(), calls=%async_computation.4 | async-start | bytes 3538944 | tf_op jit(solution)/shard_map/all_gather | solution.py:866
  155.1 48.4 %collective-permute-start.15 = (bf16[4,192,2560]{2,1,0:T(8,128)(2,1)}, bf16[4,192,2560]{2,1,0:T(8,128)(2,1)}, u32[]{:S(2)}, u32[]{:S(2)}) collective-permute-start(bf16[4,192,2560]{2,1,0:T(8,128)(2,1)} %get-tuple-element.168), channel_id=1, source_target_pairs={{0,1},{1,0},{2,3},{3,2},{4,5},{5,4},{6,7},{7,6},{8,9},{9,8},{10,11... | collective-permute-start | bytes 11796488 | tf_op jit(solution)/shard_map/ppermute | solution.py:919
  181.7 186.9 %reduce-scatter.2.cloned.1.call-start = ((), (), s32[]{:S(2)}) async-start(), calls=%async_computation.3 | async-start | bytes 1769472 | tf_op jit(solution)/shard_map/reduce_scatter | solution.py:975
  195.4 70.3 %collective-permute-start.6 = (bf16[192,1536]{1,0:T(8,128)(2,1)}, bf16[192,1536]{1,0:T(8,128)(2,1)S(1)}, u32[]{:S(2)}, u32[]{:S(2)}) collective-permute-start(bf16[192,1536]{1,0:T(8,128)(2,1)} %get-tuple-element.141), channel_id=1, source_target_pairs={{0,2},{1,3},{8,10},{9,11},{16,18},{17,19},{24,26},{25,27}} | collective-permute-start | bytes 1769480 | tf_op jit(solution)/shard_map/ppermute | solution.py:753
  199.3 66.5 %collective-permute-start.7 = (bf16[192,1536]{1,0:T(8,128)(2,1)}, bf16[192,1536]{1,0:T(8,128)(2,1)}, u32[]{:S(2)}, u32[]{:S(2)}) collective-permute-start(bf16[192,1536]{1,0:T(8,128)(2,1)} %get-tuple-element.142), channel_id=1, source_target_pairs={{7,5},{6,4},{15,13},{14,12},{23,21},{22,20},{31,29},{30,28}} | collective-permute-start | bytes 1769480 | tf_op jit(solution)/shard_map/ppermute | solution.py:755
  203.4 58.7 %collective-permute-start.9 = (f32[54,128]{1,0:T(8,128)S(1)}, f32[54,128]{1,0:T(8,128)}, u32[]{:S(2)}, u32[]{:S(2)}) collective-permute-start(f32[54,128]{1,0:T(8,128)S(1)} %fusion.30), channel_id=1, source_target_pairs={{0,2},{1,3},{2,0},{3,1},{4,6},{5,7},{6,4},{7,5},{8,10},{9,11},{10,... | collective-permute-start | bytes 82952 | tf_op jit(solution)/shard_map/ppermute | solution.py:703
  208.0 43.4 %collective-permute-start.16 = (bf16[192,2560]{1,0:T(8,128)(2,1)}, bf16[192,2560]{1,0:T(8,128)(2,1)S(1)}, u32[]{:S(2)}, u32[]{:S(2)}) collective-permute-start(bf16[192,2560]{1,0:T(8,128)(2,1)} %get-tuple-element.169), channel_id=1, source_target_pairs={{0,2},{1,3},{8,10},{9,11},{16,18},{17,19},{24,26},{25,27}} | collective-permute-start | bytes 2949128 | tf_op jit(solution)/shard_map/ppermute | solution.py:753
  211.9 41.2 %collective-permute-start.17 = (bf16[192,2560]{1,0:T(8,128)(2,1)}, bf16[192,2560]{1,0:T(8,128)(2,1)}, u32[]{:S(2)}, u32[]{:S(2)}) collective-permute-start(bf16[192,2560]{1,0:T(8,128)(2,1)} %get-tuple-element.170), channel_id=1, source_target_pairs={{7,5},{6,4},{15,13},{14,12},{23,21},{22,20},{31,29},{30,28}} | collective-permute-start | bytes 2949128 | tf_op jit(solution)/shard_map/ppermute | solution.py:755
  251.4 23.5 %collective-permute-start.20 = (bf16[128,1536]{1,0:T(8,128)(2,1)S(1)}, bf16[128,1536]{1,0:T(8,128)(2,1)S(1)}, u32[]{:S(2)}, u32[]{:S(2)}) collective-permute-start(bf16[128,1536]{1,0:T(8,128)(2,1)S(1)} %copy-done.9), channel_id=1, source_target_pairs={{0,8},{8,0},{16,24},{24,16},{1,9},{9,1},{17,25},{25,17},{2,10},{10... | collective-permute-start | bytes 1179656 | tf_op jit(solution)/shard_map/ppermute | solution.py:703
  257.7 64.6 %collective-permute-start.18 = (bf16[192,2560]{1,0:T(8,128)(2,1)}, bf16[192,2560]{1,0:T(8,128)(2,1)S(1)}, u32[]{:S(2)}, u32[]{:S(2)}) collective-permute-start(bf16[192,2560]{1,0:T(8,128)(2,1)} %get-tuple-element.171), channel_id=1, source_target_pairs={{0,2},{1,3},{2,4},{3,5},{8,10},{9,11},{10,12},{11,13},{16,18},{17,... | collective-permute-start | bytes 2949128 | tf_op jit(solution)/shard_map/ppermute | solution.py:753
  262.1 60.3 %collective-permute-start.19 = (bf16[192,2560]{1,0:T(8,128)(2,1)}, bf16[192,2560]{1,0:T(8,128)(2,1)}, u32[]{:S(2)}, u32[]{:S(2)}) collective-permute-start(bf16[192,2560]{1,0:T(8,128)(2,1)} %get-tuple-element.172), channel_id=1, source_target_pairs={{7,5},{6,4},{5,3},{4,2},{15,13},{14,12},{13,11},{12,10},{23,21},{2... | collective-permute-start | bytes 2949128 | tf_op jit(solution)/shard_map/ppermute | solution.py:755
  270.2 47.6 %collective-permute-start.10 = (bf16[192,1536]{1,0:T(8,128)(2,1)}, bf16[192,1536]{1,0:T(8,128)(2,1)S(1)}, u32[]{:S(2)}, u32[]{:S(2)}) collective-permute-start(bf16[192,1536]{1,0:T(8,128)(2,1)} %get-tuple-element.156), channel_id=1, source_target_pairs={{0,2},{1,3},{2,4},{3,5},{8,10},{9,11},{10,12},{11,13},{16,18},{17,... | collective-permute-start | bytes 1769480 | tf_op jit(solution)/shard_map/ppermute | solution.py:753
  272.8 45.1 %collective-permute-start.11 = (bf16[192,1536]{1,0:T(8,128)(2,1)}, bf16[192,1536]{1,0:T(8,128)(2,1)}, u32[]{:S(2)}, u32[]{:S(2)}) collective-permute-start(bf16[192,1536]{1,0:T(8,128)(2,1)} %get-tuple-element.157), channel_id=1, source_target_pairs={{7,5},{6,4},{5,3},{4,2},{15,13},{14,12},{13,11},{12,10},{23,21},{2... | collective-permute-start | bytes 1769480 | tf_op jit(solution)/shard_map/ppermute | solution.py:755
  274.9 41.7 %collective-permute-start.14 = (f32[54,128]{1,0:T(8,128)S(1)}, f32[54,128]{1,0:T(8,128)S(1)}, u32[]{:S(2)}, u32[]{:S(2)}) collective-permute-start(f32[54,128]{1,0:T(8,128)S(1)} %add.162), channel_id=1, source_target_pairs={{0,4},{1,5},{2,6},{3,7},{4,0},{5,1},{6,2},{7,3},{8,12},{9,13},{10,... | collective-permute-start | bytes 82952 | tf_op jit(solution)/shard_map/ppermute | solution.py:703
  331.7 19.9 %collective-permute-start.23 = (f32[78,128]{1,0:T(8,128)S(1)}, f32[78,128]{1,0:T(8,128)S(1)}, u32[]{:S(2)}, u32[]{:S(2)}) collective-permute-start(f32[78,128]{1,0:T(8,128)S(1)} %pad_maximum_fusion.2), channel_id=1, source_target_pairs={{0,8},{8,0},{16,24},{24,16},{1,9},{9,1},{17,25},{25,17},{2,10},{10... | collective-permute-start | bytes 119816 | tf_op jit(solution)/shard_map/ppermute | solution.py:703
  340.3 46.0 %all-to-all-start.1 = ((bf16[8,192,512]{2,1,0:T(8,128)(2,1)}), bf16[8,192,512]{2,1,0:T(8,128)(2,1)S(1)}, u32[]{:S(2)}, u32[]{:S(2)}) async-start(bf16[8,192,512]{2,1,0:T(8,128)(2,1)} %shard_map.290), calls=%async_computation.1 | async-start | bytes 3145728 | tf_op jit(solution)/shard_map/all_to_all | solution.py:917
  345.2 57.3 %collective-permute-start.21 = (bf16[192,2560]{1,0:T(8,128)(2,1)}, bf16[192,2560]{1,0:T(8,128)(2,1)}, u32[]{:S(2)}, u32[]{:S(2)}) collective-permute-start(bf16[192,2560]{1,0:T(8,128)(2,1)} %get-tuple-element.175), channel_id=1, source_target_pairs={{0,2},{1,3},{2,4},{3,5},{4,6},{5,7},{8,10},{9,11},{10,12},{11,13},... | collective-permute-start | bytes 2949128 | tf_op jit(solution)/shard_map/ppermute | solution.py:753
  350.1 52.5 %collective-permute-start.22 = (bf16[192,2560]{1,0:T(8,128)(2,1)}, bf16[192,2560]{1,0:T(8,128)(2,1)}, u32[]{:S(2)}, u32[]{:S(2)}) collective-permute-start(bf16[192,2560]{1,0:T(8,128)(2,1)} %get-tuple-element.176), channel_id=1, source_target_pairs={{7,5},{6,4},{5,3},{4,2},{3,1},{2,0},{15,13},{14,12},{13,11},{12,10... | collective-permute-start | bytes 2949128 | tf_op jit(solution)/shard_map/ppermute | solution.py:755
  361.6 21.3 %collective-permute-start.31 = (bf16[128,1536]{1,0:T(8,128)(2,1)S(1)}, bf16[128,1536]{1,0:T(8,128)(2,1)}, u32[]{:S(2)}, u32[]{:S(2)}) collective-permute-start(bf16[128,1536]{1,0:T(8,128)(2,1)S(1)} %convert_add_fusion.3), channel_id=1, source_target_pairs={{0,16},{8,24},{16,0},{24,8},{1,17},{9,25},{17,1},{25,9},{2,18},{10... | collective-permute-start | bytes 1179656 | tf_op jit(solution)/shard_map/ppermute | solution.py:703
  375.9 22.4 %collective-permute-start.26 = (bf16[1536,128]{1,0:T(8,128)(2,1)S(1)}, bf16[1536,128]{1,0:T(8,128)(2,1)S(1)}, u32[]{:S(2)}, u32[]{:S(2)}) collective-permute-start(bf16[1536,128]{1,0:T(8,128)(2,1)S(1)} %add_convert_fusion.1), channel_id=1, source_target_pairs={{0,8},{8,0},{16,24},{24,16},{1,9},{9,1},{17,25},{25,17},{2,10},{10... | collective-permute-start | bytes 1179656 | tf_op jit(solution)/shard_map/ppermute | solution.py:703
  381.3 19.2 %collective-permute-start.28 = (bf16[1536,128]{1,0:T(8,128)(2,1)S(1)}, bf16[1536,128]{1,0:T(8,128)(2,1)}, u32[]{:S(2)}, u32[]{:S(2)}) collective-permute-start(bf16[1536,128]{1,0:T(8,128)(2,1)S(1)} %add_convert_fusion), channel_id=1, source_target_pairs={{0,16},{8,24},{16,0},{24,8},{1,17},{9,25},{17,1},{25,9},{2,18},{10... | collective-permute-start | bytes 1179656 | tf_op jit(solution)/shard_map/ppermute | solution.py:703
  392.4 17.9 %collective-permute-start.12 = (bf16[192,1536]{1,0:T(8,128)(2,1)}, bf16[192,1536]{1,0:T(8,128)(2,1)S(1)}, u32[]{:S(2)}, u32[]{:S(2)}) collective-permute-start(bf16[192,1536]{1,0:T(8,128)(2,1)} %get-tuple-element.163), channel_id=1, source_target_pairs={{0,2},{1,3},{2,4},{3,5},{4,6},{5,7},{8,10},{9,11},{10,12},{11,13},... | collective-permute-start | bytes 1769480 | tf_op jit(solution)/shard_map/ppermute | solution.py:753
  (53 other events, 464.7 us)
Sparse Core Ops, SparseCore 0:
  181.8 52.0 all-gather.4
  275.0 41.0 reduce-scatter.1
